TPU v7x, 256 devices: a whole 4x4x8 slice. The times are simulated.
256 devices in a mesh: grp: 8 (over x, core), box: 32 (over y, z).
Axes of the slice: x: 4, y: 4, z: 8, core: 2. Of those that a mesh axis runs over, the one named last changes fastest.
Arguments:
- source_field: float32 [256, 1024, 128], P('grp', 'box'), may hold values from -7 to 7
- region_tags: int32 [256, 1024, 128], P('grp', 'box'), may hold values from 0 to 7
- region_coef: float32 [8], replicated, may hold values from 0.2 to 5
- roughness: float32 [256, 1024, 128], P('grp', 'box'), may hold values from 0.5 to 2
Outputs:
- solution: float32 [256, 1024, 128], P('grp', 'box')
- residual: float32 [256, 1024, 128], P('grp', 'box')
All inputs are finite; a program needn't handle non-finite values.
Results may differ from a plain program's by a relative error of at most 0.0003.
Values sent between devices are 32-bit elements; how exact they have to be, the bound alone decides.
No kernel may reach another device: no remote copies, remote signals or barrier semaphores. Data moves between devices by JAX's collectives and lax.ppermute only.
A program may use at most 192 MiB of HBM per device.

v0:
```python
import jax
import jax.numpy as jnp
from jax import lax
from jax.experimental import pallas as pl
from jax.experimental.pallas import tpu as pltpu
from jax.sharding import PartitionSpec as P

F32 = jnp.float32
NB = 4
INTERPRET = False


def params():
    return pltpu.CompilerParams(vmem_limit_bytes=56 << 20)


def call(kernel, ins, outs, scratch=(), smem=()):
    specs = [
        pl.BlockSpec(memory_space=pltpu.SMEM if i in smem else pltpu.VMEM) for i in range(len(ins))
    ]
    return pl.pallas_call(
        kernel,
        out_shape=[jax.ShapeDtypeStruct(s, F32) for s in outs],
        in_specs=specs,
        out_specs=[pl.BlockSpec(memory_space=pltpu.VMEM) for _ in outs],
        scratch_shapes=[pltpu.VMEM(s, F32) for s in scratch],
        compiler_params=params(),
        interpret=INTERPRET,
    )(*ins)


def iota(shape, dim):
    return lax.broadcasted_iota(jnp.int32, shape, dim)


def halver(n):
    k, j = iota((n, n), 0), iota((n, n), 1)
    return jnp.where((k >> 1) == j, F32(0.5), F32(0.0))


def doubler(n):
    j, k = iota((n, n), 0), iota((n, n), 1)
    return jnp.where((k >> 1) == j, F32(1.0), F32(0.0))


def dot(a, b):
    return lax.dot_general(
        a, b, (((1,), (0,)), ((), ())), precision=lax.Precision.HIGHEST, preferred_element_type=F32
    )


def up(v, axis):
    return pltpu.roll(v, v.shape[axis] - 1, axis)


def down(v, axis):
    return pltpu.roll(v, 1, axis)


def near_sum(vc, vn, carry, wxx, wss, wll):
    t = wxx * vn + carry
    t = t + (wss * up(vc, 0) + down(wss * vc, 0))
    return t + (wll * up(vc, 1) + down(wll * vc, 1))


def sweep(v, f, op, lo, hi):
    wx, ws, wl, di = op

    def step(x, state):
        carry, vc = state
        vn = v[x + 1]
        wxx = wx[x]
        t = near_sum(vc, vn, carry, wxx, ws[x], wl[x])
        v[x] = F32(0.2) * vc + di[x] * (f[x] + t)
        return (wxx * vc, vn)

    lax.fori_loop(lo, hi, step, (wx[lo - 1] * v[lo - 1], v[lo]), unroll=2)


def first_sweep(v, f, op, lo, hi):
    di = op[3]

    def step(x, _):
        v[x] = di[x] * f[x]
        return 0

    lax.fori_loop(lo, hi, step, 0, unroll=2)


def resid(v, f, op, x):
    wx, ws, wl, di = op
    vc = v[x]
    t = near_sum(vc, v[x + 1], wx[x - 1] * v[x - 1], wx[x], ws[x], wl[x])
    dinv = di[x]
    inside = dinv > 0
    diag = jnp.where(inside, F32(0.8) / jnp.where(inside, dinv, F32(1.0)), F32(0.0))
    return f[x] - (diag * vc - t)


def resid_pairs(v, f, op, lo, n, out):
    def step(i, _):
        x = lo + 2 * i
        out[i] = resid(v, f, op, x) + resid(v, f, op, x + 1)
        return 0

    lax.fori_loop(0, n, step, 0)


def weights(c, cbase, op, lo, hi, lane_last, sub_last, edge=None):
    wx, ws, wl, di = op
    half = F32(0.5)

    def step(x, _):
        cc = c[x + cbase]
        ch = cc * half
        cp = ch + c[x + cbase + 1] * half
        cm = ch + c[x + cbase - 1] * half
        rows, lanes = iota(cc.shape, 0), iota(cc.shape, 1)
        ny, nl = cc.shape
        s_next, s_prev = up(ch, 0), down(ch, 0)
        if sub_last:
            s_next = jnp.where(rows == ny - 1, F32(0.0), s_next)
            s_prev = jnp.where(rows == 0, F32(0.0), s_prev)
        if edge is not None:
            s_next = jnp.where(rows == ny - 1, edge[1, pl.ds(x + cbase, 1), :] * half, s_next)
            s_prev = jnp.where(rows == 0, edge[0, pl.ds(x + cbase, 1), :] * half, s_prev)
        l_next = jnp.where(lanes >= lane_last, F32(0.0), up(ch, 1))
        l_prev = jnp.where(lanes == 0, F32(0.0), down(ch, 1))
        s_up, l_up = ch + s_next, ch + l_next
        diag = (cp + cm) + (s_up + (ch + s_prev)) + (l_up + (ch + l_prev))
        inside = cc > 0
        wx[x] = cp
        ws[x] = jnp.where(rows == ny - 1, F32(0.0), s_up) if sub_last else s_up
        wl[x] = jnp.where(lanes >= lane_last, F32(0.0), l_up)
        di[x] = jnp.where(inside, F32(0.8) / jnp.where(inside, diag, F32(1.0)), F32(0.0))
        return 0

    lax.fori_loop(lo, hi, step, 0)


def pair_rows(s, start, n):
    return s[:, pl.ds(start, n, stride=2), :] + s[:, pl.ds(start + 1, n, stride=2), :]


def flat(a):
    return a.reshape(a.shape[0] * a.shape[1], a.shape[2])


def add_double(v, es, lo, hi):
    def step(x, _):
        v[x] = v[x] + es[x >> 1]
        return 0

    lax.fori_loop(lo, hi, step, 0, unroll=2)


def coef_kernel(f, tags, table, rough, coef, to_next, to_prev):
    def step(x, _):
        tag = tags[x]
        picked = jnp.zeros(tag.shape, F32)
        for region in range(8):
            picked = jnp.where(tag == region, table[region], picked)
        coef[x] = picked * rough[x]
        return 0

    lax.fori_loop(0, 32, step, 0)
    to_next[0:8] = f[24:32]
    to_next[8:17] = coef[23:32]
    to_prev[0:8] = f[0:8]
    to_prev[8:17] = coef[0:9]


def rows_kernel(f, coef, left, right, to_next, to_prev):
    for out, row, extra in ((to_next, 24, 23), (to_prev, 0, 8)):
        sl = slice(row, row + 8)
        out[0:8] = left[0:8, sl]
        out[8:40] = f[:, sl]
        out[40:48] = right[0:8, sl]
        out[48:57] = left[8:17, sl]
        out[57:89] = coef[:, sl]
        out[89:98] = right[8:17, sl]
        for x in range(50):
            if x < 9:
                line = left[8 + x, extra : extra + 1, :]
            elif x < 41:
                line = coef[x - 9, extra : extra + 1, :]
            else:
                line = right[8 + x - 41, extra : extra + 1, :]
            out[98 + x // 8, x % 8 : x % 8 + 1, :] = line
        out[104, 2:8, :] = jnp.zeros((6, 128), F32)


def edge_flags(ng, nb):
    g, b = lax.axis_index("grp"), lax.axis_index("box")
    one, zero = F32(1.0), F32(0.0)
    return (
        jnp.where(g > 0, one, zero),
        jnp.where(g < ng - 1, one, zero),
        jnp.where(b > 0, one, zero),
        jnp.where(b < nb - 1, one, zero),
    )


def fine_restrict(v, f, op, s):
    resid_pairs(v, f, op, 8, 16, s)
    pairs = pair_rows(s, 8, 16)
    return dot(flat(pairs), halver(128)).reshape(16, 16, 128)


def start_kernel(
    ng, nb, f, coef, left, right, above, below, v, fx, wx, ws, wl, di, packed, cx, edge, s
):
    gl, gr, bl, br = edge_flags(ng, nb)
    fx[0:8, 8:40] = left[0:8]
    fx[8:40, 8:40] = f[...]
    fx[40:48, 8:40] = right[0:8]
    fx[:, 0:8] = above[0:48]
    fx[:, 40:48] = below[0:48]
    cx[0:9, 8:40] = left[8:17] * gl
    cx[9:41, 8:40] = coef[...]
    cx[41:50, 8:40] = right[8:17] * gr
    for rows, src, flag in ((slice(0, 8), above, bl), (slice(40, 48), below, br)):
        cx[0:9, rows] = src[48:57] * (gl * flag)
        cx[9:41, rows] = src[57:89] * flag
        cx[41:50, rows] = src[89:98] * (gr * flag)
    for i, (src, flag) in enumerate(((above, bl), (below, br))):
        lines = flat(src[98:105])
        x = iota(lines.shape, 0)
        scale = jnp.where(x < 9, gl * flag, jnp.where(x < 41, flag, gr * flag))
        edge[i] = lines * scale
    op = (wx, ws, wl, di)
    weights(cx, 1, op, 0, 48, 127, False, edge)
    first_sweep(v, fx, op, 0, 48)
    sweep(v, fx, op, 1, 47)
    f1 = fine_restrict(v, fx, op, s)

    def pair(i, _):
        s[i, 8:40] = coef[2 * i] + coef[2 * i + 1]
        return 0

    lax.fori_loop(0, 16, pair, 0)
    c1 = dot(flat(pair_rows(s, 8, 16) * F32(0.25)), halver(128)).reshape(16, 16, 128)
    packed[...] = f1 + pltpu.roll(c1, 64, 2)


def mid_down(f1, v1, op1, f2, v2, op2, s, payload, extra):
    first_sweep(v1, f1, op1, 2, 46)
    sweep(v1, f1, op1, 3, 45)
    resid_pairs(v1, f1, op1, 4, 20, s)
    half = halver(128)
    f2[2:22] = dot(flat(pair_rows(s.at[0:20], 0, 24)), half).reshape(20, 24, 128)
    first_sweep(v2, f2, op2, 2, 22)
    sweep(v2, f2, op2, 3, 21)
    resid_pairs(v2, f2, op2, 8, 4, s.at[0:4, 0:24])
    send = collect(s, half, 0, F32(1.0))
    if extra is not None:
        send = send + extra
    payload[...] = jnp.broadcast_to(send[None], payload.shape)


def collect(s, half, lane, scale):
    total = jnp.zeros((12, 128), F32)
    lanes = iota((12, 128), 1)
    for x in range(4):
        pairs = flat(pair_rows(s.at[x : x + 1], 0, 12))
        cut = jnp.where(lanes < 16, dot(pairs * scale, half), F32(0.0))
        shift = lane + 16 * x
        total = total + (pltpu.roll(cut, shift, 1) if shift else cut)
    return total[4:8]


def mid_kernel(
    ng, nb, own, left, right, above, below,
    f1, v1, wx1, ws1, wl1, di1, f2, v2, wx2, ws2, wl2, di2, payload, c1, c2, s,
):
    gl, gr, bl, br = edge_flags(ng, nb)
    lanes = iota((16, 128), 1)

    def put(x, rows, slab, flag):
        f1[x, rows] = jnp.where(lanes < 64, slab, F32(0.0))
        c1[x, rows] = jnp.where(lanes < 64, pltpu.roll(slab, 64, 1) * flag, F32(0.0))

    for x in range(48):
        src, flag = ((left, gl), (own, None), (right, gr))[x // 16]
        fx = F32(1.0) if flag is None else flag
        put(x, slice(16, 32), src[x % 16], fx)
        put(x, slice(0, 16), above[x], fx * bl)
        put(x, slice(32, 48), below[x], fx * br)
    op1, op2 = (wx1, ws1, wl1, di1), (wx2, ws2, wl2, di2)
    weights(c1, 0, op1, 1, 47, 63, False)

    def pair(i, _):
        s[i] = c1[2 * i] + c1[2 * i + 1]
        return 0

    lax.fori_loop(0, 24, pair, 0)
    half = halver(128)
    c2[...] = dot(flat(pair_rows(s, 0, 24) * F32(0.25)), half).reshape(24, 24, 128)
    weights(c2, 0, op2, 1, 23, 31, False)
    for x in range(4):
        s[x, 0:24] = c2[8 + 2 * x] + c2[9 + 2 * x]
    extra = collect(s, half, 64, F32(0.25))
    mid_down(f1, v1, op1, f2, v2, op2, s, payload, extra)


def mid2_kernel(
    own, left, right, above, below, wx1, ws1, wl1, di1, wx2, ws2, wl2, di2,
    f1, v1, f2, v2, payload, s,
):
    lanes = iota((16, 128), 1)

    def put(x, rows, slab):
        if x % 16 >= 8:
            slab = pltpu.roll(slab, 64, 1)
        f1[x, rows] = jnp.where(lanes < 64, slab, F32(0.0))

    for x in range(48):
        i = x % 8
        put(x, slice(16, 32), (left, own, right)[x // 16][i])
        put(x, slice(0, 16), above[8 * (x // 16) + i])
        put(x, slice(32, 48), below[8 * (x // 16) + i])
    op1, op2 = (wx1, ws1, wl1, di1), (wx2, ws2, wl2, di2)
    mid_down(f1, v1, op1, f2, v2, op2, s, payload, None)


def apply3(p, wx, ws, wl, diag):
    zero = jnp.zeros_like(p[:1])
    q = wx * jnp.concatenate([p[1:], zero], 0)
    q = q + jnp.concatenate([zero, (wx * p)[:-1]], 0)
    q = q + (ws * up(p, 1) + down(ws * p, 1))
    q = q + (wl * up(p, 2) + down(wl * p, 2))
    return diag * p - q


def bottom(f4, c4, ny4):
    nx, nz, nl = c4.shape
    ch = c4 * F32(0.5)
    zero = jnp.zeros_like(ch[:1])
    rows, lanes, slabs = iota(c4.shape, 1), iota(c4.shape, 2), iota(c4.shape, 0)
    o = F32(0.0)
    x_up = ch + jnp.concatenate([ch[1:], zero], 0)
    x_dn = ch + jnp.concatenate([zero, ch[:-1]], 0)
    s_up = ch + jnp.where(rows == nz - 1, o, up(ch, 1))
    s_dn = ch + jnp.where(rows == 0, o, down(ch, 1))
    l_up = ch + jnp.where(lanes >= ny4 - 1, o, up(ch, 2))
    l_dn = ch + jnp.where(lanes == 0, o, down(ch, 2))
    diag = x_up + x_dn + s_up + s_dn + l_up + l_dn
    wx = jnp.where(slabs == nx - 1, o, x_up)
    ws = jnp.where(rows == nz - 1, o, s_up)
    wl = jnp.where(lanes >= ny4 - 1, o, l_up)

    def total(a):
        return jnp.sum(jnp.sum(a, axis=0))

    v = None
    r = p = f4
    rr = total(r * r)
    for i in range(NB):
        q = apply3(p, wx, ws, wl, diag)
        alpha = rr / total(p * q)
        v = alpha * p if v is None else v + alpha * p
        if i < NB - 1:
            r = r - alpha * q
            new = total(r * r)
            p = r + (new / rr) * p
            rr = new
    return v


def coarse(ng, nb, got, got_c, v3, f3, op3, c3, s3):
    n3, nl = 4 * ng, 4 * nb
    for g in range(ng):
        t = got[g * nl : (g + 1) * nl, :].T
        f3[4 + 4 * g : 8 + 4 * g] = t[0:64].reshape(4, 16, nl)
        if got_c is not got:
            t = got_c[g * nl : (g + 1) * nl, :].T
        c3[4 + 4 * g : 8 + 4 * g] = t[64:128].reshape(4, 16, nl)
    pad = jnp.zeros((4, 16, nl), F32)
    for ref in (v3, c3, op3[0]):
        ref[0:4] = pad
        ref[4 + n3 : 8 + n3] = pad
    weights(c3, 0, op3, 4, 4 + n3, nl - 1, True)
    lo, hi = 4, 4 + n3
    first_sweep(v3, f3, op3, lo, hi)
    sweep(v3, f3, op3, lo, hi)
    half = halver(nl)

    def pair(i, _):
        s3[i] = c3[4 + 2 * i] + c3[5 + 2 * i]
        return 0

    lax.fori_loop(0, n3 // 2, pair, 0)
    c4 = dot(flat(pair_rows(s3, 0, 8) * F32(0.25)), half).reshape(n3 // 2, 8, nl)
    resid_pairs(v3, f3, op3, 4, n3 // 2, s3)
    f4 = dot(flat(pair_rows(s3, 0, 8)), half).reshape(n3 // 2, 8, nl)
    v4 = bottom(f4, c4, nl // 2)
    e = dot(flat(v4), doubler(nl)).reshape(n3 // 2, 8, nl)
    s3[:, pl.ds(0, 8, stride=2), :] = e
    s3[:, pl.ds(1, 8, stride=2), :] = e

    def add(x, _):
        v3[4 + x] = v3[4 + x] + s3[x >> 1]
        return 0

    lax.fori_loop(0, n3, add, 0)
    sweep(v3, f3, op3, lo, hi)
    sweep(v3, f3, op3, lo, hi)


def coarse_to_mid(nb, v3, v2, s2, nl):
    g, b = lax.axis_index("grp"), lax.axis_index("box")
    for x in range(12):
        e = v3[4 * g + x]
        s2[x : x + 1, pl.ds(0, 16, stride=2), :] = e[None]
        s2[x : x + 1, pl.ds(1, 16, stride=2), :] = e[None]
    j, y = iota((24, nl), 0), iota((24, nl), 1)
    pick = jnp.where(y == 4 * b - 4 + (j >> 1), F32(1.0), F32(0.0))
    lanes = iota((24, 128), 1)
    zero = F32(0.0)
    for q in range(3):
        block = flat(s2[4 * q : 4 * q + 4])
        e = lax.dot_general(
            pick, block, (((1,), (1,)), ((), ())),
            precision=lax.Precision.HIGHEST, preferred_element_type=F32,
        )
        for i in range(4):
            part = e if i == 0 else pltpu.roll(e, 128 - 32 * i, 1)
            part = jnp.where(lanes < 32, part, zero)
            x = 2 * (4 * q + i)
            v2[x] = v2[x] + part
            v2[x + 1] = v2[x + 1] + part


def climb(ng, nb, got, got_c, v0, f0, op0, v1, f1, op1, v2, f2, op2, scr):
    v3, f3, c3, wx3, ws3, wl3, di3, s3, s2, es = scr
    op3 = (wx3, ws3, wl3, di3)
    coarse(ng, nb, got, got_c, v3, f3, op3, c3, s3)
    coarse_to_mid(nb, v3, v2, s2, 4 * nb)
    sweep(v2, f2, op2, 4, 20)
    sweep(v2, f2, op2, 5, 19)
    twice = doubler(128)
    e = dot(flat(v2[5:19]), twice).reshape(14, 24, 128)
    es[5:19, pl.ds(0, 24, stride=2), :] = e
    es[5:19, pl.ds(1, 24, stride=2), :] = e
    add_double(v1, es, 10, 38)
    sweep(v1, f1, op1, 11, 37)
    sweep(v1, f1, op1, 12, 36)
    e = dot(flat(v1[12:36, 12:36, :]), twice).reshape(24, 24, 128)
    es[:, pl.ds(0, 24, stride=2), :] = e
    es[:, pl.ds(1, 24, stride=2), :] = e


def turn_kernel(ng, nb, *refs):
    got, f0, wx0, ws0, wl0, di0, f1, wx1, ws1, wl1, di1, f2, wx2, ws2, wl2, di2 = refs[:16]
    v0i, v1i, v2i = refs[16:19]
    v0, packed = refs[19:21]
    v1, v2, s = refs[21:24]
    scr = refs[24:]
    v0[...] = v0i[...]
    v1[...] = v1i[...]
    v2[...] = v2i[...]
    op0, op1, op2 = (wx0, ws0, wl0, di0), (wx1, ws1, wl1, di1), (wx2, ws2, wl2, di2)
    climb(ng, nb, got, got, v0, f0, op0, v1, f1, op1, v2, f2, op2, scr)
    add_double(v0, scr[-1], 1, 47)
    for lo in (2, 3, 4, 5):
        sweep(v0, f0, op0, lo, 48 - lo)
    f1n = fine_restrict(v0, f0, op0, s)
    packed[...] = f1n[0:8] + pltpu.roll(f1n[8:16], 64, 2)


def end_kernel(ng, nb, *refs):
    got, got_c = refs[:2]
    f0, wx0, ws0, wl0, di0, f1, wx1, ws1, wl1, di1, f2, wx2, ws2, wl2, di2 = refs[2:17]
    v0i, v1i, v2i = refs[17:20]
    sol, res = refs[20:22]
    v0, v1, v2 = refs[22:25]
    scr = refs[25:]
    v0[...] = v0i[...]
    v1[...] = v1i[...]
    v2[...] = v2i[...]
    op0, op1, op2 = (wx0, ws0, wl0, di0), (wx1, ws1, wl1, di1), (wx2, ws2, wl2, di2)
    climb(ng, nb, got, got_c, v0, f0, op0, v1, f1, op1, v2, f2, op2, scr)
    add_double(v0, scr[-1], 5, 43)
    sweep(v0, f0, op0, 6, 42)
    sweep(v0, f0, op0, 7, 41)

    def step(x, _):
        sol[x] = v0[x + 8, 8:40]
        res[x] = resid(v0, f0, op0, x + 8)[8:40]
        return 0

    lax.fori_loop(0, 32, step, 0)


def ring(x, axis, n):
    before = lax.ppermute(x[0], axis, [(i, (i + 1) % n) for i in range(n)])
    after = lax.ppermute(x[1], axis, [(i, (i - 1) % n) for i in range(n)])
    return before, after


def gather_all(payload):
    got = lax.all_to_all(payload, ("grp", "box"), 0, 0, tiled=True)
    return got.reshape(got.shape[0] * got.shape[1], got.shape[2])


def make_body(ng, nb):
    big, mid, low = (48, 48, 128), (48, 48, 128), (24, 24, 128)
    n3, nl = 4 * ng, 4 * nb
    nd = ng * nb
    pay = (nd, 4, 128)
    lev3 = (n3 + 8, 16, nl)
    climb_scratch = [lev3] * 7 + [(n3 // 2, 16, nl), (12, 32, nl), (24, 48, 128)]

    def fix(kernel):
        return lambda *refs: kernel(ng, nb, *refs)

    def body(f, tags, table, rough):
        coef, to_next, to_prev = call(
            coef_kernel, (f, tags, table, rough), [(32, 32, 128), (17, 32, 128), (17, 32, 128)],
            smem=(2,),
        )
        left, right = ring((to_next, to_prev), "grp", ng)
        to_next, to_prev = call(rows_kernel, (f, coef, left, right), [(105, 8, 128)] * 2)
        above, below = ring((to_next, to_prev), "box", nb)
        v0, f0, wx0, ws0, wl0, di0, packed = call(
            fix(start_kernel), (f, coef, left, right, above, below), [big] * 6 + [(16, 16, 128)],
            scratch=[(50, 48, 128), (2, 56, 128), (16, 48, 128)],
        )
        l0 = (f0, wx0, ws0, wl0, di0)
        left, right = ring((packed, packed), "grp", ng)
        wide = jnp.concatenate([left, packed, right], 0)
        above, below = ring((wide, wide), "box", nb)
        f1, v1, wx1, ws1, wl1, di1, f2, v2, wx2, ws2, wl2, di2, payload = call(
            fix(mid_kernel), (packed, left, right, above, below), [mid] * 6 + [low] * 6 + [pay],
            scratch=[(48, 48, 128), (24, 24, 128), (24, 48, 128)],
        )
        got_c = gather_all(payload)
        l1, l2 = (f1, wx1, ws1, wl1, di1), (f2, wx2, ws2, wl2, di2)
        v0, packed = call(
            fix(turn_kernel), (got_c,) + l0 + l1 + l2 + (v0, v1, v2), [big, (8, 16, 128)],
            scratch=[mid, low, (16, 48, 128)] + climb_scratch,
        )
        left, right = ring((packed, packed), "grp", ng)
        wide = jnp.concatenate([left, packed, right], 0)
        above, below = ring((wide, wide), "box", nb)
        f1, v1, f2, v2, payload = call(
            mid2_kernel, (packed, left, right, above, below) + l1[1:] + l2[1:],
            [mid, mid, low, low, pay], scratch=[(24, 48, 128)],
        )
        got = gather_all(payload)
        l1, l2 = (f1,) + l1[1:], (f2,) + l2[1:]
        return tuple(call(
            fix(end_kernel), (got, got_c) + l0 + l1 + l2 + (v0, v1, v2), [(32, 32, 128)] * 2,
            scratch=[big, mid, low] + climb_scratch,
        ))

    return body


def solution(mesh):
    body = make_body(mesh.shape["grp"], mesh.shape["box"])
    return jax.shard_map(
        body,
        mesh=mesh,
        in_specs=(P("grp", "box", None), P("grp", "box", None), P(), P("grp", "box", None)),
        out_specs=(P("grp", "box", None), P("grp", "box", None)),
        check_vma=False,
    )
```

profile of v0, /device:TPU:1, one launch (start us, length us, event | category | flops | bytes accessed | tf_op | source)
XLA Modules:
  0.0 237.3 jit_solution(6814982743017993570)
XLA Ops:
  0.6 2.9 %shard_map.59 = (f32[32,32,128]{2,1,0:T(8,128)}, f32[17,32,128]{2,1,0:T(8,128)}, f32[17,32,128]{2,1,0:T(8,128)}) custom-call(f32[32,32,128]{2,1,0:T(8,128)} %refs_0_.1, s32[32,32,128]{2,1,0:T(8,128)} %tags.1, f32[8]{0:T(128)} %table.1, f32[32,32,128]{2,1,0:T(8,128)} %rough.1), custom_call_target="tpu_custom_call" | custom-call | tf_op jit(solution)/shard_map/pallas_call | solution.py:21
  3.5 2.6 %collective-permute-start = (f32[17,32,128]{2,1,0:T(8,128)}, f32[17,32,128]{2,1,0:T(8,128)S(1)}, u32[]{:S(2)}, u32[]{:S(2)}) collective-permute-start(f32[17,32,128]{2,1,0:T(8,128)} %get-tuple-element.35), channel_id=1, source_target_pairs={{0,32},{32,64},{64,96},{96,128},{128,160},{160,192},{192,224},{224... | collective-permute-start | bytes 835592 | tf_op jit(solution)/shard_map/ppermute | solution.py:496
  6.7 3.2 %collective-permute-done.left.refs_2_ = f32[17,32,128]{2,1,0:T(8,128)S(1)} collective-permute-done((f32[17,32,128]{2,1,0:T(8,128)}, f32[17,32,128]{2,1,0:T(8,128)S(1)}, u32[]{:S(2)}, u32[]{:S(2)}) %collective-permute-start) | collective-permute-done | bytes 278560 | tf_op jit(solution)/shard_map/ppermute | solution.py:496
  9.9 2.7 %collective-permute-done.1.right.refs_3_ = f32[17,32,128]{2,1,0:T(8,128)S(1)} collective-permute-done((f32[17,32,128]{2,1,0:T(8,128)}, f32[17,32,128]{2,1,0:T(8,128)S(1)}, u32[]{:S(2)}, u32[]{:S(2)}) %collective-permute-start.1) | collective-permute-done | bytes 278560 | tf_op jit(solution)/shard_map/ppermute | solution.py:497
  12.6 0.7 copy-done.1
  13.3 2.3 shard_map.60
  15.6 1.3 collective-permute-start.2
  17.0 6.4 %collective-permute-start.3 = (f32[105,8,128]{2,1,0:T(8,128)}, f32[105,8,128]{2,1,0:T(8,128)S(1)}, u32[]{:S(2)}, u32[]{:S(2)}) collective-permute-start(f32[105,8,128]{2,1,0:T(8,128)} %get-tuple-element.38), channel_id=1, source_target_pairs={{0,31},{1,0},{2,1},{3,2},{4,3},{5,4},{6,5},{7,6},{8,7},{9,8},{10,9... | collective-permute-start | bytes 1290248 | tf_op jit(solution)/shard_map/ppermute | solution.py:497
  23.3 10.4 %collective-permute-done.2.refs_4_ = f32[105,8,128]{2,1,0:T(8,128)S(1)} collective-permute-done((f32[105,8,128]{2,1,0:T(8,128)}, f32[105,8,128]{2,1,0:T(8,128)S(1)}, u32[]{:S(2)}, u32[]{:S(2)}) %collective-permute-start.2) | collective-permute-done | bytes 430112 | tf_op jit(solution)/shard_map/ppermute | solution.py:496
  33.7 0.8 copy-done.4
  34.5 0.8 copy-done.5
  35.2 13.6 %shard_map.61 = (f32[48,48,128]{2,1,0:T(8,128)}, f32[48,48,128]{2,1,0:T(8,128)}, f32[48,48,128]{2,1,0:T(8,128)}, f32[48,48,128]{2,1,0:T(8,128)}, f32[48,48,128]{...) custom-call(f32[32,32,128]{2,1,0:T(8,128)} %refs_0_.1, f32[32,32,128]{2,1,0:T(8,128)} %get-tuple-element.34.coef.refs_1_, ...), custom_call_target="tpu_custom_call" | custom-call | tf_op jit(solution)/shard_map/pallas_call | solution.py:21
  49.5 1.7 collective-permute-done.4.refs_1_
  51.3 1.0 constant_dynamic-update-slice_fusion.1
  52.2 1.7 collective-permute-done.5.refs_2_
  53.9 4.7 %collective-permute-start.7 = (f32[48,16,128]{2,1,0:T(8,128)S(1)}, f32[48,16,128]{2,1,0:T(8,128)S(1)}, u32[]{:S(2)}, u32[]{:S(2)}) collective-permute-start(f32[48,16,128]{2,1,0:T(8,128)S(1)} %constant_dynamic-update-slice_fusion), channel_id=1, source_target_pairs={{0,31},{1,0},{2,1},{3,2},{4,3},{5,4},{6,5},{7,6},{8,7},{9,8},{10,9... | collective-permute-start | bytes 1179656 | tf_op jit(solution)/shard_map/ppermute | solution.py:497
  58.6 6.6 %collective-permute-done.7.refs_4_ = f32[48,16,128]{2,1,0:T(8,128)S(1)} collective-permute-done((f32[48,16,128]{2,1,0:T(8,128)S(1)}, f32[48,16,128]{2,1,0:T(8,128)S(1)}, u32[]{:S(2)}, u32[]{:S(2)}) %collective-permute-start.7) | collective-permute-done | bytes 393248 | tf_op jit(solution)/shard_map/ppermute | solution.py:497
  65.2 5.2 %collective-permute-done.6.refs_3_ = f32[48,16,128]{2,1,0:T(8,128)S(1)} collective-permute-done((f32[48,16,128]{2,1,0:T(8,128)S(1)}, f32[48,16,128]{2,1,0:T(8,128)S(1)}, u32[]{:S(2)}, u32[]{:S(2)}) %collective-permute-start.6) | collective-permute-done | bytes 393248 | tf_op jit(solution)/shard_map/ppermute | solution.py:496
  70.5 0.7 copy-done.7
  71.2 18.5 %shard_map.62 = (f32[48,48,128]{2,1,0:T(8,128)}, f32[48,48,128]{2,1,0:T(8,128)}, f32[48,48,128]{2,1,0:T(8,128)}, f32[48,48,128]{2,1,0:T(8,128)}, f32[48,48,128]{...) custom-call(f32[16,16,128]{2,1,0:T(8,128)} %get-tuple-element.39.ref, ...), custom_call_target="tpu_custom_call" | custom-call | tf_op jit(solution)/shard_map/pallas_call | solution.py:21
  89.7 30.8 %all_to_all.10 = f32[256,4,128]{2,1,0:T(4,128)} all-to-all(f32[256,4,128]{2,1,0:T(4,128)} %get-tuple-element.40), channel_id=1, replica_groups=mesh['grp'=8,'box'=32] {'grp','box'}, dimensions={0} | all-to-all | bytes 1048576 | tf_op jit(solution)/shard_map/all_to_all | solution.py:502
  120.5 32.7 %shard_map.63 = (f32[48,48,128]{2,1,0:T(8,128)}, f32[8,16,128]{2,1,0:T(8,128)}) custom-call(f32[1024,128]{1,0:T(8,128)} %bitcast.2, f32[48,48,128]{2,1,0:T(8,128)} %get-tuple-element.41.refs_1_.refs_2_, f32[48,48,128]{2,1,0:T(8,128)} %get-tuple-element.42.refs_2_.refs_3_, f32[48,48,128]{2,1,0:T(8,128)} %get-tuple-element.43.refs_3_.refs_4_, ...), custom_call_target="tpu_custom_call" | custom-call | tf_op jit(solution)/shard_map/pallas_call | solution.py:21
  153.8 1.6 collective-permute-done.8.left
  155.5 0.9 constant_dynamic-update-slice_fusion.4
  156.3 1.7 collective-permute-done.9.right
  158.4 1.2 collective-permute-start.10
  159.6 3.1 %collective-permute-done.11.below = f32[24,16,128]{2,1,0:T(8,128)S(1)} collective-permute-done((f32[24,16,128]{2,1,0:T(8,128)S(1)}, f32[24,16,128]{2,1,0:T(8,128)S(1)}, u32[]{:S(2)}, u32[]{:S(2)}) %collective-permute-start.11) | collective-permute-done | bytes 196640 | tf_op jit(solution)/shard_map/ppermute | solution.py:497
  162.6 3.6 %collective-permute-done.10.above = f32[24,16,128]{2,1,0:T(8,128)S(1)} collective-permute-done((f32[24,16,128]{2,1,0:T(8,128)S(1)}, f32[24,16,128]{2,1,0:T(8,128)S(1)}, u32[]{:S(2)}, u32[]{:S(2)}) %collective-permute-start.10) | collective-permute-done | bytes 196640 | tf_op jit(solution)/shard_map/ppermute | solution.py:496
  166.2 0.7 copy-done.11
  166.9 10.6 %shard_map.64 = (f32[48,48,128]{2,1,0:T(8,128)}, f32[48,48,128]{2,1,0:T(8,128)}, f32[24,24,128]{2,1,0:T(8,128)}, f32[24,24,128]{2,1,0:T(8,128)}, f32[256,4,128]{2,1,0:T(4,128)}) custom-call(f32[8,16,128]{2,1,0:T(8,128)} %get-tuple-element.59.own, f32[8,16,128]{2,1,0:T(8,128)} %copy-done.8, f32[8,16,128]{2,1,0:T(8,128)} %copy-done.9, ...), custom_call_target="tpu_custom_call" | custom-call | tf_op jit(solution)/shard_map/pallas_call | solution.py:21
  177.5 30.6 %all_to_all.11 = f32[256,4,128]{2,1,0:T(4,128)} all-to-all(f32[256,4,128]{2,1,0:T(4,128)} %get-tuple-element.60), channel_id=1, replica_groups=mesh['grp'=8,'box'=32] {'grp','box'}, dimensions={0} | all-to-all | bytes 1048576 | tf_op jit(solution)/shard_map/all_to_all | solution.py:502
  208.1 29.1 %shard_map.65 = (f32[32,32,128]{2,1,0:T(8,128)}, f32[32,32,128]{2,1,0:T(8,128)}) custom-call(f32[1024,128]{1,0:T(8,128)} %bitcast.4, f32[1024,128]{1,0:T(8,128)} %bitcast.3, f32[48,48,128]{2,1,0:T(8,128)} %get-tuple-element.41.refs_1_.refs_2_, f32[48,48,128]{2,1,0:T(8,128)} %get-tuple-element.42.refs_2_.refs_3_, ...), custom_call_target="tpu_custom_call" | custom-call | tf_op jit(solution)/shard_map/pallas_call | solution.py:21
  (31 shorter events, 2.4 us)
Async XLA Ops:
  3.5 6.4 %collective-permute-start = (f32[17,32,128]{2,1,0:T(8,128)}, f32[17,32,128]{2,1,0:T(8,128)S(1)}, u32[]{:S(2)}, u32[]{:S(2)}) collective-permute-start(f32[17,32,128]{2,1,0:T(8,128)} %get-tuple-element.35), channel_id=1, source_target_pairs={{0,32},{32,64},{64,96},{96,128},{128,160},{160,192},{192,224},{224... | collective-permute-start | bytes 835592 | tf_op jit(solution)/shard_map/ppermute | solution.py:496
  6.1 6.5 %collective-permute-start.1 = (f32[17,32,128]{2,1,0:T(8,128)}, f32[17,32,128]{2,1,0:T(8,128)S(1)}, u32[]{:S(2)}, u32[]{:S(2)}) collective-permute-start(f32[17,32,128]{2,1,0:T(8,128)} %get-tuple-element.36), channel_id=1, source_target_pairs={{0,224},{32,0},{64,32},{96,64},{128,96},{160,128},{192,160},{224,1... | collective-permute-start | bytes 835592 | tf_op jit(solution)/shard_map/ppermute | solution.py:497
  9.9 2.7 %copy-start = (f32[17,32,128]{2,1,0:T(8,128)}, f32[17,32,128]{2,1,0:T(8,128)S(1)}, u32[]{:S(2)}) copy-start(f32[17,32,128]{2,1,0:T(8,128)S(1)} %collective-permute-done.left.refs_2_) | copy-start | bytes 835588
  12.6 0.7 copy-start.1
  15.6 18.1 %collective-permute-start.2 = (f32[105,8,128]{2,1,0:T(8,128)}, f32[105,8,128]{2,1,0:T(8,128)S(1)}, u32[]{:S(2)}, u32[]{:S(2)}) collective-permute-start(f32[105,8,128]{2,1,0:T(8,128)} %get-tuple-element.37), channel_id=1, source_target_pairs={{0,1},{1,2},{2,3},{3,4},{4,5},{5,6},{6,7},{7,8},{8,9},{9,10},{10,1... | collective-permute-start | bytes 1290248 | tf_op jit(solution)/shard_map/ppermute | solution.py:496
  17.0 16.8 %collective-permute-start.3 = (f32[105,8,128]{2,1,0:T(8,128)}, f32[105,8,128]{2,1,0:T(8,128)S(1)}, u32[]{:S(2)}, u32[]{:S(2)}) collective-permute-start(f32[105,8,128]{2,1,0:T(8,128)} %get-tuple-element.38), channel_id=1, source_target_pairs={{0,31},{1,0},{2,1},{3,2},{4,3},{5,4},{6,5},{7,6},{8,7},{9,8},{10,9... | collective-permute-start | bytes 1290248 | tf_op jit(solution)/shard_map/ppermute | solution.py:497
  33.7 0.8 copy-start.4
  34.5 0.8 copy-start.5
  48.8 2.4 %collective-permute-start.4 = (f32[16,16,128]{2,1,0:T(8,128)}, f32[16,16,128]{2,1,0:T(8,128)S(1)}, u32[]{:S(2)}, u32[]{:S(2)}) collective-permute-start(f32[16,16,128]{2,1,0:T(8,128)} %get-tuple-element.39.refs_0_), channel_id=1, source_target_pairs={{0,32},{32,64},{64,96},{96,128},{128,160},{160,192},{192,224},{224... | collective-permute-start | bytes 393224 | tf_op jit(solution)/shard_map/ppermute | solution.py:496
  49.0 4.9 %collective-permute-start.5 = (f32[16,16,128]{2,1,0:T(8,128)}, f32[16,16,128]{2,1,0:T(8,128)S(1)}, u32[]{:S(2)}, u32[]{:S(2)}) collective-permute-start(f32[16,16,128]{2,1,0:T(8,128)} %get-tuple-element.39.refs_0_), channel_id=1, source_target_pairs={{0,224},{32,0},{64,32},{96,64},{128,96},{160,128},{192,160},{224,1... | collective-permute-start | bytes 393224 | tf_op jit(solution)/shard_map/ppermute | solution.py:497
  51.3 19.2 %copy-start.2 = (f32[16,16,128]{2,1,0:T(8,128)}, f32[16,16,128]{2,1,0:T(8,128)S(1)}, u32[]{:S(2)}) copy-start(f32[16,16,128]{2,1,0:T(8,128)S(1)} %collective-permute-done.4.refs_1_) | copy-start | bytes 393220
  53.9 16.5 %copy-start.3 = (f32[16,16,128]{2,1,0:T(8,128)}, f32[16,16,128]{2,1,0:T(8,128)S(1)}, u32[]{:S(2)}) copy-start(f32[16,16,128]{2,1,0:T(8,128)S(1)} %collective-permute-done.5.refs_2_) | copy-start | bytes 393220
  53.9 11.3 %collective-permute-start.7 = (f32[48,16,128]{2,1,0:T(8,128)S(1)}, f32[48,16,128]{2,1,0:T(8,128)S(1)}, u32[]{:S(2)}, u32[]{:S(2)}) collective-permute-start(f32[48,16,128]{2,1,0:T(8,128)S(1)} %constant_dynamic-update-slice_fusion), channel_id=1, source_target_pairs={{0,31},{1,0},{2,1},{3,2},{4,3},{5,4},{6,5},{7,6},{8,7},{9,8},{10,9... | collective-permute-start | bytes 1179656 | tf_op jit(solution)/shard_map/ppermute | solution.py:497
  58.6 11.8 %collective-permute-start.6 = (f32[48,16,128]{2,1,0:T(8,128)S(1)}, f32[48,16,128]{2,1,0:T(8,128)S(1)}, u32[]{:S(2)}, u32[]{:S(2)}) collective-permute-start(f32[48,16,128]{2,1,0:T(8,128)S(1)} %constant_dynamic-update-slice_fusion), channel_id=1, source_target_pairs={{0,1},{1,2},{2,3},{3,4},{4,5},{5,6},{6,7},{7,8},{8,9},{9,10},{10,1... | collective-permute-start | bytes 1179656 | tf_op jit(solution)/shard_map/ppermute | solution.py:496
  65.2 5.2 %copy-start.6 = (f32[48,16,128]{2,1,0:T(8,128)}, f32[48,16,128]{2,1,0:T(8,128)S(1)}, u32[]{:S(2)}) copy-start(f32[48,16,128]{2,1,0:T(8,128)S(1)} %collective-permute-done.7.refs_4_) | copy-start | bytes 1179652
  70.4 0.7 copy-start.7
  153.2 2.2 collective-permute-start.8
  153.8 4.2 %collective-permute-start.9 = (f32[8,16,128]{2,1,0:T(8,128)}, f32[8,16,128]{2,1,0:T(8,128)S(1)}, u32[]{:S(2)}, u32[]{:S(2)}) collective-permute-start(f32[8,16,128]{2,1,0:T(8,128)} %get-tuple-element.59.own), channel_id=1, source_target_pairs={{0,224},{32,0},{64,32},{96,64},{128,96},{160,128},{192,160},{224,1... | collective-permute-start | bytes 196616 | tf_op jit(solution)/shard_map/ppermute | solution.py:497
  155.4 10.8 %copy-start.8 = (f32[8,16,128]{2,1,0:T(8,128)}, f32[8,16,128]{2,1,0:T(8,128)S(1)}, u32[]{:S(2)}) copy-start(f32[8,16,128]{2,1,0:T(8,128)S(1)} %collective-permute-done.8.left) | copy-start | bytes 196612
  158.0 8.2 %copy-start.9 = (f32[8,16,128]{2,1,0:T(8,128)}, f32[8,16,128]{2,1,0:T(8,128)S(1)}, u32[]{:S(2)}) copy-start(f32[8,16,128]{2,1,0:T(8,128)S(1)} %collective-permute-done.9.right) | copy-start | bytes 196612
  158.0 4.6 %collective-permute-start.11 = (f32[24,16,128]{2,1,0:T(8,128)S(1)}, f32[24,16,128]{2,1,0:T(8,128)S(1)}, u32[]{:S(2)}, u32[]{:S(2)}) collective-permute-start(f32[24,16,128]{2,1,0:T(8,128)S(1)} %constant_dynamic-update-slice_fusion.3), channel_id=1, source_target_pairs={{0,31},{1,0},{2,1},{3,2},{4,3},{5,4},{6,5},{7,6},{8,7},{9,8},{10,9... | collective-permute-start | bytes 589832 | tf_op jit(solution)/shard_map/ppermute | solution.py:497
  158.4 7.8 %collective-permute-start.10 = (f32[24,16,128]{2,1,0:T(8,128)S(1)}, f32[24,16,128]{2,1,0:T(8,128)S(1)}, u32[]{:S(2)}, u32[]{:S(2)}) collective-permute-start(f32[24,16,128]{2,1,0:T(8,128)S(1)} %constant_dynamic-update-slice_fusion.3), channel_id=1, source_target_pairs={{0,1},{1,2},{2,3},{3,4},{4,5},{5,6},{6,7},{7,8},{8,9},{9,10},{10,1... | collective-permute-start | bytes 589832 | tf_op jit(solution)/shard_map/ppermute | solution.py:496
  162.6 3.6 %copy-start.10 = (f32[24,16,128]{2,1,0:T(8,128)}, f32[24,16,128]{2,1,0:T(8,128)S(1)}, u32[]{:S(2)}) copy-start(f32[24,16,128]{2,1,0:T(8,128)S(1)} %collective-permute-done.11.below) | copy-start | bytes 589828
  166.2 0.7 copy-start.11
where the time goes:
time: 238 us; the launch traced here: 237 us
  Pallas kernels  110 us (46%)
  blocking collectives  61.4 us (26%)
  waiting for transfers between devices  41.4 us (17%)
  starting transfers between devices  18.5 us (8%)
  local copies, waits for them, and re-layouts  5.53 us (2%)
    pallas_call x7, Pallas kernels, call(): pl.pallas_call(kernel, out_shape=[jax.ShapeDtypeStruct(s, F32) for s in o...  110 us
    all_to_all x2, blocking collectives, gather_all(): got = lax.all_to_all(payload, ('grp', 'box'), 0, 0, tiled=True)  61.4 us
    ppermute x6, waiting for transfers between devices, ring(): before = lax.ppermute(x[0], axis, [(i, (i + 1) % n) for i in range(n)])  25.8 us
    ppermute x6, waiting for transfers between devices, ring(): after = lax.ppermute(x[1], axis, [(i, (i - 1) % n) for i in range(n)])  15.6 us
    ppermute x6, starting transfers between devices, ring(): after = lax.ppermute(x[1], axis, [(i, (i - 1) % n) for i in range(n)])  12.6 us
    ppermute x6, starting transfers between devices, ring(): before = lax.ppermute(x[0], axis, [(i, (i + 1) % n) for i in range(n)])  5.88 us
    unnamed x28, local copies, waits for them, and re-layouts  5.51 us
  transfers between devices with their start and end apart: 12, of which 11 were waited for; matrix products, arithmetic and copies ran while one was open for 1% of the time, Pallas kernels for 0%

commit v1 on v0

--- a/solution.py
+++ b/solution.py
@@ -11,22 +11,33 @@
 
 
 def params():
-    return pltpu.CompilerParams(vmem_limit_bytes=56 << 20)
-
-
-def call(kernel, ins, outs, scratch=(), smem=()):
+    return pltpu.CompilerParams(vmem_limit_bytes=24 << 20)
+
+
+def call(kernel, ins, outs, scratch=(), smem=(), leave=(), aliases=None):
+    def shape_of(i, s):
+        if INTERPRET or i in leave:
+            return jax.ShapeDtypeStruct(s, F32)
+        return pltpu.VMEM(s, F32)
+
+    def place(i, x):
+        if INTERPRET or i in smem:
+            return x
+        return pltpu.with_memory_space_constraint(x, pltpu.VMEM)
+
     specs = [
         pl.BlockSpec(memory_space=pltpu.SMEM if i in smem else pltpu.VMEM) for i in range(len(ins))
     ]
     return pl.pallas_call(
         kernel,
-        out_shape=[jax.ShapeDtypeStruct(s, F32) for s in outs],
+        out_shape=[shape_of(i, s) for i, s in enumerate(outs)],
         in_specs=specs,
         out_specs=[pl.BlockSpec(memory_space=pltpu.VMEM) for _ in outs],
         scratch_shapes=[pltpu.VMEM(s, F32) for s in scratch],
         compiler_params=params(),
+        input_output_aliases=aliases or {},
         interpret=INTERPRET,
-    )(*ins)
+    )(*[place(i, x) for i, x in enumerate(ins)])
 
 
 def iota(shape, dim):
@@ -243,6 +254,13 @@
     packed[...] = f1 + pltpu.roll(c1, 64, 2)
 
 
+def fold_rows(send):
+    lanes = iota((2, 128), 1)
+    even = jnp.concatenate([send[0:1], send[2:3]], 0)
+    odd = jnp.concatenate([send[1:2], send[3:4]], 0)
+    return jnp.where(lanes < 64, even, pltpu.roll(odd, 64, 1))
+
+
 def mid_down(f1, v1, op1, f2, v2, op2, s, payload, extra):
     first_sweep(v1, f1, op1, 2, 46)
     sweep(v1, f1, op1, 3, 45)
@@ -253,8 +271,7 @@
     sweep(v2, f2, op2, 3, 21)
     resid_pairs(v2, f2, op2, 8, 4, s.at[0:4, 0:24])
     send = collect(s, half, 0, F32(1.0))
-    if extra is not None:
-        send = send + extra
+    send = fold_rows(send) if extra is None else send + extra
     payload[...] = jnp.broadcast_to(send[None], payload.shape)
 
 
@@ -370,11 +387,19 @@
 def coarse(ng, nb, got, got_c, v3, f3, op3, c3, s3):
     n3, nl = 4 * ng, 4 * nb
     for g in range(ng):
-        t = got[g * nl : (g + 1) * nl, :].T
-        f3[4 + 4 * g : 8 + 4 * g] = t[0:64].reshape(4, 16, nl)
-        if got_c is not got:
-            t = got_c[g * nl : (g + 1) * nl, :].T
-        c3[4 + 4 * g : 8 + 4 * g] = t[64:128].reshape(4, 16, nl)
+        slabs = slice(4 + 4 * g, 8 + 4 * g)
+        t = got_c[g * nl : (g + 1) * nl, :].T
+        c3[slabs] = t[64:128].reshape(4, 16, nl)
+        if got is None:
+            f3[slabs] = t[0:64].reshape(4, 16, nl)
+    if got is not None:
+        k, y = iota((nl // 2, nl), 0), iota((nl // 2, nl), 1)
+        even = jnp.where(y == 2 * k, F32(1.0), F32(0.0))
+        odd = jnp.where(y == 2 * k + 1, F32(1.0), F32(0.0))
+        ts = [got[g * (nl // 2) : (g + 1) * (nl // 2), :].T for g in range(ng)]
+        lhs0 = jnp.concatenate([t[0:64] for t in ts], 0)
+        lhs1 = jnp.concatenate([t[64:128] for t in ts], 0)
+        f3[4 : 4 + n3] = (dot(lhs0, even) + dot(lhs1, odd)).reshape(n3, 16, nl)
     pad = jnp.zeros((4, 16, nl), F32)
     for ref in (v3, c3, op3[0]):
         ref[0:4] = pad
@@ -456,11 +481,10 @@
     v0, packed = refs[19:21]
     v1, v2, s = refs[21:24]
     scr = refs[24:]
-    v0[...] = v0i[...]
     v1[...] = v1i[...]
     v2[...] = v2i[...]
     op0, op1, op2 = (wx0, ws0, wl0, di0), (wx1, ws1, wl1, di1), (wx2, ws2, wl2, di2)
-    climb(ng, nb, got, got, v0, f0, op0, v1, f1, op1, v2, f2, op2, scr)
+    climb(ng, nb, None, got, v0, f0, op0, v1, f1, op1, v2, f2, op2, scr)
     add_double(v0, scr[-1], 1, 47)
     for lo in (2, 3, 4, 5):
         sweep(v0, f0, op0, lo, 48 - lo)
@@ -507,7 +531,7 @@
     big, mid, low = (48, 48, 128), (48, 48, 128), (24, 24, 128)
     n3, nl = 4 * ng, 4 * nb
     nd = ng * nb
-    pay = (nd, 4, 128)
+    pay, pay2 = (nd, 4, 128), (nd, 2, 128)
     lev3 = (n3 + 8, 16, nl)
     climb_scratch = [lev3] * 7 + [(n3 // 2, 16, nl), (12, 32, nl), (24, 48, 128)]
 
@@ -532,26 +556,26 @@
         above, below = ring((wide, wide), "box", nb)
         f1, v1, wx1, ws1, wl1, di1, f2, v2, wx2, ws2, wl2, di2, payload = call(
             fix(mid_kernel), (packed, left, right, above, below), [mid] * 6 + [low] * 6 + [pay],
-            scratch=[(48, 48, 128), (24, 24, 128), (24, 48, 128)],
+            scratch=[(48, 48, 128), (24, 24, 128), (24, 48, 128)], leave=(12,),
         )
         got_c = gather_all(payload)
         l1, l2 = (f1, wx1, ws1, wl1, di1), (f2, wx2, ws2, wl2, di2)
         v0, packed = call(
             fix(turn_kernel), (got_c,) + l0 + l1 + l2 + (v0, v1, v2), [big, (8, 16, 128)],
-            scratch=[mid, low, (16, 48, 128)] + climb_scratch,
+            aliases={16: 0}, scratch=[mid, low, (16, 48, 128)] + climb_scratch,
         )
         left, right = ring((packed, packed), "grp", ng)
         wide = jnp.concatenate([left, packed, right], 0)
         above, below = ring((wide, wide), "box", nb)
         f1, v1, f2, v2, payload = call(
             mid2_kernel, (packed, left, right, above, below) + l1[1:] + l2[1:],
-            [mid, mid, low, low, pay], scratch=[(24, 48, 128)],
+            [mid, mid, low, low, pay2], scratch=[(24, 48, 128)], leave=(4,),
         )
         got = gather_all(payload)
         l1, l2 = (f1,) + l1[1:], (f2,) + l2[1:]
         return tuple(call(
             fix(end_kernel), (got, got_c) + l0 + l1 + l2 + (v0, v1, v2), [(32, 32, 128)] * 2,
-            scratch=[big, mid, low] + climb_scratch,
+            scratch=[big, mid, low] + climb_scratch, leave=(0, 1),
         ))
 
     return body

time: 238 us -> 201 us (0.84)
  Pallas kernels: 110 us -> 82.2 us
  blocking collectives: 61.4 us -> 50.7 us
  waiting for transfers between devices: 41.4 us -> 44.1 us
    pallas_call x7, Pallas kernels: 110 us -> 82.2 us  [call(): pl.pallas_call(kernel, out_shape=[shape_of(i, s) for i, s in enumerate(ou...]
    all_to_all x2, blocking collectives: 61.4 us -> 50.7 us  [gather_all(): got = lax.all_to_all(payload, ('grp', 'box'), 0, 0, tiled=True)]
    ppermute x6, waiting for transfers between devices: 15.6 us -> 19.6 us  [ring(): after = lax.ppermute(x[1], axis, [(i, (i - 1) % n) for i in range(n)])]
    unnamed x28 -> x12, local copies, waits for them, and re-layouts: 5.51 us -> 3.8 us
  transfers between devices with their start and end apart: 12 -> 12, of which waited for: 11 -> 11; matrix products, arithmetic and copies ran while one was open for 1% -> 0% of each run, Pallas kernels for 0% -> 0%
where the time goes in v1:
time: 201 us
  Pallas kernels  82.2 us (41%)
  blocking collectives  50.7 us (25%)
  waiting for transfers between devices  44.1 us (22%)
  starting transfers between devices  19.5 us (10%)
  local copies, waits for them, and re-layouts  3.82 us (2%)
    pallas_call x7, Pallas kernels, call(): pl.pallas_call(kernel, out_shape=[shape_of(i, s) for i, s in enumerate(ou...  82.2 us
    all_to_all x2, blocking collectives, gather_all(): got = lax.all_to_all(payload, ('grp', 'box'), 0, 0, tiled=True)  50.7 us
    ppermute x6, waiting for transfers between devices, ring(): before = lax.ppermute(x[0], axis, [(i, (i + 1) % n) for i in range(n)])  24.5 us
    ppermute x6, waiting for transfers between devices, ring(): after = lax.ppermute(x[1], axis, [(i, (i - 1) % n) for i in range(n)])  19.6 us
    ppermute x6, starting transfers between devices, ring(): after = lax.ppermute(x[1], axis, [(i, (i - 1) % n) for i in range(n)])  13.8 us
    ppermute x6, starting transfers between devices, ring(): before = lax.ppermute(x[0], axis, [(i, (i + 1) % n) for i in range(n)])  5.67 us
  transfers between devices with their start and end apart: 12, of which 11 were waited for; matrix products, arithmetic and copies ran while one was open for 0% of the time, Pallas kernels for 0%

profile of v1, /device:TPU:1, one launch (start us, length us, event | category | flops | bytes accessed | tf_op | source)
XLA Modules:
  0.0 201.0 jit_solution(7446773523826874525)
XLA Ops:
  0.6 1.0 copy-done
  1.7 1.0 copy-done.1
  2.7 1.0 copy-done.2
  3.8 0.7 copy-done.3
  4.4 1.1 shard_map.59
  5.5 2.6 %collective-permute-start = (f32[17,32,128]{2,1,0:T(8,128)S(1)}, f32[17,32,128]{2,1,0:T(8,128)S(1)}, u32[]{:S(2)}, u32[]{:S(2)}) collective-permute-start(f32[17,32,128]{2,1,0:T(8,128)S(1)} %get-tuple-element.35), channel_id=1, source_target_pairs={{0,32},{32,64},{64,96},{96,128},{128,160},{160,192},{192,224},{224... | collective-permute-start | bytes 835592 | tf_op jit(solution)/shard_map/ppermute | solution.py:520
  8.1 0.7 collective-permute-start.1
  8.8 2.8 %collective-permute-done.left.refs_2_ = f32[17,32,128]{2,1,0:T(8,128)S(1)} collective-permute-done((f32[17,32,128]{2,1,0:T(8,128)S(1)}, f32[17,32,128]{2,1,0:T(8,128)S(1)}, u32[]{:S(2)}, u32[]{:S(2)}) %collective-permute-start) | collective-permute-done | bytes 278560 | tf_op jit(solution)/shard_map/ppermute | solution.py:520
  11.6 2.8 %collective-permute-done.1.right.refs_3_ = f32[17,32,128]{2,1,0:T(8,128)S(1)} collective-permute-done((f32[17,32,128]{2,1,0:T(8,128)S(1)}, f32[17,32,128]{2,1,0:T(8,128)S(1)}, u32[]{:S(2)}, u32[]{:S(2)}) %collective-permute-start.1) | collective-permute-done | bytes 278560 | tf_op jit(solution)/shard_map/ppermute | solution.py:521
  14.5 1.4 collective-permute-start.2
  15.9 6.5 %collective-permute-start.3 = (f32[105,8,128]{2,1,0:T(8,128)S(1)}, f32[105,8,128]{2,1,0:T(8,128)S(1)}, u32[]{:S(2)}, u32[]{:S(2)}) collective-permute-start(f32[105,8,128]{2,1,0:T(8,128)S(1)} %get-tuple-element.38), channel_id=1, source_target_pairs={{0,31},{1,0},{2,1},{3,2},{4,3},{5,4},{6,5},{7,6},{8,7},{9,8},{10,9... | collective-permute-start | bytes 1290248 | tf_op jit(solution)/shard_map/ppermute | solution.py:521
  22.4 10.1 %collective-permute-done.2.refs_4_ = f32[105,8,128]{2,1,0:T(8,128)S(1)} collective-permute-done((f32[105,8,128]{2,1,0:T(8,128)S(1)}, f32[105,8,128]{2,1,0:T(8,128)S(1)}, u32[]{:S(2)}, u32[]{:S(2)}) %collective-permute-start.2) | collective-permute-done | bytes 430112 | tf_op jit(solution)/shard_map/ppermute | solution.py:520
  32.4 9.4 %shard_map.61 = (f32[48,48,128]{2,1,0:T(8,128)S(1)}, f32[48,48,128]{2,1,0:T(8,128)S(1)}, f32[48,48,128]{2,1,0:T(8,128)S(1)}, f32[48,48,128]{2,1,0:T(8,128)S(1)},...) custom-call(f32[32,32,128]{2,1,0:T(8,128)S(1)} %copy-done, ...), custom_call_target="tpu_custom_call" | custom-call | tf_op jit(solution)/shard_map/pallas_call | solution.py:31
  41.9 0.7 collective-permute-start.5
  42.6 1.2 collective-permute-done.4.refs_1_
  43.9 2.7 %collective-permute-done.5.refs_2_ = f32[16,16,128]{2,1,0:T(8,128)S(1)} collective-permute-done((f32[16,16,128]{2,1,0:T(8,128)S(1)}, f32[16,16,128]{2,1,0:T(8,128)S(1)}, u32[]{:S(2)}, u32[]{:S(2)}) %collective-permute-start.5) | collective-permute-done | bytes 131104 | tf_op jit(solution)/shard_map/ppermute | solution.py:521
  46.6 5.5 %collective-permute-start.7 = (f32[48,16,128]{2,1,0:T(8,128)S(1)}, f32[48,16,128]{2,1,0:T(8,128)S(1)}, u32[]{:S(2)}, u32[]{:S(2)}) collective-permute-start(f32[48,16,128]{2,1,0:T(8,128)S(1)} %constant_dynamic-update-slice_fusion), channel_id=1, source_target_pairs={{0,31},{1,0},{2,1},{3,2},{4,3},{5,4},{6,5},{7,6},{8,7},{9,8},{10,9... | collective-permute-start | bytes 1179656 | tf_op jit(solution)/shard_map/ppermute | solution.py:521
  52.1 7.3 %collective-permute-done.7.refs_4_ = f32[48,16,128]{2,1,0:T(8,128)S(1)} collective-permute-done((f32[48,16,128]{2,1,0:T(8,128)S(1)}, f32[48,16,128]{2,1,0:T(8,128)S(1)}, u32[]{:S(2)}, u32[]{:S(2)}) %collective-permute-start.7) | collective-permute-done | bytes 393248 | tf_op jit(solution)/shard_map/ppermute | solution.py:521
  59.4 5.2 %collective-permute-done.6.refs_3_ = f32[48,16,128]{2,1,0:T(8,128)S(1)} collective-permute-done((f32[48,16,128]{2,1,0:T(8,128)S(1)}, f32[48,16,128]{2,1,0:T(8,128)S(1)}, u32[]{:S(2)}, u32[]{:S(2)}) %collective-permute-start.6) | collective-permute-done | bytes 393248 | tf_op jit(solution)/shard_map/ppermute | solution.py:520
  64.7 14.3 %shard_map.62 = (f32[48,48,128]{2,1,0:T(8,128)S(1)}, f32[48,48,128]{2,1,0:T(8,128)S(1)}, f32[48,48,128]{2,1,0:T(8,128)S(1)}, f32[48,48,128]{2,1,0:T(8,128)S(1)},...) custom-call(f32[16,16,128]{2,1,0:T(8,128)S(1)} %get-tuple-element.39, ...), custom_call_target="tpu_custom_call" | custom-call | tf_op jit(solution)/shard_map/pallas_call | solution.py:31
  79.0 28.5 %all_to_all.10 = f32[256,4,128]{2,1,0:T(4,128)S(1)} all-to-all(f32[256,4,128]{2,1,0:T(4,128)S(1)} %get-tuple-element.40), channel_id=1, replica_groups=mesh['grp'=8,'box'=32] {'grp','box'}, dimensions={0} | all-to-all | bytes 1048576 | tf_op jit(solution)/shard_map/all_to_all | solution.py:526
  107.5 26.3 %shard_map.63 = (f32[48,48,128]{2,1,0:T(8,128)S(1)}, f32[8,16,128]{2,1,0:T(8,128)S(1)}) custom-call(f32[1024,128]{1,0:T(8,128)S(1)} %bitcast.2, f32[48,48,128]{2,1,0:T(8,128)S(1)} %get-tuple-element.41.refs_1_.refs_2_, f32[48,48,128]{2,1,0:T(8,128)S(1)} %get-tuple-element.42.refs_2_.refs_3_, ...), custom_call_target="tpu_custom_call", output_to_operand_aliasing={{0}: (16, {})} | custom-call | tf_op jit(solution)/shard_map/pallas_call | solution.py:31
  133.8 0.6 collective-permute-start.8
  134.4 1.3 collective-permute-done.8.left
  135.8 2.6 %collective-permute-done.9.right = f32[8,16,128]{2,1,0:T(8,128)S(1)} collective-permute-done((f32[8,16,128]{2,1,0:T(8,128)S(1)}, f32[8,16,128]{2,1,0:T(8,128)S(1)}, u32[]{:S(2)}, u32[]{:S(2)}) %collective-permute-start.9) | collective-permute-done | bytes 65568 | tf_op jit(solution)/shard_map/ppermute | solution.py:521
  138.4 0.4 collective-permute-start.11
  138.8 1.0 collective-permute-start.10
  139.9 4.1 %collective-permute-done.11.below = f32[24,16,128]{2,1,0:T(8,128)S(1)} collective-permute-done((f32[24,16,128]{2,1,0:T(8,128)S(1)}, f32[24,16,128]{2,1,0:T(8,128)S(1)}, u32[]{:S(2)}, u32[]{:S(2)}) %collective-permute-start.11) | collective-permute-done | bytes 196640 | tf_op jit(solution)/shard_map/ppermute | solution.py:521
  144.0 3.8 %collective-permute-done.10.above = f32[24,16,128]{2,1,0:T(8,128)S(1)} collective-permute-done((f32[24,16,128]{2,1,0:T(8,128)S(1)}, f32[24,16,128]{2,1,0:T(8,128)S(1)}, u32[]{:S(2)}, u32[]{:S(2)}) %collective-permute-start.10) | collective-permute-done | bytes 196640 | tf_op jit(solution)/shard_map/ppermute | solution.py:520
  147.8 6.8 %shard_map.64 = (f32[48,48,128]{2,1,0:T(8,128)S(1)}, f32[48,48,128]{2,1,0:T(8,128)S(1)}, f32[24,24,128]{2,1,0:T(8,128)S(1)}, f32[24,24,128]{2,1,0:T(8,128)S(1)}, f32[256,2,128]{2,1,0:T(2,128)S(1)}) custom-call(f32[8,16,128]{2,1,0:T(8,128)S(1)} %get-tuple-element.59.own, f32[8,16,128]{2,1,0:T(8,128)S(1)} %collective-permute-done.8.left, ...), custom_call_target="tpu_custom_call" | custom-call | tf_op jit(solution)/shard_map/pallas_call | solution.py:31
  154.6 22.2 %all_to_all.11 = f32[256,2,128]{2,1,0:T(2,128)S(1)} all-to-all(f32[256,2,128]{2,1,0:T(2,128)S(1)} %get-tuple-element.60), channel_id=1, replica_groups=mesh['grp'=8,'box'=32] {'grp','box'}, dimensions={0} | all-to-all | bytes 524288 | tf_op jit(solution)/shard_map/all_to_all | solution.py:526
  176.8 24.2 %shard_map.65 = (f32[32,32,128]{2,1,0:T(8,128)}, f32[32,32,128]{2,1,0:T(8,128)}) custom-call(f32[512,128]{1,0:T(8,128)S(1)} %bitcast.4, f32[1024,128]{1,0:T(8,128)S(1)} %bitcast.3, f32[48,48,128]{2,1,0:T(8,128)S(1)} %get-tuple-element.41.refs_1_.refs_2_, f32[48,48,128]{2,1,0:T(8,128)S(1)} %get-tuple-element.42.refs_2_.refs_3_, ...), custom_call_target="tpu_custom_call" | custom-call | tf_op jit(solution)/shard_map/pallas_call | solution.py:31
  (15 shorter events, 0.2 us)
Async XLA Ops:
  0.6 1.0 copy-start
  1.7 1.0 copy-start.1
  2.7 1.0 copy-start.2
  3.8 0.7 copy-start.3
  5.5 6.1 %collective-permute-start = (f32[17,32,128]{2,1,0:T(8,128)S(1)}, f32[17,32,128]{2,1,0:T(8,128)S(1)}, u32[]{:S(2)}, u32[]{:S(2)}) collective-permute-start(f32[17,32,128]{2,1,0:T(8,128)S(1)} %get-tuple-element.35), channel_id=1, source_target_pairs={{0,32},{32,64},{64,96},{96,128},{128,160},{160,192},{192,224},{224... | collective-permute-start | bytes 835592 | tf_op jit(solution)/shard_map/ppermute | solution.py:520
  8.1 6.3 %collective-permute-start.1 = (f32[17,32,128]{2,1,0:T(8,128)S(1)}, f32[17,32,128]{2,1,0:T(8,128)S(1)}, u32[]{:S(2)}, u32[]{:S(2)}) collective-permute-start(f32[17,32,128]{2,1,0:T(8,128)S(1)} %get-tuple-element.36), channel_id=1, source_target_pairs={{0,224},{32,0},{64,32},{96,64},{128,96},{160,128},{192,160},{224,1... | collective-permute-start | bytes 835592 | tf_op jit(solution)/shard_map/ppermute | solution.py:521
  14.5 18.0 %collective-permute-start.2 = (f32[105,8,128]{2,1,0:T(8,128)S(1)}, f32[105,8,128]{2,1,0:T(8,128)S(1)}, u32[]{:S(2)}, u32[]{:S(2)}) collective-permute-start(f32[105,8,128]{2,1,0:T(8,128)S(1)} %get-tuple-element.37), channel_id=1, source_target_pairs={{0,1},{1,2},{2,3},{3,4},{4,5},{5,6},{6,7},{7,8},{8,9},{9,10},{10,1... | collective-permute-start | bytes 1290248 | tf_op jit(solution)/shard_map/ppermute | solution.py:520
  15.9 16.6 %collective-permute-start.3 = (f32[105,8,128]{2,1,0:T(8,128)S(1)}, f32[105,8,128]{2,1,0:T(8,128)S(1)}, u32[]{:S(2)}, u32[]{:S(2)}) collective-permute-start(f32[105,8,128]{2,1,0:T(8,128)S(1)} %get-tuple-element.38), channel_id=1, source_target_pairs={{0,31},{1,0},{2,1},{3,2},{4,3},{5,4},{6,5},{7,6},{8,7},{9,8},{10,9... | collective-permute-start | bytes 1290248 | tf_op jit(solution)/shard_map/ppermute | solution.py:521
  41.9 2.0 collective-permute-start.4
  41.9 4.7 %collective-permute-start.5 = (f32[16,16,128]{2,1,0:T(8,128)S(1)}, f32[16,16,128]{2,1,0:T(8,128)S(1)}, u32[]{:S(2)}, u32[]{:S(2)}) collective-permute-start(f32[16,16,128]{2,1,0:T(8,128)S(1)} %get-tuple-element.39.refs_0_), channel_id=1, source_target_pairs={{0,224},{32,0},{64,32},{96,64},{128,96},{160,128},{192,160},{224,1... | collective-permute-start | bytes 393224 | tf_op jit(solution)/shard_map/ppermute | solution.py:521
  46.6 12.8 %collective-permute-start.7 = (f32[48,16,128]{2,1,0:T(8,128)S(1)}, f32[48,16,128]{2,1,0:T(8,128)S(1)}, u32[]{:S(2)}, u32[]{:S(2)}) collective-permute-start(f32[48,16,128]{2,1,0:T(8,128)S(1)} %constant_dynamic-update-slice_fusion), channel_id=1, source_target_pairs={{0,31},{1,0},{2,1},{3,2},{4,3},{5,4},{6,5},{7,6},{8,7},{9,8},{10,9... | collective-permute-start | bytes 1179656 | tf_op jit(solution)/shard_map/ppermute | solution.py:521
  52.1 12.6 %collective-permute-start.6 = (f32[48,16,128]{2,1,0:T(8,128)S(1)}, f32[48,16,128]{2,1,0:T(8,128)S(1)}, u32[]{:S(2)}, u32[]{:S(2)}) collective-permute-start(f32[48,16,128]{2,1,0:T(8,128)S(1)} %constant_dynamic-update-slice_fusion), channel_id=1, source_target_pairs={{0,1},{1,2},{2,3},{3,4},{4,5},{5,6},{6,7},{7,8},{8,9},{9,10},{10,1... | collective-permute-start | bytes 1179656 | tf_op jit(solution)/shard_map/ppermute | solution.py:520
  133.8 1.9 collective-permute-start.8
  134.4 4.0 %collective-permute-start.9 = (f32[8,16,128]{2,1,0:T(8,128)S(1)}, f32[8,16,128]{2,1,0:T(8,128)S(1)}, u32[]{:S(2)}, u32[]{:S(2)}) collective-permute-start(f32[8,16,128]{2,1,0:T(8,128)S(1)} %get-tuple-element.59.own), channel_id=1, source_target_pairs={{0,224},{32,0},{64,32},{96,64},{128,96},{160,128},{192,160},{224,1... | collective-permute-start | bytes 196616 | tf_op jit(solution)/shard_map/ppermute | solution.py:521
  138.4 5.6 %collective-permute-start.11 = (f32[24,16,128]{2,1,0:T(8,128)S(1)}, f32[24,16,128]{2,1,0:T(8,128)S(1)}, u32[]{:S(2)}, u32[]{:S(2)}) collective-permute-start(f32[24,16,128]{2,1,0:T(8,128)S(1)} %constant_dynamic-update-slice_fusion.3), channel_id=1, source_target_pairs={{0,31},{1,0},{2,1},{3,2},{4,3},{5,4},{6,5},{7,6},{8,7},{9,8},{10,9... | collective-permute-start | bytes 589832 | tf_op jit(solution)/shard_map/ppermute | solution.py:521
  138.8 8.9 %collective-permute-start.10 = (f32[24,16,128]{2,1,0:T(8,128)S(1)}, f32[24,16,128]{2,1,0:T(8,128)S(1)}, u32[]{:S(2)}, u32[]{:S(2)}) collective-permute-start(f32[24,16,128]{2,1,0:T(8,128)S(1)} %constant_dynamic-update-slice_fusion.3), channel_id=1, source_target_pairs={{0,1},{1,2},{2,3},{3,4},{4,5},{5,6},{6,7},{7,8},{8,9},{9,10},{10,1... | collective-permute-start | bytes 589832 | tf_op jit(solution)/shard_map/ppermute | solution.py:520

commit v2 on v1

--- a/solution.py
+++ b/solution.py
@@ -74,79 +74,122 @@
     return t + (wll * up(vc, 1) + down(wll * vc, 1))
 
 
+def blocks(lo, hi, size, fn, state=0):
+    count = (hi - lo) // size
+    if count > 1:
+        state = lax.fori_loop(0, count, lambda i, st: fn(lo + i * size, size, st), state)
+    elif count == 1:
+        state = fn(lo, size, state)
+    rest = (hi - lo) - count * size
+    if rest:
+        state = fn(hi - rest, rest, state)
+    return state
+
+
+def block_of(ref):
+    return max(1, 384 // ref.shape[1])
+
+
 def sweep(v, f, op, lo, hi):
     wx, ws, wl, di = op
 
-    def step(x, state):
+    def step(x, n, state):
         carry, vc = state
-        vn = v[x + 1]
-        wxx = wx[x]
-        t = near_sum(vc, vn, carry, wxx, ws[x], wl[x])
-        v[x] = F32(0.2) * vc + di[x] * (f[x] + t)
-        return (wxx * vc, vn)
-
-    lax.fori_loop(lo, hi, step, (wx[lo - 1] * v[lo - 1], v[lo]), unroll=2)
+        vs = [vc] + [v[x + i + 1] for i in range(n)]
+        new = []
+        for i in range(n):
+            wxx = wx[x + i]
+            t = near_sum(vs[i], vs[i + 1], carry, wxx, ws[x + i], wl[x + i])
+            new.append(F32(0.2) * vs[i] + di[x + i] * (f[x + i] + t))
+            carry = wxx * vs[i]
+        for i in range(n):
+            v[x + i] = new[i]
+        return carry, vs[n]
+
+    blocks(lo, hi, block_of(v), step, (wx[lo - 1] * v[lo - 1], v[lo]))
 
 
 def first_sweep(v, f, op, lo, hi):
     di = op[3]
 
-    def step(x, _):
-        v[x] = di[x] * f[x]
+    def step(x, n, _):
+        new = [di[x + i] * f[x + i] for i in range(n)]
+        for i in range(n):
+            v[x + i] = new[i]
         return 0
 
-    lax.fori_loop(lo, hi, step, 0, unroll=2)
-
-
-def resid(v, f, op, x):
+    blocks(lo, hi, block_of(v), step)
+
+
+def resid_slabs(v, f, op, x, n):
     wx, ws, wl, di = op
-    vc = v[x]
-    t = near_sum(vc, v[x + 1], wx[x - 1] * v[x - 1], wx[x], ws[x], wl[x])
-    dinv = di[x]
-    inside = dinv > 0
-    diag = jnp.where(inside, F32(0.8) / jnp.where(inside, dinv, F32(1.0)), F32(0.0))
-    return f[x] - (diag * vc - t)
+    vs = [v[x + i - 1] for i in range(n + 2)]
+    wxs = [wx[x + i - 1] for i in range(n + 1)]
+    out = []
+    for i in range(n):
+        vc = vs[i + 1]
+        t = near_sum(vc, vs[i + 2], wxs[i] * vs[i], wxs[i + 1], ws[x + i], wl[x + i])
+        dinv = di[x + i]
+        inside = dinv > 0
+        diag = jnp.where(inside, F32(0.8) / jnp.where(inside, dinv, F32(1.0)), F32(0.0))
+        out.append(f[x + i] - (diag * vc - t))
+    return out
 
 
 def resid_pairs(v, f, op, lo, n, out):
-    def step(i, _):
-        x = lo + 2 * i
-        out[i] = resid(v, f, op, x) + resid(v, f, op, x + 1)
+    def step(j, m, _):
+        rs = resid_slabs(v, f, op, lo + 2 * j, 2 * m)
+        for i in range(m):
+            out[j + i] = rs[2 * i] + rs[2 * i + 1]
         return 0
 
-    lax.fori_loop(0, n, step, 0)
+    blocks(0, n, max(1, block_of(v) // 2), step)
+
+
+def sum_pairs(src, lo, n, out):
+    def step(j, m, _):
+        new = [src[lo + 2 * (j + i)] + src[lo + 2 * (j + i) + 1] for i in range(m)]
+        for i in range(m):
+            out[j + i] = new[i]
+        return 0
+
+    blocks(0, n, max(1, block_of(out) // 2), step)
 
 
 def weights(c, cbase, op, lo, hi, lane_last, sub_last, edge=None):
     wx, ws, wl, di = op
-    half = F32(0.5)
-
-    def step(x, _):
-        cc = c[x + cbase]
-        ch = cc * half
-        cp = ch + c[x + cbase + 1] * half
-        cm = ch + c[x + cbase - 1] * half
-        rows, lanes = iota(cc.shape, 0), iota(cc.shape, 1)
-        ny, nl = cc.shape
-        s_next, s_prev = up(ch, 0), down(ch, 0)
-        if sub_last:
-            s_next = jnp.where(rows == ny - 1, F32(0.0), s_next)
-            s_prev = jnp.where(rows == 0, F32(0.0), s_prev)
-        if edge is not None:
-            s_next = jnp.where(rows == ny - 1, edge[1, pl.ds(x + cbase, 1), :] * half, s_next)
-            s_prev = jnp.where(rows == 0, edge[0, pl.ds(x + cbase, 1), :] * half, s_prev)
-        l_next = jnp.where(lanes >= lane_last, F32(0.0), up(ch, 1))
-        l_prev = jnp.where(lanes == 0, F32(0.0), down(ch, 1))
-        s_up, l_up = ch + s_next, ch + l_next
-        diag = (cp + cm) + (s_up + (ch + s_prev)) + (l_up + (ch + l_prev))
-        inside = cc > 0
-        wx[x] = cp
-        ws[x] = jnp.where(rows == ny - 1, F32(0.0), s_up) if sub_last else s_up
-        wl[x] = jnp.where(lanes >= lane_last, F32(0.0), l_up)
-        di[x] = jnp.where(inside, F32(0.8) / jnp.where(inside, diag, F32(1.0)), F32(0.0))
+    ny, nl = c.shape[1:]
+    half, zero = F32(0.5), F32(0.0)
+
+    def step(x, n, _):
+        x = x + cbase
+        rows, lanes = iota((ny, nl), 0), iota((ny, nl), 1)
+        hs = [c[x + i - 1] * half for i in range(n + 2)]
+        new = []
+        for i in range(n):
+            ch = hs[i + 1]
+            cp, cm = ch + hs[i + 2], ch + hs[i]
+            s_next, s_prev = up(ch, 0), down(ch, 0)
+            if sub_last:
+                s_next = jnp.where(rows == ny - 1, zero, s_next)
+                s_prev = jnp.where(rows == 0, zero, s_prev)
+            if edge is not None:
+                s_next = jnp.where(rows == ny - 1, edge[1, pl.ds(x + i, 1), :] * half, s_next)
+                s_prev = jnp.where(rows == 0, edge[0, pl.ds(x + i, 1), :] * half, s_prev)
+            l_next = jnp.where(lanes >= lane_last, zero, up(ch, 1))
+            l_prev = jnp.where(lanes == 0, zero, down(ch, 1))
+            s_up, l_up = ch + s_next, ch + l_next
+            diag = (cp + cm) + (s_up + (ch + s_prev)) + (l_up + (ch + l_prev))
+            inside = ch > 0
+            dinv = jnp.where(inside, F32(0.8) / jnp.where(inside, diag, F32(1.0)), zero)
+            s_up = jnp.where(rows == ny - 1, zero, s_up) if sub_last else s_up
+            new.append((cp, s_up, jnp.where(lanes >= lane_last, zero, l_up), dinv))
+        for i in range(n):
+            for ref, value in zip(op, new[i]):
+                ref[x - cbase + i] = value
         return 0
 
-    lax.fori_loop(lo, hi, step, 0)
+    blocks(lo, hi, max(1, block_of(c) // 2), step)
 
 
 def pair_rows(s, start, n):
@@ -157,24 +200,30 @@
     return a.reshape(a.shape[0] * a.shape[1], a.shape[2])
 
 
-def add_double(v, es, lo, hi):
-    def step(x, _):
-        v[x] = v[x] + es[x >> 1]
+def add_double(v, es, lo, hi, base=0):
+    def step(x, n, _):
+        new = [v[x + i] + es[((x - base) >> 1) + (i >> 1)] for i in range(n)]
+        for i in range(n):
+            v[x + i] = new[i]
         return 0
 
-    lax.fori_loop(lo, hi, step, 0, unroll=2)
+    blocks(lo, hi, max(2, block_of(v) & ~1), step)
 
 
 def coef_kernel(f, tags, table, rough, coef, to_next, to_prev):
-    def step(x, _):
-        tag = tags[x]
-        picked = jnp.zeros(tag.shape, F32)
-        for region in range(8):
-            picked = jnp.where(tag == region, table[region], picked)
-        coef[x] = picked * rough[x]
+    def step(x, n, _):
+        new = []
+        for i in range(n):
+            tag = tags[x + i]
+            picked = jnp.zeros(tag.shape, F32)
+            for region in range(8):
+                picked = jnp.where(tag == region, table[region], picked)
+            new.append(picked * rough[x + i])
+        for i in range(n):
+            coef[x + i] = new[i]
         return 0
 
-    lax.fori_loop(0, 32, step, 0)
+    blocks(0, 32, 8, step)
     to_next[0:8] = f[24:32]
     to_next[8:17] = coef[23:32]
     to_prev[0:8] = f[0:8]
@@ -245,11 +294,7 @@
     sweep(v, fx, op, 1, 47)
     f1 = fine_restrict(v, fx, op, s)
 
-    def pair(i, _):
-        s[i, 8:40] = coef[2 * i] + coef[2 * i + 1]
-        return 0
-
-    lax.fori_loop(0, 16, pair, 0)
+    sum_pairs(coef, 0, 16, s.at[:, 8:40])
     c1 = dot(flat(pair_rows(s, 8, 16) * F32(0.25)), halver(128)).reshape(16, 16, 128)
     packed[...] = f1 + pltpu.roll(c1, 64, 2)
 
@@ -306,11 +351,7 @@
     op1, op2 = (wx1, ws1, wl1, di1), (wx2, ws2, wl2, di2)
     weights(c1, 0, op1, 1, 47, 63, False)
 
-    def pair(i, _):
-        s[i] = c1[2 * i] + c1[2 * i + 1]
-        return 0
-
-    lax.fori_loop(0, 24, pair, 0)
+    sum_pairs(c1, 0, 24, s)
     half = halver(128)
     c2[...] = dot(flat(pair_rows(s, 0, 24) * F32(0.25)), half).reshape(24, 24, 128)
     weights(c2, 0, op2, 1, 23, 31, False)
@@ -410,11 +451,7 @@
     sweep(v3, f3, op3, lo, hi)
     half = halver(nl)
 
-    def pair(i, _):
-        s3[i] = c3[4 + 2 * i] + c3[5 + 2 * i]
-        return 0
-
-    lax.fori_loop(0, n3 // 2, pair, 0)
+    sum_pairs(c3, 4, n3 // 2, s3)
     c4 = dot(flat(pair_rows(s3, 0, 8) * F32(0.25)), half).reshape(n3 // 2, 8, nl)
     resid_pairs(v3, f3, op3, 4, n3 // 2, s3)
     f4 = dot(flat(pair_rows(s3, 0, 8)), half).reshape(n3 // 2, 8, nl)
@@ -423,11 +460,7 @@
     s3[:, pl.ds(0, 8, stride=2), :] = e
     s3[:, pl.ds(1, 8, stride=2), :] = e
 
-    def add(x, _):
-        v3[4 + x] = v3[4 + x] + s3[x >> 1]
-        return 0
-
-    lax.fori_loop(0, n3, add, 0)
+    add_double(v3, s3, 4, 4 + n3, 4)
     sweep(v3, f3, op3, lo, hi)
     sweep(v3, f3, op3, lo, hi)
 
@@ -485,7 +518,7 @@
     v2[...] = v2i[...]
     op0, op1, op2 = (wx0, ws0, wl0, di0), (wx1, ws1, wl1, di1), (wx2, ws2, wl2, di2)
     climb(ng, nb, None, got, v0, f0, op0, v1, f1, op1, v2, f2, op2, scr)
-    add_double(v0, scr[-1], 1, 47)
+    add_double(v0, scr[-1], 0, 48)
     for lo in (2, 3, 4, 5):
         sweep(v0, f0, op0, lo, 48 - lo)
     f1n = fine_restrict(v0, f0, op0, s)
@@ -504,16 +537,18 @@
     v2[...] = v2i[...]
     op0, op1, op2 = (wx0, ws0, wl0, di0), (wx1, ws1, wl1, di1), (wx2, ws2, wl2, di2)
     climb(ng, nb, got, got_c, v0, f0, op0, v1, f1, op1, v2, f2, op2, scr)
-    add_double(v0, scr[-1], 5, 43)
+    add_double(v0, scr[-1], 4, 44)
     sweep(v0, f0, op0, 6, 42)
     sweep(v0, f0, op0, 7, 41)
 
-    def step(x, _):
-        sol[x] = v0[x + 8, 8:40]
-        res[x] = resid(v0, f0, op0, x + 8)[8:40]
+    def step(x, n, _):
+        rs = resid_slabs(v0, f0, op0, x + 8, n)
+        for i in range(n):
+            res[x + i] = rs[i][8:40]
         return 0
 
-    lax.fori_loop(0, 32, step, 0)
+    sol[...] = v0[8:40, 8:40]
+    blocks(0, 32, 8, step)
 
 
 def ring(x, axis, n):

time: 201 us -> 156 us (0.78)
  Pallas kernels: 82.2 us -> 37.2 us
    pallas_call x7, Pallas kernels: 82.2 us -> 37.2 us  [call(): pl.pallas_call(kernel, out_shape=[shape_of(i, s) for i, s in enumerate(ou...]
where the time goes in v2:
time: 156 us
  blocking collectives  50.7 us (32%)
  waiting for transfers between devices  44.1 us (28%)
  Pallas kernels  37.2 us (24%)
  starting transfers between devices  19.5 us (12%)
  local copies, waits for them, and re-layouts  3.82 us (2%)
    all_to_all x2, blocking collectives, gather_all(): got = lax.all_to_all(payload, ('grp', 'box'), 0, 0, tiled=True)  50.7 us
    pallas_call x7, Pallas kernels, call(): pl.pallas_call(kernel, out_shape=[shape_of(i, s) for i, s in enumerate(ou...  37.2 us
    ppermute x6, waiting for transfers between devices, ring(): before = lax.ppermute(x[0], axis, [(i, (i + 1) % n) for i in range(n)])  24.5 us
    ppermute x6, waiting for transfers between devices, ring(): after = lax.ppermute(x[1], axis, [(i, (i - 1) % n) for i in range(n)])  19.6 us
    ppermute x6, starting transfers between devices, ring(): after = lax.ppermute(x[1], axis, [(i, (i - 1) % n) for i in range(n)])  13.8 us
    ppermute x6, starting transfers between devices, ring(): before = lax.ppermute(x[0], axis, [(i, (i + 1) % n) for i in range(n)])  5.67 us
    unnamed x12, local copies, waits for them, and re-layouts  3.8 us
  transfers between devices with their start and end apart: 12, of which 11 were waited for; matrix products, arithmetic and copies ran while one was open for 0% of the time, Pallas kernels for 0%

profile of v2, /device:TPU:1, one launch (start us, length us, event | category | flops | bytes accessed | tf_op | source)
XLA Modules:
  0.0 156.0 jit_solution(4010358473985171181)
XLA Ops:
  0.6 1.0 copy-done
  1.7 1.0 copy-done.1
  2.7 1.0 copy-done.2
  3.8 0.7 copy-done.3
  4.4 0.9 shard_map.59
  5.3 2.6 %collective-permute-start = (f32[17,32,128]{2,1,0:T(8,128)S(1)}, f32[17,32,128]{2,1,0:T(8,128)S(1)}, u32[]{:S(2)}, u32[]{:S(2)}) collective-permute-start(f32[17,32,128]{2,1,0:T(8,128)S(1)} %get-tuple-element.35), channel_id=1, source_target_pairs={{0,32},{32,64},{64,96},{96,128},{128,160},{160,192},{192,224},{224... | collective-permute-start | bytes 835592 | tf_op jit(solution)/shard_map/ppermute | solution.py:555
  7.9 0.7 collective-permute-start.1
  8.6 2.8 %collective-permute-done.left.refs_2_ = f32[17,32,128]{2,1,0:T(8,128)S(1)} collective-permute-done((f32[17,32,128]{2,1,0:T(8,128)S(1)}, f32[17,32,128]{2,1,0:T(8,128)S(1)}, u32[]{:S(2)}, u32[]{:S(2)}) %collective-permute-start) | collective-permute-done | bytes 278560 | tf_op jit(solution)/shard_map/ppermute | solution.py:555
  11.4 2.8 %collective-permute-done.1.right.refs_3_ = f32[17,32,128]{2,1,0:T(8,128)S(1)} collective-permute-done((f32[17,32,128]{2,1,0:T(8,128)S(1)}, f32[17,32,128]{2,1,0:T(8,128)S(1)}, u32[]{:S(2)}, u32[]{:S(2)}) %collective-permute-start.1) | collective-permute-done | bytes 278560 | tf_op jit(solution)/shard_map/ppermute | solution.py:556
  14.3 1.4 collective-permute-start.2
  15.7 6.5 %collective-permute-start.3 = (f32[105,8,128]{2,1,0:T(8,128)S(1)}, f32[105,8,128]{2,1,0:T(8,128)S(1)}, u32[]{:S(2)}, u32[]{:S(2)}) collective-permute-start(f32[105,8,128]{2,1,0:T(8,128)S(1)} %get-tuple-element.38), channel_id=1, source_target_pairs={{0,31},{1,0},{2,1},{3,2},{4,3},{5,4},{6,5},{7,6},{8,7},{9,8},{10,9... | collective-permute-start | bytes 1290248 | tf_op jit(solution)/shard_map/ppermute | solution.py:556
  22.2 10.1 %collective-permute-done.2.refs_4_ = f32[105,8,128]{2,1,0:T(8,128)S(1)} collective-permute-done((f32[105,8,128]{2,1,0:T(8,128)S(1)}, f32[105,8,128]{2,1,0:T(8,128)S(1)}, u32[]{:S(2)}, u32[]{:S(2)}) %collective-permute-start.2) | collective-permute-done | bytes 430112 | tf_op jit(solution)/shard_map/ppermute | solution.py:555
  32.3 4.4 %shard_map.61 = (f32[48,48,128]{2,1,0:T(8,128)S(1)}, f32[48,48,128]{2,1,0:T(8,128)S(1)}, f32[48,48,128]{2,1,0:T(8,128)S(1)}, f32[48,48,128]{2,1,0:T(8,128)S(1)},...) custom-call(f32[32,32,128]{2,1,0:T(8,128)S(1)} %copy-done, ...), custom_call_target="tpu_custom_call" | custom-call | tf_op jit(solution)/shard_map/pallas_call | solution.py:31
  36.7 0.7 collective-permute-start.5
  37.4 1.2 collective-permute-done.4.refs_1_
  38.7 2.7 %collective-permute-done.5.refs_2_ = f32[16,16,128]{2,1,0:T(8,128)S(1)} collective-permute-done((f32[16,16,128]{2,1,0:T(8,128)S(1)}, f32[16,16,128]{2,1,0:T(8,128)S(1)}, u32[]{:S(2)}, u32[]{:S(2)}) %collective-permute-start.5) | collective-permute-done | bytes 131104 | tf_op jit(solution)/shard_map/ppermute | solution.py:556
  41.4 5.5 %collective-permute-start.7 = (f32[48,16,128]{2,1,0:T(8,128)S(1)}, f32[48,16,128]{2,1,0:T(8,128)S(1)}, u32[]{:S(2)}, u32[]{:S(2)}) collective-permute-start(f32[48,16,128]{2,1,0:T(8,128)S(1)} %constant_dynamic-update-slice_fusion), channel_id=1, source_target_pairs={{0,31},{1,0},{2,1},{3,2},{4,3},{5,4},{6,5},{7,6},{8,7},{9,8},{10,9... | collective-permute-start | bytes 1179656 | tf_op jit(solution)/shard_map/ppermute | solution.py:556
  46.9 7.3 %collective-permute-done.7.refs_4_ = f32[48,16,128]{2,1,0:T(8,128)S(1)} collective-permute-done((f32[48,16,128]{2,1,0:T(8,128)S(1)}, f32[48,16,128]{2,1,0:T(8,128)S(1)}, u32[]{:S(2)}, u32[]{:S(2)}) %collective-permute-start.7) | collective-permute-done | bytes 393248 | tf_op jit(solution)/shard_map/ppermute | solution.py:556
  54.2 5.2 %collective-permute-done.6.refs_3_ = f32[48,16,128]{2,1,0:T(8,128)S(1)} collective-permute-done((f32[48,16,128]{2,1,0:T(8,128)S(1)}, f32[48,16,128]{2,1,0:T(8,128)S(1)}, u32[]{:S(2)}, u32[]{:S(2)}) %collective-permute-start.6) | collective-permute-done | bytes 393248 | tf_op jit(solution)/shard_map/ppermute | solution.py:555
  59.5 6.7 %shard_map.62 = (f32[48,48,128]{2,1,0:T(8,128)S(1)}, f32[48,48,128]{2,1,0:T(8,128)S(1)}, f32[48,48,128]{2,1,0:T(8,128)S(1)}, f32[48,48,128]{2,1,0:T(8,128)S(1)},...) custom-call(f32[16,16,128]{2,1,0:T(8,128)S(1)} %get-tuple-element.39, ...), custom_call_target="tpu_custom_call" | custom-call | tf_op jit(solution)/shard_map/pallas_call | solution.py:31
  66.2 28.5 %all_to_all.10 = f32[256,4,128]{2,1,0:T(4,128)S(1)} all-to-all(f32[256,4,128]{2,1,0:T(4,128)S(1)} %get-tuple-element.40), channel_id=1, replica_groups=mesh['grp'=8,'box'=32] {'grp','box'}, dimensions={0} | all-to-all | bytes 1048576 | tf_op jit(solution)/shard_map/all_to_all | solution.py:561
  94.7 11.2 %shard_map.63 = (f32[48,48,128]{2,1,0:T(8,128)S(1)}, f32[8,16,128]{2,1,0:T(8,128)S(1)}) custom-call(f32[1024,128]{1,0:T(8,128)S(1)} %bitcast.2, f32[48,48,128]{2,1,0:T(8,128)S(1)} %get-tuple-element.41.refs_1_.refs_2_, f32[48,48,128]{2,1,0:T(8,128)S(1)} %get-tuple-element.42.refs_2_.refs_3_, ...), custom_call_target="tpu_custom_call", output_to_operand_aliasing={{0}: (16, {})} | custom-call | tf_op jit(solution)/shard_map/pallas_call | solution.py:31
  105.9 0.6 collective-permute-start.8
  106.5 1.3 collective-permute-done.8.left
  107.8 2.6 %collective-permute-done.9.right = f32[8,16,128]{2,1,0:T(8,128)S(1)} collective-permute-done((f32[8,16,128]{2,1,0:T(8,128)S(1)}, f32[8,16,128]{2,1,0:T(8,128)S(1)}, u32[]{:S(2)}, u32[]{:S(2)}) %collective-permute-start.9) | collective-permute-done | bytes 65568 | tf_op jit(solution)/shard_map/ppermute | solution.py:556
  110.5 0.4 collective-permute-start.11
  110.9 1.0 collective-permute-start.10
  111.9 4.1 %collective-permute-done.11.below = f32[24,16,128]{2,1,0:T(8,128)S(1)} collective-permute-done((f32[24,16,128]{2,1,0:T(8,128)S(1)}, f32[24,16,128]{2,1,0:T(8,128)S(1)}, u32[]{:S(2)}, u32[]{:S(2)}) %collective-permute-start.11) | collective-permute-done | bytes 196640 | tf_op jit(solution)/shard_map/ppermute | solution.py:556
  116.1 3.8 %collective-permute-done.10.above = f32[24,16,128]{2,1,0:T(8,128)S(1)} collective-permute-done((f32[24,16,128]{2,1,0:T(8,128)S(1)}, f32[24,16,128]{2,1,0:T(8,128)S(1)}, u32[]{:S(2)}, u32[]{:S(2)}) %collective-permute-start.10) | collective-permute-done | bytes 196640 | tf_op jit(solution)/shard_map/ppermute | solution.py:555
  119.9 3.6 %shard_map.64 = (f32[48,48,128]{2,1,0:T(8,128)S(1)}, f32[48,48,128]{2,1,0:T(8,128)S(1)}, f32[24,24,128]{2,1,0:T(8,128)S(1)}, f32[24,24,128]{2,1,0:T(8,128)S(1)}, f32[256,2,128]{2,1,0:T(2,128)S(1)}) custom-call(f32[8,16,128]{2,1,0:T(8,128)S(1)} %get-tuple-element.59.own, f32[8,16,128]{2,1,0:T(8,128)S(1)} %collective-permute-done.8.left, ...), custom_call_target="tpu_custom_call" | custom-call | tf_op jit(solution)/shard_map/pallas_call | solution.py:31
  123.4 22.2 %all_to_all.11 = f32[256,2,128]{2,1,0:T(2,128)S(1)} all-to-all(f32[256,2,128]{2,1,0:T(2,128)S(1)} %get-tuple-element.60), channel_id=1, replica_groups=mesh['grp'=8,'box'=32] {'grp','box'}, dimensions={0} | all-to-all | bytes 524288 | tf_op jit(solution)/shard_map/all_to_all | solution.py:561
  145.7 10.4 %shard_map.65 = (f32[32,32,128]{2,1,0:T(8,128)}, f32[32,32,128]{2,1,0:T(8,128)}) custom-call(f32[512,128]{1,0:T(8,128)S(1)} %bitcast.4, f32[1024,128]{1,0:T(8,128)S(1)} %bitcast.3, f32[48,48,128]{2,1,0:T(8,128)S(1)} %get-tuple-element.41.refs_1_.refs_2_, f32[48,48,128]{2,1,0:T(8,128)S(1)} %get-tuple-element.42.refs_2_.refs_3_, ...), custom_call_target="tpu_custom_call" | custom-call | tf_op jit(solution)/shard_map/pallas_call | solution.py:31
  (15 shorter events, 0.2 us)
Async XLA Ops:
  0.6 1.0 copy-start
  1.7 1.0 copy-start.1
  2.7 1.0 copy-start.2
  3.8 0.7 copy-start.3
  5.3 6.1 %collective-permute-start = (f32[17,32,128]{2,1,0:T(8,128)S(1)}, f32[17,32,128]{2,1,0:T(8,128)S(1)}, u32[]{:S(2)}, u32[]{:S(2)}) collective-permute-start(f32[17,32,128]{2,1,0:T(8,128)S(1)} %get-tuple-element.35), channel_id=1, source_target_pairs={{0,32},{32,64},{64,96},{96,128},{128,160},{160,192},{192,224},{224... | collective-permute-start | bytes 835592 | tf_op jit(solution)/shard_map/ppermute | solution.py:555
  7.9 6.3 %collective-permute-start.1 = (f32[17,32,128]{2,1,0:T(8,128)S(1)}, f32[17,32,128]{2,1,0:T(8,128)S(1)}, u32[]{:S(2)}, u32[]{:S(2)}) collective-permute-start(f32[17,32,128]{2,1,0:T(8,128)S(1)} %get-tuple-element.36), channel_id=1, source_target_pairs={{0,224},{32,0},{64,32},{96,64},{128,96},{160,128},{192,160},{224,1... | collective-permute-start | bytes 835592 | tf_op jit(solution)/shard_map/ppermute | solution.py:556
  14.3 18.0 %collective-permute-start.2 = (f32[105,8,128]{2,1,0:T(8,128)S(1)}, f32[105,8,128]{2,1,0:T(8,128)S(1)}, u32[]{:S(2)}, u32[]{:S(2)}) collective-permute-start(f32[105,8,128]{2,1,0:T(8,128)S(1)} %get-tuple-element.37), channel_id=1, source_target_pairs={{0,1},{1,2},{2,3},{3,4},{4,5},{5,6},{6,7},{7,8},{8,9},{9,10},{10,1... | collective-permute-start | bytes 1290248 | tf_op jit(solution)/shard_map/ppermute | solution.py:555
  15.7 16.6 %collective-permute-start.3 = (f32[105,8,128]{2,1,0:T(8,128)S(1)}, f32[105,8,128]{2,1,0:T(8,128)S(1)}, u32[]{:S(2)}, u32[]{:S(2)}) collective-permute-start(f32[105,8,128]{2,1,0:T(8,128)S(1)} %get-tuple-element.38), channel_id=1, source_target_pairs={{0,31},{1,0},{2,1},{3,2},{4,3},{5,4},{6,5},{7,6},{8,7},{9,8},{10,9... | collective-permute-start | bytes 1290248 | tf_op jit(solution)/shard_map/ppermute | solution.py:556
  36.7 2.0 %collective-permute-start.4 = (f32[16,16,128]{2,1,0:T(8,128)S(1)}, f32[16,16,128]{2,1,0:T(8,128)S(1)}, u32[]{:S(2)}, u32[]{:S(2)}) collective-permute-start(f32[16,16,128]{2,1,0:T(8,128)S(1)} %get-tuple-element.39.refs_0_), channel_id=1, source_target_pairs={{0,32},{32,64},{64,96},{96,128},{128,160},{160,192},{192,224},{224... | collective-permute-start | bytes 393224 | tf_op jit(solution)/shard_map/ppermute | solution.py:555
  36.7 4.7 %collective-permute-start.5 = (f32[16,16,128]{2,1,0:T(8,128)S(1)}, f32[16,16,128]{2,1,0:T(8,128)S(1)}, u32[]{:S(2)}, u32[]{:S(2)}) collective-permute-start(f32[16,16,128]{2,1,0:T(8,128)S(1)} %get-tuple-element.39.refs_0_), channel_id=1, source_target_pairs={{0,224},{32,0},{64,32},{96,64},{128,96},{160,128},{192,160},{224,1... | collective-permute-start | bytes 393224 | tf_op jit(solution)/shard_map/ppermute | solution.py:556
  41.4 12.8 %collective-permute-start.7 = (f32[48,16,128]{2,1,0:T(8,128)S(1)}, f32[48,16,128]{2,1,0:T(8,128)S(1)}, u32[]{:S(2)}, u32[]{:S(2)}) collective-permute-start(f32[48,16,128]{2,1,0:T(8,128)S(1)} %constant_dynamic-update-slice_fusion), channel_id=1, source_target_pairs={{0,31},{1,0},{2,1},{3,2},{4,3},{5,4},{6,5},{7,6},{8,7},{9,8},{10,9... | collective-permute-start | bytes 1179656 | tf_op jit(solution)/shard_map/ppermute | solution.py:556
  46.9 12.6 %collective-permute-start.6 = (f32[48,16,128]{2,1,0:T(8,128)S(1)}, f32[48,16,128]{2,1,0:T(8,128)S(1)}, u32[]{:S(2)}, u32[]{:S(2)}) collective-permute-start(f32[48,16,128]{2,1,0:T(8,128)S(1)} %constant_dynamic-update-slice_fusion), channel_id=1, source_target_pairs={{0,1},{1,2},{2,3},{3,4},{4,5},{5,6},{6,7},{7,8},{8,9},{9,10},{10,1... | collective-permute-start | bytes 1179656 | tf_op jit(solution)/shard_map/ppermute | solution.py:555
  105.9 1.9 %collective-permute-start.8 = (f32[8,16,128]{2,1,0:T(8,128)S(1)}, f32[8,16,128]{2,1,0:T(8,128)S(1)}, u32[]{:S(2)}, u32[]{:S(2)}) collective-permute-start(f32[8,16,128]{2,1,0:T(8,128)S(1)} %get-tuple-element.59.own), channel_id=1, source_target_pairs={{0,32},{32,64},{64,96},{96,128},{128,160},{160,192},{192,224},{224... | collective-permute-start | bytes 196616 | tf_op jit(solution)/shard_map/ppermute | solution.py:555
  106.5 4.0 %collective-permute-start.9 = (f32[8,16,128]{2,1,0:T(8,128)S(1)}, f32[8,16,128]{2,1,0:T(8,128)S(1)}, u32[]{:S(2)}, u32[]{:S(2)}) collective-permute-start(f32[8,16,128]{2,1,0:T(8,128)S(1)} %get-tuple-element.59.own), channel_id=1, source_target_pairs={{0,224},{32,0},{64,32},{96,64},{128,96},{160,128},{192,160},{224,1... | collective-permute-start | bytes 196616 | tf_op jit(solution)/shard_map/ppermute | solution.py:556
  110.5 5.6 %collective-permute-start.11 = (f32[24,16,128]{2,1,0:T(8,128)S(1)}, f32[24,16,128]{2,1,0:T(8,128)S(1)}, u32[]{:S(2)}, u32[]{:S(2)}) collective-permute-start(f32[24,16,128]{2,1,0:T(8,128)S(1)} %constant_dynamic-update-slice_fusion.3), channel_id=1, source_target_pairs={{0,31},{1,0},{2,1},{3,2},{4,3},{5,4},{6,5},{7,6},{8,7},{9,8},{10,9... | collective-permute-start | bytes 589832 | tf_op jit(solution)/shard_map/ppermute | solution.py:556
  110.9 8.9 %collective-permute-start.10 = (f32[24,16,128]{2,1,0:T(8,128)S(1)}, f32[24,16,128]{2,1,0:T(8,128)S(1)}, u32[]{:S(2)}, u32[]{:S(2)}) collective-permute-start(f32[24,16,128]{2,1,0:T(8,128)S(1)} %constant_dynamic-update-slice_fusion.3), channel_id=1, source_target_pairs={{0,1},{1,2},{2,3},{3,4},{4,5},{5,6},{6,7},{7,8},{8,9},{9,10},{10,1... | collective-permute-start | bytes 589832 | tf_op jit(solution)/shard_map/ppermute | solution.py:555

commit v3 on v2

--- a/solution.py
+++ b/solution.py
@@ -14,29 +14,34 @@
     return pltpu.CompilerParams(vmem_limit_bytes=24 << 20)
 
 
-def call(kernel, ins, outs, scratch=(), smem=(), leave=(), aliases=None):
+def call(kernel, ins, outs, scratch=(), leave=(), aliases=None, hbm=(), touched=0):
     def shape_of(i, s):
         if INTERPRET or i in leave:
             return jax.ShapeDtypeStruct(s, F32)
         return pltpu.VMEM(s, F32)
 
     def place(i, x):
-        if INTERPRET or i in smem:
+        if INTERPRET:
             return x
-        return pltpu.with_memory_space_constraint(x, pltpu.VMEM)
+        return pltpu.with_memory_space_constraint(x, pltpu.HBM if i in hbm else pltpu.VMEM)
 
     specs = [
-        pl.BlockSpec(memory_space=pltpu.SMEM if i in smem else pltpu.VMEM) for i in range(len(ins))
+        pl.BlockSpec(memory_space=pl.ANY if i in hbm else pltpu.VMEM) for i in range(len(ins))
     ]
     return pl.pallas_call(
         kernel,
         out_shape=[shape_of(i, s) for i, s in enumerate(outs)],
         in_specs=specs,
         out_specs=[pl.BlockSpec(memory_space=pltpu.VMEM) for _ in outs],
-        scratch_shapes=[pltpu.VMEM(s, F32) for s in scratch],
+        scratch_shapes=[pltpu.VMEM(s, F32) if isinstance(s, tuple) else s for s in scratch],
         compiler_params=params(),
         input_output_aliases=aliases or {},
         interpret=INTERPRET,
+        cost_estimate=pl.CostEstimate(
+            flops=3 * touched, bytes_accessed=touched, transcendentals=0
+        )
+        if touched
+        else None,
     )(*[place(i, x) for i, x in enumerate(ins)])
 
 
@@ -210,7 +215,23 @@
     blocks(lo, hi, max(2, block_of(v) & ~1), step)
 
 
-def coef_kernel(f, tags, table, rough, coef, to_next, to_prev):
+def coef_kernel(
+    f_hbm, tags_hbm, table_hbm, rough_hbm, coef, to_next, to_prev, packed,
+    tags, table, rough, s, sems,
+):
+    pairs = (
+        (table_hbm, table),
+        (tags_hbm, tags),
+        (rough_hbm, rough),
+        (f_hbm.at[24:32], to_next.at[0:8]),
+        (f_hbm.at[0:8], to_prev.at[0:8]),
+    )
+    copies = [pltpu.make_async_copy(a, b, sems.at[i]) for i, (a, b) in enumerate(pairs)]
+    for copy in copies:
+        copy.start()
+    for copy in copies[:3]:
+        copy.wait()
+
     def step(x, n, _):
         new = []
         for i in range(n):
@@ -224,10 +245,13 @@
         return 0
 
     blocks(0, 32, 8, step)
-    to_next[0:8] = f[24:32]
+    sum_pairs(coef, 0, 16, s)
+    c1 = dot(flat(pair_rows(s, 0, 16) * F32(0.25)), halver(128)).reshape(16, 16, 128)
+    packed[...] = pack_halves(c1)
     to_next[8:17] = coef[23:32]
-    to_prev[0:8] = f[0:8]
     to_prev[8:17] = coef[0:9]
+    for copy in copies[3:]:
+        copy.wait()
 
 
 def rows_kernel(f, coef, left, right, to_next, to_prev):
@@ -248,6 +272,30 @@
                 line = right[8 + x - 41, extra : extra + 1, :]
             out[98 + x // 8, x % 8 : x % 8 + 1, :] = line
         out[104, 2:8, :] = jnp.zeros((6, 128), F32)
+
+
+def pack_halves(a):
+    return a[0:8] + pltpu.roll(a[8:16], 64, 2)
+
+
+def unpack(dst, own, left, right, above, below, flags=None):
+    lanes = iota((48, 128), 1)
+    rows = iota((48, 128), 0)
+    for k in range(3):
+        scale = None
+        if flags is not None:
+            gl, gr, bl, br = flags
+            one = F32(1.0)
+            scale = jnp.where(rows < 16, bl, jnp.where(rows < 32, one, br)) * (gl, one, gr)[k]
+        for i in range(8):
+            if k == 1:
+                slab = jnp.concatenate([above[i], own[i], below[i]], 0)
+            else:
+                slab = (left, None, right)[k][i]
+            if scale is not None:
+                slab = slab * scale
+            dst[16 * k + i] = jnp.where(lanes < 64, slab, F32(0.0))
+            dst[16 * k + 8 + i] = jnp.where(lanes < 64, pltpu.roll(slab, 64, 1), F32(0.0))
 
 
 def edge_flags(ng, nb):
@@ -294,9 +342,7 @@
     sweep(v, fx, op, 1, 47)
     f1 = fine_restrict(v, fx, op, s)
 
-    sum_pairs(coef, 0, 16, s.at[:, 8:40])
-    c1 = dot(flat(pair_rows(s, 8, 16) * F32(0.25)), halver(128)).reshape(16, 16, 128)
-    packed[...] = f1 + pltpu.roll(c1, 64, 2)
+    packed[...] = pack_halves(f1)
 
 
 def fold_rows(send):
@@ -332,22 +378,11 @@
 
 
 def mid_kernel(
-    ng, nb, own, left, right, above, below,
+    ng, nb, own, left, right, above, below, cown, cleft, cright, cabove, cbelow,
     f1, v1, wx1, ws1, wl1, di1, f2, v2, wx2, ws2, wl2, di2, payload, c1, c2, s,
 ):
-    gl, gr, bl, br = edge_flags(ng, nb)
-    lanes = iota((16, 128), 1)
-
-    def put(x, rows, slab, flag):
-        f1[x, rows] = jnp.where(lanes < 64, slab, F32(0.0))
-        c1[x, rows] = jnp.where(lanes < 64, pltpu.roll(slab, 64, 1) * flag, F32(0.0))
-
-    for x in range(48):
-        src, flag = ((left, gl), (own, None), (right, gr))[x // 16]
-        fx = F32(1.0) if flag is None else flag
-        put(x, slice(16, 32), src[x % 16], fx)
-        put(x, slice(0, 16), above[x], fx * bl)
-        put(x, slice(32, 48), below[x], fx * br)
+    unpack(f1, own, left, right, above, below)
+    unpack(c1, cown, cleft, cright, cabove, cbelow, edge_flags(ng, nb))
     op1, op2 = (wx1, ws1, wl1, di1), (wx2, ws2, wl2, di2)
     weights(c1, 0, op1, 1, 47, 63, False)
 
@@ -365,18 +400,7 @@
     own, left, right, above, below, wx1, ws1, wl1, di1, wx2, ws2, wl2, di2,
     f1, v1, f2, v2, payload, s,
 ):
-    lanes = iota((16, 128), 1)
-
-    def put(x, rows, slab):
-        if x % 16 >= 8:
-            slab = pltpu.roll(slab, 64, 1)
-        f1[x, rows] = jnp.where(lanes < 64, slab, F32(0.0))
-
-    for x in range(48):
-        i = x % 8
-        put(x, slice(16, 32), (left, own, right)[x // 16][i])
-        put(x, slice(0, 16), above[8 * (x // 16) + i])
-        put(x, slice(32, 48), below[8 * (x // 16) + i])
+    unpack(f1, own, left, right, above, below)
     op1, op2 = (wx1, ws1, wl1, di1), (wx2, ws2, wl2, di2)
     mid_down(f1, v1, op1, f2, v2, op2, s, payload, None)
 
@@ -500,10 +524,12 @@
     e = dot(flat(v2[5:19]), twice).reshape(14, 24, 128)
     es[5:19, pl.ds(0, 24, stride=2), :] = e
     es[5:19, pl.ds(1, 24, stride=2), :] = e
-    add_double(v1, es, 10, 38)
+    v1, f1 = v1.at[:, 8:40], f1.at[:, 8:40]
+    op1 = tuple(ref.at[:, 8:40] for ref in op1)
+    add_double(v1, es.at[:, 8:40], 10, 38)
     sweep(v1, f1, op1, 11, 37)
     sweep(v1, f1, op1, 12, 36)
-    e = dot(flat(v1[12:36, 12:36, :]), twice).reshape(24, 24, 128)
+    e = dot(flat(v1[12:36, 4:28, :]), twice).reshape(24, 24, 128)
     es[:, pl.ds(0, 24, stride=2), :] = e
     es[:, pl.ds(1, 24, stride=2), :] = e
 
@@ -522,7 +548,7 @@
     for lo in (2, 3, 4, 5):
         sweep(v0, f0, op0, lo, 48 - lo)
     f1n = fine_restrict(v0, f0, op0, s)
-    packed[...] = f1n[0:8] + pltpu.roll(f1n[8:16], 64, 2)
+    packed[...] = pack_halves(f1n)
 
 
 def end_kernel(ng, nb, *refs):
@@ -557,6 +583,17 @@
     return before, after
 
 
+def tall_of(packed, nb):
+    above, below = ring((packed, packed), "box", nb)
+    return above, below, jnp.concatenate([above, packed, below], 1)
+
+
+def around(packed, ng, nb):
+    above, below, tall = tall_of(packed, nb)
+    left, right = ring((tall, tall), "grp", ng)
+    return packed, left, right, above, below
+
+
 def gather_all(payload):
     got = lax.all_to_all(payload, ("grp", "box"), 0, 0, tiled=True)
     return got.reshape(got.shape[0] * got.shape[1], got.shape[2])
@@ -574,23 +611,32 @@
         return lambda *refs: kernel(ng, nb, *refs)
 
     def body(f, tags, table, rough):
-        coef, to_next, to_prev = call(
-            coef_kernel, (f, tags, table, rough), [(32, 32, 128), (17, 32, 128), (17, 32, 128)],
-            smem=(2,),
+        coef, to_next, to_prev, cpack = call(
+            coef_kernel, (f, tags, table, rough),
+            [(32, 32, 128), (17, 32, 128), (17, 32, 128), (8, 16, 128)],
+            scratch=[
+                pltpu.VMEM((32, 32, 128), jnp.int32), pltpu.SMEM((8,), F32), (32, 32, 128),
+                (16, 32, 128), pltpu.SemaphoreType.DMA((5,)),
+            ],
+            hbm=(0, 1, 2, 3),
         )
         left, right = ring((to_next, to_prev), "grp", ng)
+        coarse_above, coarse_below, tall = tall_of(cpack, nb)
+        left, right, tall = lax.optimization_barrier((left, right, tall))
         to_next, to_prev = call(rows_kernel, (f, coef, left, right), [(105, 8, 128)] * 2)
         above, below = ring((to_next, to_prev), "box", nb)
+        coarse_left, coarse_right = ring((tall, tall), "grp", ng)
+        above, below, coarse_left, coarse_right = lax.optimization_barrier(
+            (above, below, coarse_left, coarse_right)
+        )
+        coarse_coef = (cpack, coarse_left, coarse_right, coarse_above, coarse_below)
         v0, f0, wx0, ws0, wl0, di0, packed = call(
-            fix(start_kernel), (f, coef, left, right, above, below), [big] * 6 + [(16, 16, 128)],
-            scratch=[(50, 48, 128), (2, 56, 128), (16, 48, 128)],
+            fix(start_kernel), (f, coef, left, right, above, below), [big] * 6 + [(8, 16, 128)],
+            scratch=[(50, 48, 128), (2, 56, 128), (16, 48, 128)], touched=20_000_000,
         )
         l0 = (f0, wx0, ws0, wl0, di0)
-        left, right = ring((packed, packed), "grp", ng)
-        wide = jnp.concatenate([left, packed, right], 0)
-        above, below = ring((wide, wide), "box", nb)
         f1, v1, wx1, ws1, wl1, di1, f2, v2, wx2, ws2, wl2, di2, payload = call(
-            fix(mid_kernel), (packed, left, right, above, below), [mid] * 6 + [low] * 6 + [pay],
+            fix(mid_kernel), around(packed, ng, nb) + coarse_coef, [mid] * 6 + [low] * 6 + [pay],
             scratch=[(48, 48, 128), (24, 24, 128), (24, 48, 128)], leave=(12,),
         )
         got_c = gather_all(payload)
@@ -599,11 +645,8 @@
             fix(turn_kernel), (got_c,) + l0 + l1 + l2 + (v0, v1, v2), [big, (8, 16, 128)],
             aliases={16: 0}, scratch=[mid, low, (16, 48, 128)] + climb_scratch,
         )
-        left, right = ring((packed, packed), "grp", ng)
-        wide = jnp.concatenate([left, packed, right], 0)
-        above, below = ring((wide, wide), "box", nb)
         f1, v1, f2, v2, payload = call(
-            mid2_kernel, (packed, left, right, above, below) + l1[1:] + l2[1:],
+            mid2_kernel, around(packed, ng, nb) + l1[1:] + l2[1:],
             [mid, mid, low, low, pay2], scratch=[(24, 48, 128)], leave=(4,),
         )
         got = gather_all(payload)

time: 156 us -> 151 us (0.968)
  waiting for transfers between devices: 44.1 us -> 20.5 us
  starting transfers between devices: 19.5 us -> 36.6 us
  blocking collectives: 50.7 us -> 56 us
  local copies, waits for them, and re-layouts: 3.82 us -> 0.04 us
    ppermute x6 -> x8, starting transfers between devices: 13.8 us -> 31.9 us  [ring(): after = lax.ppermute(x[1], axis, [(i, (i - 1) % n) for i in range(n)])]
    ppermute x6 -> x8, waiting for transfers between devices: 24.5 us -> 8.42 us  [ring(): before = lax.ppermute(x[0], axis, [(i, (i + 1) % n) for i in range(n)])]
    ppermute x6 -> x8, waiting for transfers between devices: 19.6 us -> 12.1 us  [ring(): after = lax.ppermute(x[1], axis, [(i, (i - 1) % n) for i in range(n)])]
    all_to_all x2, blocking collectives: 50.7 us -> 56 us  [gather_all(): got = lax.all_to_all(payload, ('grp', 'box'), 0, 0, tiled=True)]
    unnamed x12 -> x6, local copies, waits for them, and re-layouts: 3.8 us -> 0.03 us
    ppermute x6 -> x8, starting transfers between devices: 5.67 us -> 4.72 us  [ring(): before = lax.ppermute(x[0], axis, [(i, (i + 1) % n) for i in range(n)])]
  transfers between devices with their start and end apart: 12 -> 16, of which waited for: 11 -> 7; matrix products, arithmetic and copies ran while one was open for 0% -> 0% of each run, Pallas kernels for 0% -> 0%
where the time goes in v3:
time: 151 us
  blocking collectives  56 us (37%)
  Pallas kernels  37.1 us (25%)
  starting transfers between devices  36.6 us (24%)
  waiting for transfers between devices  20.5 us (14%)
    all_to_all x2, blocking collectives, gather_all(): got = lax.all_to_all(payload, ('grp', 'box'), 0, 0, tiled=True)  56 us
    pallas_call x7, Pallas kernels, call(): pl.pallas_call(kernel, out_shape=[shape_of(i, s) for i, s in enumerate(ou...  37.1 us
    ppermute x8, starting transfers between devices, ring(): after = lax.ppermute(x[1], axis, [(i, (i - 1) % n) for i in range(n)])  31.9 us
    ppermute x8, waiting for transfers between devices, ring(): after = lax.ppermute(x[1], axis, [(i, (i - 1) % n) for i in range(n)])  12.1 us
    ppermute x8, waiting for transfers between devices, ring(): before = lax.ppermute(x[0], axis, [(i, (i + 1) % n) for i in range(n)])  8.42 us
    ppermute x8, starting transfers between devices, ring(): before = lax.ppermute(x[0], axis, [(i, (i + 1) % n) for i in range(n)])  4.72 us
  transfers between devices with their start and end apart: 16, of which 7 were waited for; matrix products, arithmetic and copies ran while one was open for 0% of the time, Pallas kernels for 0%

profile of v3, /device:TPU:1, one launch (start us, length us, event | category | flops | bytes accessed | tf_op | source)
XLA Modules:
  0.0 151.1 jit_solution(11212315778594307901)
XLA Ops:
  0.6 2.0 %shard_map.59 = (f32[32,32,128]{2,1,0:T(8,128)S(1)}, f32[17,32,128]{2,1,0:T(8,128)S(1)}, f32[17,32,128]{2,1,0:T(8,128)S(1)}, f32[8,16,128]{2,1,0:T(8,128)S(1)}) custom-call(f32[32,32,128]{2,1,0:T(8,128)} %refs_0_.1, s32[32,32,128]{2,1,0:T(8,128)} %tags_hbm.1, f32[8]{0:T(128)} %table_hbm.1, f32[32,32,128]{2,1,0:T(8,128)} %rough_hbm.1), custom_call_target="tpu_custom_call" | custom-call | tf_op jit(solution)/shard_map/pallas_call | solution.py:31
  2.6 2.6 %collective-permute-start = (f32[17,32,128]{2,1,0:T(8,128)S(1)}, f32[17,32,128]{2,1,0:T(8,128)S(1)}, u32[]{:S(2)}, u32[]{:S(2)}) collective-permute-start(f32[17,32,128]{2,1,0:T(8,128)S(1)} %get-tuple-element.43), channel_id=1, source_target_pairs={{0,32},{32,64},{64,96},{96,128},{128,160},{160,192},{192,224},{224... | collective-permute-start | bytes 835592 | tf_op jit(solution)/shard_map/ppermute | solution.py:581
  5.2 0.7 collective-permute-start.1
  5.9 7.4 %collective-permute-start.3 = (f32[8,16,128]{2,1,0:T(8,128)S(1)}, f32[8,16,128]{2,1,0:T(8,128)S(1)}, u32[]{:S(2)}, u32[]{:S(2)}) collective-permute-start(f32[8,16,128]{2,1,0:T(8,128)S(1)} %get-tuple-element.45.refs_5_), channel_id=1, source_target_pairs={{0,31},{1,0},{2,1},{3,2},{4,3},{5,4},{6,5},{7,6},{8,7},{9,8},{10,9... | collective-permute-start | bytes 196616 | tf_op jit(solution)/shard_map/ppermute | solution.py:582
  13.3 0.0 collective-permute-start.2
  13.3 1.3 collective-permute-done.3.refs_9_
  14.6 5.1 %collective-permute-done.2.refs_8_ = f32[8,16,128]{2,1,0:T(8,128)S(1)} collective-permute-done((f32[8,16,128]{2,1,0:T(8,128)S(1)}, f32[8,16,128]{2,1,0:T(8,128)S(1)}, u32[]{:S(2)}, u32[]{:S(2)}) %collective-permute-start.2) | collective-permute-done | bytes 65568 | tf_op jit(solution)/shard_map/ppermute | solution.py:581
  19.7 0.1 shard_map.60
  19.9 0.1 collective-permute-start.4
  19.9 4.8 %collective-permute-start.5 = (f32[105,8,128]{2,1,0:T(8,128)S(1)}, f32[105,8,128]{2,1,0:T(8,128)S(1)}, u32[]{:S(2)}, u32[]{:S(2)}) collective-permute-start(f32[105,8,128]{2,1,0:T(8,128)S(1)} %get-tuple-element.49), channel_id=1, source_target_pairs={{0,31},{1,0},{2,1},{3,2},{4,3},{5,4},{6,5},{7,6},{8,7},{9,8},{10,9... | collective-permute-start | bytes 1290248 | tf_op jit(solution)/shard_map/ppermute | solution.py:582
  24.7 3.8 %collective-permute-start.7 = (f32[8,48,128]{2,1,0:T(8,128)S(1)}, f32[8,48,128]{2,1,0:T(8,128)S(1)}, u32[]{:S(2)}, u32[]{:S(2)}) collective-permute-start(f32[8,48,128]{2,1,0:T(8,128)S(1)} %pad_maximum_fusion), channel_id=1, source_target_pairs={{0,224},{32,0},{64,32},{96,64},{128,96},{160,128},{192,160},{224,1... | collective-permute-start | bytes 589832 | tf_op jit(solution)/shard_map/ppermute | solution.py:582
  28.6 3.5 %collective-permute-done.7.refs_7_ = f32[8,48,128]{2,1,0:T(8,128)S(1)} collective-permute-done((f32[8,48,128]{2,1,0:T(8,128)S(1)}, f32[8,48,128]{2,1,0:T(8,128)S(1)}, u32[]{:S(2)}, u32[]{:S(2)}) %collective-permute-start.7) | collective-permute-done | bytes 196640 | tf_op jit(solution)/shard_map/ppermute | solution.py:582
  32.1 0.0 collective-permute-done.6.refs_6_
  32.1 4.0 %shard_map.61 = (f32[48,48,128]{2,1,0:T(8,128)S(1)}, f32[48,48,128]{2,1,0:T(8,128)S(1)}, f32[48,48,128]{2,1,0:T(8,128)S(1)}, f32[48,48,128]{2,1,0:T(8,128)S(1)},...) custom-call(f32[32,32,128]{2,1,0:T(8,128)S(1)} %copy-done, ...), custom_call_target="tpu_custom_call" | custom-call | flops 60000000 | bytes 20000000 | tf_op jit(solution)/shard_map/pallas_call | solution.py:31
  36.1 0.1 collective-permute-start.8
  36.2 4.8 %collective-permute-start.9 = (f32[8,16,128]{2,1,0:T(8,128)S(1)}, f32[8,16,128]{2,1,0:T(8,128)S(1)}, u32[]{:S(2)}, u32[]{:S(2)}) collective-permute-start(f32[8,16,128]{2,1,0:T(8,128)S(1)} %get-tuple-element.53.refs_0_), channel_id=1, source_target_pairs={{0,31},{1,0},{2,1},{3,2},{4,3},{5,4},{6,5},{7,6},{8,7},{9,8},{10,9... | collective-permute-start | bytes 196616 | tf_op jit(solution)/shard_map/ppermute | solution.py:582
  41.0 1.6 %collective-permute-done.8.refs_3_ = f32[8,16,128]{2,1,0:T(8,128)S(1)} collective-permute-done((f32[8,16,128]{2,1,0:T(8,128)S(1)}, f32[8,16,128]{2,1,0:T(8,128)S(1)}, u32[]{:S(2)}, u32[]{:S(2)}) %collective-permute-start.8) | collective-permute-done | bytes 65568 | tf_op jit(solution)/shard_map/ppermute | solution.py:581
  42.6 4.6 %collective-permute-start.11 = (f32[8,48,128]{2,1,0:T(8,128)S(1)}, f32[8,48,128]{2,1,0:T(8,128)S(1)}, u32[]{:S(2)}, u32[]{:S(2)}) collective-permute-start(f32[8,48,128]{2,1,0:T(8,128)S(1)} %constant_dynamic-update-slice_fusion), channel_id=1, source_target_pairs={{0,224},{32,0},{64,32},{96,64},{128,96},{160,128},{192,160},{224,1... | collective-permute-start | bytes 589832 | tf_op jit(solution)/shard_map/ppermute | solution.py:582
  47.3 1.1 collective-permute-start.10
  48.4 3.6 %collective-permute-done.11.refs_2_ = f32[8,48,128]{2,1,0:T(8,128)S(1)} collective-permute-done((f32[8,48,128]{2,1,0:T(8,128)S(1)}, f32[8,48,128]{2,1,0:T(8,128)S(1)}, u32[]{:S(2)}, u32[]{:S(2)}) %collective-permute-start.11) | collective-permute-done | bytes 196640 | tf_op jit(solution)/shard_map/ppermute | solution.py:582
  52.0 6.7 %shard_map.62 = (f32[48,48,128]{2,1,0:T(8,128)S(1)}, f32[48,48,128]{2,1,0:T(8,128)S(1)}, f32[48,48,128]{2,1,0:T(8,128)S(1)}, f32[48,48,128]{2,1,0:T(8,128)S(1)},...) custom-call(f32[8,16,128]{2,1,0:T(8,128)S(1)} %get-tuple-element.53., ...), custom_call_target="tpu_custom_call" | custom-call | tf_op jit(solution)/shard_map/pallas_call | solution.py:31
  58.7 30.9 %all_to_all.10 = f32[256,4,128]{2,1,0:T(4,128)S(1)} all-to-all(f32[256,4,128]{2,1,0:T(4,128)S(1)} %get-tuple-element.56), channel_id=1, replica_groups=mesh['grp'=8,'box'=32] {'grp','box'}, dimensions={0} | all-to-all | bytes 1048576 | tf_op jit(solution)/shard_map/all_to_all | solution.py:598
  89.6 10.8 %shard_map.63 = (f32[48,48,128]{2,1,0:T(8,128)S(1)}, f32[8,16,128]{2,1,0:T(8,128)S(1)}) custom-call(f32[1024,128]{1,0:T(8,128)S(1)} %bitcast.2, f32[48,48,128]{2,1,0:T(8,128)S(1)} %get-tuple-element.57.refs_1_.refs_2_, f32[48,48,128]{2,1,0:T(8,128)S(1)} %get-tuple-element.58.refs_2_.refs_3_, ...), custom_call_target="tpu_custom_call", output_to_operand_aliasing={{0}: (16, {})} | custom-call | tf_op jit(solution)/shard_map/pallas_call | solution.py:31
  100.4 0.6 collective-permute-start.12
  101.0 4.3 %collective-permute-start.13 = (f32[8,16,128]{2,1,0:T(8,128)S(1)}, f32[8,16,128]{2,1,0:T(8,128)S(1)}, u32[]{:S(2)}, u32[]{:S(2)}) collective-permute-start(f32[8,16,128]{2,1,0:T(8,128)S(1)} %get-tuple-element.75.own), channel_id=1, source_target_pairs={{0,31},{1,0},{2,1},{3,2},{4,3},{5,4},{6,5},{7,6},{8,7},{9,8},{10,9... | collective-permute-start | bytes 196616 | tf_op jit(solution)/shard_map/ppermute | solution.py:582
  105.3 1.6 %collective-permute-done.12.above = f32[8,16,128]{2,1,0:T(8,128)S(1)} collective-permute-done((f32[8,16,128]{2,1,0:T(8,128)S(1)}, f32[8,16,128]{2,1,0:T(8,128)S(1)}, u32[]{:S(2)}, u32[]{:S(2)}) %collective-permute-start.12) | collective-permute-done | bytes 65568 | tf_op jit(solution)/shard_map/ppermute | solution.py:581
  107.0 1.6 %collective-permute-start.15 = (f32[8,48,128]{2,1,0:T(8,128)S(1)}, f32[8,48,128]{2,1,0:T(8,128)S(1)}, u32[]{:S(2)}, u32[]{:S(2)}) collective-permute-start(f32[8,48,128]{2,1,0:T(8,128)S(1)} %constant_dynamic-update-slice_fusion.3), channel_id=1, source_target_pairs={{0,224},{32,0},{64,32},{96,64},{128,96},{160,128},{192,160},{224,1... | collective-permute-start | bytes 589832 | tf_op jit(solution)/shard_map/ppermute | solution.py:582
  108.5 0.2 collective-permute-start.14
  108.7 3.6 %collective-permute-done.15.right = f32[8,48,128]{2,1,0:T(8,128)S(1)} collective-permute-done((f32[8,48,128]{2,1,0:T(8,128)S(1)}, f32[8,48,128]{2,1,0:T(8,128)S(1)}, u32[]{:S(2)}, u32[]{:S(2)}) %collective-permute-start.15) | collective-permute-done | bytes 196640 | tf_op jit(solution)/shard_map/ppermute | solution.py:582
  112.4 3.6 %shard_map.64 = (f32[48,48,128]{2,1,0:T(8,128)S(1)}, f32[48,48,128]{2,1,0:T(8,128)S(1)}, f32[24,24,128]{2,1,0:T(8,128)S(1)}, f32[24,24,128]{2,1,0:T(8,128)S(1)}, f32[256,2,128]{2,1,0:T(2,128)S(1)}) custom-call(f32[8,16,128]{2,1,0:T(8,128)S(1)} %get-tuple-element.75.own, f32[8,48,128]{2,1,0:T(8,128)S(1)} %collective-permute-done.14.left, ...), custom_call_target="tpu_custom_call" | custom-call | tf_op jit(solution)/shard_map/pallas_call | solution.py:31
  116.0 25.1 %all_to_all.11 = f32[256,2,128]{2,1,0:T(2,128)S(1)} all-to-all(f32[256,2,128]{2,1,0:T(2,128)S(1)} %get-tuple-element.76), channel_id=1, replica_groups=mesh['grp'=8,'box'=32] {'grp','box'}, dimensions={0} | all-to-all | bytes 524288 | tf_op jit(solution)/shard_map/all_to_all | solution.py:598
  141.1 10.0 %shard_map.65 = (f32[32,32,128]{2,1,0:T(8,128)}, f32[32,32,128]{2,1,0:T(8,128)}) custom-call(f32[512,128]{1,0:T(8,128)S(1)} %bitcast.4, f32[1024,128]{1,0:T(8,128)S(1)} %bitcast.3, f32[48,48,128]{2,1,0:T(8,128)S(1)} %get-tuple-element.57.refs_1_.refs_2_, f32[48,48,128]{2,1,0:T(8,128)S(1)} %get-tuple-element.58.refs_2_.refs_3_, ...), custom_call_target="tpu_custom_call" | custom-call | tf_op jit(solution)/shard_map/pallas_call | solution.py:31
  (18 shorter events, 0.1 us)
Async XLA Ops:
  0.6 19.1 %copy-start = (f32[32,32,128]{2,1,0:T(8,128)S(1)}, f32[32,32,128]{2,1,0:T(8,128)}, u32[]{:S(2)}) copy-start(f32[32,32,128]{2,1,0:T(8,128)} %refs_0_.1) | copy-start | bytes 1572868
  2.6 17.1 %collective-permute-start = (f32[17,32,128]{2,1,0:T(8,128)S(1)}, f32[17,32,128]{2,1,0:T(8,128)S(1)}, u32[]{:S(2)}, u32[]{:S(2)}) collective-permute-start(f32[17,32,128]{2,1,0:T(8,128)S(1)} %get-tuple-element.43), channel_id=1, source_target_pairs={{0,32},{32,64},{64,96},{96,128},{128,160},{160,192},{192,224},{224... | collective-permute-start | bytes 835592 | tf_op jit(solution)/shard_map/ppermute | solution.py:581
  5.2 14.5 %collective-permute-start.1 = (f32[17,32,128]{2,1,0:T(8,128)S(1)}, f32[17,32,128]{2,1,0:T(8,128)S(1)}, u32[]{:S(2)}, u32[]{:S(2)}) collective-permute-start(f32[17,32,128]{2,1,0:T(8,128)S(1)} %get-tuple-element.44), channel_id=1, source_target_pairs={{0,224},{32,0},{64,32},{96,64},{128,96},{160,128},{192,160},{224,1... | collective-permute-start | bytes 835592 | tf_op jit(solution)/shard_map/ppermute | solution.py:582
  5.9 8.7 %collective-permute-start.3 = (f32[8,16,128]{2,1,0:T(8,128)S(1)}, f32[8,16,128]{2,1,0:T(8,128)S(1)}, u32[]{:S(2)}, u32[]{:S(2)}) collective-permute-start(f32[8,16,128]{2,1,0:T(8,128)S(1)} %get-tuple-element.45.refs_5_), channel_id=1, source_target_pairs={{0,31},{1,0},{2,1},{3,2},{4,3},{5,4},{6,5},{7,6},{8,7},{9,8},{10,9... | collective-permute-start | bytes 196616 | tf_op jit(solution)/shard_map/ppermute | solution.py:582
  13.3 6.4 %collective-permute-start.2 = (f32[8,16,128]{2,1,0:T(8,128)S(1)}, f32[8,16,128]{2,1,0:T(8,128)S(1)}, u32[]{:S(2)}, u32[]{:S(2)}) collective-permute-start(f32[8,16,128]{2,1,0:T(8,128)S(1)} %get-tuple-element.45.refs_5_), channel_id=1, source_target_pairs={{0,1},{1,2},{2,3},{3,4},{4,5},{5,6},{6,7},{7,8},{8,9},{9,10},{10,1... | collective-permute-start | bytes 196616 | tf_op jit(solution)/shard_map/ppermute | solution.py:581
  19.9 12.3 %collective-permute-start.4 = (f32[105,8,128]{2,1,0:T(8,128)S(1)}, f32[105,8,128]{2,1,0:T(8,128)S(1)}, u32[]{:S(2)}, u32[]{:S(2)}) collective-permute-start(f32[105,8,128]{2,1,0:T(8,128)S(1)} %get-tuple-element.48), channel_id=1, source_target_pairs={{0,1},{1,2},{2,3},{3,4},{4,5},{5,6},{6,7},{7,8},{8,9},{9,10},{10,1... | collective-permute-start | bytes 1290248 | tf_op jit(solution)/shard_map/ppermute | solution.py:581
  19.9 12.2 %collective-permute-start.5 = (f32[105,8,128]{2,1,0:T(8,128)S(1)}, f32[105,8,128]{2,1,0:T(8,128)S(1)}, u32[]{:S(2)}, u32[]{:S(2)}) collective-permute-start(f32[105,8,128]{2,1,0:T(8,128)S(1)} %get-tuple-element.49), channel_id=1, source_target_pairs={{0,31},{1,0},{2,1},{3,2},{4,3},{5,4},{6,5},{7,6},{8,7},{9,8},{10,9... | collective-permute-start | bytes 1290248 | tf_op jit(solution)/shard_map/ppermute | solution.py:582
  24.7 7.4 %collective-permute-start.7 = (f32[8,48,128]{2,1,0:T(8,128)S(1)}, f32[8,48,128]{2,1,0:T(8,128)S(1)}, u32[]{:S(2)}, u32[]{:S(2)}) collective-permute-start(f32[8,48,128]{2,1,0:T(8,128)S(1)} %pad_maximum_fusion), channel_id=1, source_target_pairs={{0,224},{32,0},{64,32},{96,64},{128,96},{160,128},{192,160},{224,1... | collective-permute-start | bytes 589832 | tf_op jit(solution)/shard_map/ppermute | solution.py:582
  28.6 3.5 %collective-permute-start.6 = (f32[8,48,128]{2,1,0:T(8,128)S(1)}, f32[8,48,128]{2,1,0:T(8,128)S(1)}, u32[]{:S(2)}, u32[]{:S(2)}) collective-permute-start(f32[8,48,128]{2,1,0:T(8,128)S(1)} %pad_maximum_fusion), channel_id=1, source_target_pairs={{0,32},{32,64},{64,96},{96,128},{128,160},{160,192},{192,224},{224... | collective-permute-start | bytes 589832 | tf_op jit(solution)/shard_map/ppermute | solution.py:581
  36.1 6.5 %collective-permute-start.8 = (f32[8,16,128]{2,1,0:T(8,128)S(1)}, f32[8,16,128]{2,1,0:T(8,128)S(1)}, u32[]{:S(2)}, u32[]{:S(2)}) collective-permute-start(f32[8,16,128]{2,1,0:T(8,128)S(1)} %get-tuple-element.53.refs_0_), channel_id=1, source_target_pairs={{0,1},{1,2},{2,3},{3,4},{4,5},{5,6},{6,7},{7,8},{8,9},{9,10},{10,1... | collective-permute-start | bytes 196616 | tf_op jit(solution)/shard_map/ppermute | solution.py:581
  36.2 6.4 %collective-permute-start.9 = (f32[8,16,128]{2,1,0:T(8,128)S(1)}, f32[8,16,128]{2,1,0:T(8,128)S(1)}, u32[]{:S(2)}, u32[]{:S(2)}) collective-permute-start(f32[8,16,128]{2,1,0:T(8,128)S(1)} %get-tuple-element.53.refs_0_), channel_id=1, source_target_pairs={{0,31},{1,0},{2,1},{3,2},{4,3},{5,4},{6,5},{7,6},{8,7},{9,8},{10,9... | collective-permute-start | bytes 196616 | tf_op jit(solution)/shard_map/ppermute | solution.py:582
  42.6 9.4 %collective-permute-start.11 = (f32[8,48,128]{2,1,0:T(8,128)S(1)}, f32[8,48,128]{2,1,0:T(8,128)S(1)}, u32[]{:S(2)}, u32[]{:S(2)}) collective-permute-start(f32[8,48,128]{2,1,0:T(8,128)S(1)} %constant_dynamic-update-slice_fusion), channel_id=1, source_target_pairs={{0,224},{32,0},{64,32},{96,64},{128,96},{160,128},{192,160},{224,1... | collective-permute-start | bytes 589832 | tf_op jit(solution)/shard_map/ppermute | solution.py:582
  47.3 4.7 %collective-permute-start.10 = (f32[8,48,128]{2,1,0:T(8,128)S(1)}, f32[8,48,128]{2,1,0:T(8,128)S(1)}, u32[]{:S(2)}, u32[]{:S(2)}) collective-permute-start(f32[8,48,128]{2,1,0:T(8,128)S(1)} %constant_dynamic-update-slice_fusion), channel_id=1, source_target_pairs={{0,32},{32,64},{64,96},{96,128},{128,160},{160,192},{192,224},{224... | collective-permute-start | bytes 589832 | tf_op jit(solution)/shard_map/ppermute | solution.py:581
  100.4 6.5 %collective-permute-start.12 = (f32[8,16,128]{2,1,0:T(8,128)S(1)}, f32[8,16,128]{2,1,0:T(8,128)S(1)}, u32[]{:S(2)}, u32[]{:S(2)}) collective-permute-start(f32[8,16,128]{2,1,0:T(8,128)S(1)} %get-tuple-element.75.own), channel_id=1, source_target_pairs={{0,1},{1,2},{2,3},{3,4},{4,5},{5,6},{6,7},{7,8},{8,9},{9,10},{10,1... | collective-permute-start | bytes 196616 | tf_op jit(solution)/shard_map/ppermute | solution.py:581
  101.0 5.9 %collective-permute-start.13 = (f32[8,16,128]{2,1,0:T(8,128)S(1)}, f32[8,16,128]{2,1,0:T(8,128)S(1)}, u32[]{:S(2)}, u32[]{:S(2)}) collective-permute-start(f32[8,16,128]{2,1,0:T(8,128)S(1)} %get-tuple-element.75.own), channel_id=1, source_target_pairs={{0,31},{1,0},{2,1},{3,2},{4,3},{5,4},{6,5},{7,6},{8,7},{9,8},{10,9... | collective-permute-start | bytes 196616 | tf_op jit(solution)/shard_map/ppermute | solution.py:582
  107.0 5.4 %collective-permute-start.15 = (f32[8,48,128]{2,1,0:T(8,128)S(1)}, f32[8,48,128]{2,1,0:T(8,128)S(1)}, u32[]{:S(2)}, u32[]{:S(2)}) collective-permute-start(f32[8,48,128]{2,1,0:T(8,128)S(1)} %constant_dynamic-update-slice_fusion.3), channel_id=1, source_target_pairs={{0,224},{32,0},{64,32},{96,64},{128,96},{160,128},{192,160},{224,1... | collective-permute-start | bytes 589832 | tf_op jit(solution)/shard_map/ppermute | solution.py:582
  108.5 3.9 %collective-permute-start.14 = (f32[8,48,128]{2,1,0:T(8,128)S(1)}, f32[8,48,128]{2,1,0:T(8,128)S(1)}, u32[]{:S(2)}, u32[]{:S(2)}) collective-permute-start(f32[8,48,128]{2,1,0:T(8,128)S(1)} %constant_dynamic-update-slice_fusion.3), channel_id=1, source_target_pairs={{0,32},{32,64},{64,96},{96,128},{128,160},{160,192},{192,224},{224... | collective-permute-start | bytes 589832 | tf_op jit(solution)/shard_map/ppermute | solution.py:581

commit v4 on v3

--- a/solution.py
+++ b/solution.py
@@ -377,23 +377,29 @@
     return total[4:8]
 
 
-def mid_kernel(
-    ng, nb, own, left, right, above, below, cown, cleft, cright, cabove, cbelow,
-    f1, v1, wx1, ws1, wl1, di1, f2, v2, wx2, ws2, wl2, di2, payload, c1, c2, s,
+def mid_weights_kernel(
+    ng, nb, cown, cleft, cright, cabove, cbelow,
+    wx1, ws1, wl1, di1, wx2, ws2, wl2, di2, coarser, c1, c2, s,
 ):
-    unpack(f1, own, left, right, above, below)
     unpack(c1, cown, cleft, cright, cabove, cbelow, edge_flags(ng, nb))
-    op1, op2 = (wx1, ws1, wl1, di1), (wx2, ws2, wl2, di2)
-    weights(c1, 0, op1, 1, 47, 63, False)
-
+    weights(c1, 0, (wx1, ws1, wl1, di1), 1, 47, 63, False)
     sum_pairs(c1, 0, 24, s)
     half = halver(128)
     c2[...] = dot(flat(pair_rows(s, 0, 24) * F32(0.25)), half).reshape(24, 24, 128)
-    weights(c2, 0, op2, 1, 23, 31, False)
+    weights(c2, 0, (wx2, ws2, wl2, di2), 1, 23, 31, False)
     for x in range(4):
         s[x, 0:24] = c2[8 + 2 * x] + c2[9 + 2 * x]
-    extra = collect(s, half, 64, F32(0.25))
-    mid_down(f1, v1, op1, f2, v2, op2, s, payload, extra)
+    send = collect(s, half, 64, F32(0.25))
+    coarser[...] = send
+
+
+def mid_kernel(
+    own, left, right, above, below, wx1, ws1, wl1, di1, wx2, ws2, wl2, di2, coarser,
+    f1, v1, f2, v2, payload, s,
+):
+    unpack(f1, own, left, right, above, below)
+    op1, op2 = (wx1, ws1, wl1, di1), (wx2, ws2, wl2, di2)
+    mid_down(f1, v1, op1, f2, v2, op2, s, payload, coarser[...])
 
 
 def mid2_kernel(
@@ -635,12 +641,16 @@
             scratch=[(50, 48, 128), (2, 56, 128), (16, 48, 128)], touched=20_000_000,
         )
         l0 = (f0, wx0, ws0, wl0, di0)
-        f1, v1, wx1, ws1, wl1, di1, f2, v2, wx2, ws2, wl2, di2, payload = call(
-            fix(mid_kernel), around(packed, ng, nb) + coarse_coef, [mid] * 6 + [low] * 6 + [pay],
-            scratch=[(48, 48, 128), (24, 24, 128), (24, 48, 128)], leave=(12,),
+        *ops, coarser = call(
+            fix(mid_weights_kernel), coarse_coef, [mid] * 4 + [low] * 4 + [(4, 128)],
+            scratch=[(48, 48, 128), (24, 24, 128), (24, 48, 128)],
+        )
+        f1, v1, f2, v2, payload = call(
+            mid_kernel, around(packed, ng, nb) + tuple(ops) + (coarser,),
+            [mid, mid, low, low, pay], scratch=[(24, 48, 128)], leave=(4,),
         )
         got_c = gather_all(payload)
-        l1, l2 = (f1, wx1, ws1, wl1, di1), (f2, wx2, ws2, wl2, di2)
+        l1, l2 = (f1, *ops[:4]), (f2, *ops[4:])
         v0, packed = call(
             fix(turn_kernel), (got_c,) + l0 + l1 + l2 + (v0, v1, v2), [big, (8, 16, 128)],
             aliases={16: 0}, scratch=[mid, low, (16, 48, 128)] + climb_scratch,

time: 151 us -> 149 us (0.987)
  waiting for transfers between devices: 20.5 us -> 17.4 us
    ppermute x8, waiting for transfers between devices: 12.1 us -> 8.94 us  [ring(): after = lax.ppermute(x[1], axis, [(i, (i - 1) % n) for i in range(n)])]
    pallas_call x7 -> x8, Pallas kernels: 37.1 us -> 38.1 us  [call(): pl.pallas_call(kernel, out_shape=[shape_of(i, s) for i, s in enumerate(ou...]
  transfers between devices with their start and end apart: 16 -> 16, of which waited for: 7 -> 7; matrix products, arithmetic and copies ran while one was open for 0% -> 0% of each run, Pallas kernels for 0% -> 2%
where the time goes in v4:
time: 149 us
  blocking collectives  56 us (38%)
  Pallas kernels  38.1 us (26%)
  starting transfers between devices  36.6 us (25%)
  waiting for transfers between devices  17.4 us (12%)
    all_to_all x2, blocking collectives, gather_all(): got = lax.all_to_all(payload, ('grp', 'box'), 0, 0, tiled=True)  56 us
    pallas_call x8, Pallas kernels, call(): pl.pallas_call(kernel, out_shape=[shape_of(i, s) for i, s in enumerate(ou...  38.1 us
    ppermute x8, starting transfers between devices, ring(): after = lax.ppermute(x[1], axis, [(i, (i - 1) % n) for i in range(n)])  31.9 us
    ppermute x8, waiting for transfers between devices, ring(): after = lax.ppermute(x[1], axis, [(i, (i - 1) % n) for i in range(n)])  8.94 us
    ppermute x8, waiting for transfers between devices, ring(): before = lax.ppermute(x[0], axis, [(i, (i + 1) % n) for i in range(n)])  8.42 us
    ppermute x8, starting transfers between devices, ring(): before = lax.ppermute(x[0], axis, [(i, (i + 1) % n) for i in range(n)])  4.71 us
  transfers between devices with their start and end apart: 16, of which 7 were waited for; matrix products, arithmetic and copies ran while one was open for 0% of the time, Pallas kernels for 2%

profile of v4, /device:TPU:1, one launch (start us, length us, event | category | flops | bytes accessed | tf_op | source)
XLA Modules:
  0.0 148.9 jit_solution(18083641881660855527)
XLA Ops:
  0.6 2.0 %shard_map.59 = (f32[32,32,128]{2,1,0:T(8,128)S(1)}, f32[17,32,128]{2,1,0:T(8,128)S(1)}, f32[17,32,128]{2,1,0:T(8,128)S(1)}, f32[8,16,128]{2,1,0:T(8,128)S(1)}) custom-call(f32[32,32,128]{2,1,0:T(8,128)} %refs_0_.1, s32[32,32,128]{2,1,0:T(8,128)} %tags_hbm.1, f32[8]{0:T(128)} %table_hbm.1, f32[32,32,128]{2,1,0:T(8,128)} %rough_hbm.1), custom_call_target="tpu_custom_call" | custom-call | tf_op jit(solution)/shard_map/pallas_call | solution.py:31
  2.6 2.6 %collective-permute-start = (f32[17,32,128]{2,1,0:T(8,128)S(1)}, f32[17,32,128]{2,1,0:T(8,128)S(1)}, u32[]{:S(2)}, u32[]{:S(2)}) collective-permute-start(f32[17,32,128]{2,1,0:T(8,128)S(1)} %get-tuple-element.44), channel_id=1, source_target_pairs={{0,32},{32,64},{64,96},{96,128},{128,160},{160,192},{192,224},{224... | collective-permute-start | bytes 835592 | tf_op jit(solution)/shard_map/ppermute | solution.py:587
  5.2 0.7 collective-permute-start.1
  5.9 7.4 %collective-permute-start.3 = (f32[8,16,128]{2,1,0:T(8,128)S(1)}, f32[8,16,128]{2,1,0:T(8,128)S(1)}, u32[]{:S(2)}, u32[]{:S(2)}) collective-permute-start(f32[8,16,128]{2,1,0:T(8,128)S(1)} %get-tuple-element.46.refs_0_), channel_id=1, source_target_pairs={{0,31},{1,0},{2,1},{3,2},{4,3},{5,4},{6,5},{7,6},{8,7},{9,8},{10,9... | collective-permute-start | bytes 196616 | tf_op jit(solution)/shard_map/ppermute | solution.py:588
  13.3 0.0 collective-permute-start.2
  13.3 1.3 collective-permute-done.3.refs_4_
  14.6 5.1 %collective-permute-done.2.refs_3_ = f32[8,16,128]{2,1,0:T(8,128)S(1)} collective-permute-done((f32[8,16,128]{2,1,0:T(8,128)S(1)}, f32[8,16,128]{2,1,0:T(8,128)S(1)}, u32[]{:S(2)}, u32[]{:S(2)}) %collective-permute-start.2) | collective-permute-done | bytes 65568 | tf_op jit(solution)/shard_map/ppermute | solution.py:587
  19.7 0.1 shard_map.60
  19.9 0.1 collective-permute-start.4
  19.9 4.8 %collective-permute-start.5 = (f32[105,8,128]{2,1,0:T(8,128)S(1)}, f32[105,8,128]{2,1,0:T(8,128)S(1)}, u32[]{:S(2)}, u32[]{:S(2)}) collective-permute-start(f32[105,8,128]{2,1,0:T(8,128)S(1)} %get-tuple-element.50), channel_id=1, source_target_pairs={{0,31},{1,0},{2,1},{3,2},{4,3},{5,4},{6,5},{7,6},{8,7},{9,8},{10,9... | collective-permute-start | bytes 1290248 | tf_op jit(solution)/shard_map/ppermute | solution.py:588
  24.7 3.8 %collective-permute-start.7 = (f32[8,48,128]{2,1,0:T(8,128)S(1)}, f32[8,48,128]{2,1,0:T(8,128)S(1)}, u32[]{:S(2)}, u32[]{:S(2)}) collective-permute-start(f32[8,48,128]{2,1,0:T(8,128)S(1)} %pad_maximum_fusion), channel_id=1, source_target_pairs={{0,224},{32,0},{64,32},{96,64},{128,96},{160,128},{192,160},{224,1... | collective-permute-start | bytes 589832 | tf_op jit(solution)/shard_map/ppermute | solution.py:588
  28.6 3.5 %collective-permute-done.7.refs_2_ = f32[8,48,128]{2,1,0:T(8,128)S(1)} collective-permute-done((f32[8,48,128]{2,1,0:T(8,128)S(1)}, f32[8,48,128]{2,1,0:T(8,128)S(1)}, u32[]{:S(2)}, u32[]{:S(2)}) %collective-permute-start.7) | collective-permute-done | bytes 196640 | tf_op jit(solution)/shard_map/ppermute | solution.py:588
  32.1 4.2 %shard_map.61 = (f32[48,48,128]{2,1,0:T(8,128)S(1)}, f32[48,48,128]{2,1,0:T(8,128)S(1)}, f32[48,48,128]{2,1,0:T(8,128)S(1)}, f32[48,48,128]{2,1,0:T(8,128)S(1)},...) custom-call(f32[32,32,128]{2,1,0:T(8,128)S(1)} %copy-done, ...), custom_call_target="tpu_custom_call" | custom-call | flops 60000000 | bytes 20000000 | tf_op jit(solution)/shard_map/pallas_call | solution.py:31
  36.3 0.1 collective-permute-start.8
  36.4 4.8 %collective-permute-start.9 = (f32[8,16,128]{2,1,0:T(8,128)S(1)}, f32[8,16,128]{2,1,0:T(8,128)S(1)}, u32[]{:S(2)}, u32[]{:S(2)}) collective-permute-start(f32[8,16,128]{2,1,0:T(8,128)S(1)} %get-tuple-element.54.own), channel_id=1, source_target_pairs={{0,31},{1,0},{2,1},{3,2},{4,3},{5,4},{6,5},{7,6},{8,7},{9,8},{10,9... | collective-permute-start | bytes 196616 | tf_op jit(solution)/shard_map/ppermute | solution.py:588
  41.2 1.6 %collective-permute-done.8.above = f32[8,16,128]{2,1,0:T(8,128)S(1)} collective-permute-done((f32[8,16,128]{2,1,0:T(8,128)S(1)}, f32[8,16,128]{2,1,0:T(8,128)S(1)}, u32[]{:S(2)}, u32[]{:S(2)}) %collective-permute-start.8) | collective-permute-done | bytes 65568 | tf_op jit(solution)/shard_map/ppermute | solution.py:587
  42.8 4.6 %collective-permute-start.11 = (f32[8,48,128]{2,1,0:T(8,128)S(1)}, f32[8,48,128]{2,1,0:T(8,128)S(1)}, u32[]{:S(2)}, u32[]{:S(2)}) collective-permute-start(f32[8,48,128]{2,1,0:T(8,128)S(1)} %constant_dynamic-update-slice_fusion), channel_id=1, source_target_pairs={{0,224},{32,0},{64,32},{96,64},{128,96},{160,128},{192,160},{224,1... | collective-permute-start | bytes 589832 | tf_op jit(solution)/shard_map/ppermute | solution.py:588
  47.5 1.1 collective-permute-start.10
  48.6 3.2 %shard_map.62 = (f32[48,48,128]{2,1,0:T(8,128)S(1)}, f32[48,48,128]{2,1,0:T(8,128)S(1)}, f32[48,48,128]{2,1,0:T(8,128)S(1)}, f32[48,48,128]{2,1,0:T(8,128)S(1)},...) custom-call(f32[8,16,128]{2,1,0:T(8,128)S(1)} %get-tuple-element.46., ...), custom_call_target="tpu_custom_call" | custom-call | tf_op jit(solution)/shard_map/pallas_call | solution.py:31
  51.8 0.4 collective-permute-done.11.right
  52.2 3.7 %shard_map.63 = (f32[48,48,128]{2,1,0:T(8,128)S(1)}, f32[48,48,128]{2,1,0:T(8,128)S(1)}, f32[24,24,128]{2,1,0:T(8,128)S(1)}, f32[24,24,128]{2,1,0:T(8,128)S(1)}, f32[256,4,128]{2,1,0:T(4,128)S(1)}) custom-call(f32[8,16,128]{2,1,0:T(8,128)S(1)} %get-tuple-element.54.own, f32[8,48,128]{2,1,0:T(8,128)S(1)} %collective-permute-done.10.left, ...), custom_call_target="tpu_custom_call" | custom-call | tf_op jit(solution)/shard_map/pallas_call | solution.py:31
  56.0 30.9 %all_to_all.10 = f32[256,4,128]{2,1,0:T(4,128)S(1)} all-to-all(f32[256,4,128]{2,1,0:T(4,128)S(1)} %get-tuple-element.66), channel_id=1, replica_groups=mesh['grp'=8,'box'=32] {'grp','box'}, dimensions={0} | all-to-all | bytes 1048576 | tf_op jit(solution)/shard_map/all_to_all | solution.py:604
  86.9 11.3 %shard_map.64 = (f32[48,48,128]{2,1,0:T(8,128)S(1)}, f32[8,16,128]{2,1,0:T(8,128)S(1)}) custom-call(f32[1024,128]{1,0:T(8,128)S(1)} %bitcast.2, f32[48,48,128]{2,1,0:T(8,128)S(1)} %get-tuple-element.67.refs_1_.refs_2_, f32[48,48,128]{2,1,0:T(8,128)S(1)} %get-tuple-element.68.refs_2_.refs_3_, ...), custom_call_target="tpu_custom_call", output_to_operand_aliasing={{0}: (16, {})} | custom-call | tf_op jit(solution)/shard_map/pallas_call | solution.py:31
  98.1 0.6 collective-permute-start.12
  98.7 4.3 %collective-permute-start.13 = (f32[8,16,128]{2,1,0:T(8,128)S(1)}, f32[8,16,128]{2,1,0:T(8,128)S(1)}, u32[]{:S(2)}, u32[]{:S(2)}) collective-permute-start(f32[8,16,128]{2,1,0:T(8,128)S(1)} %get-tuple-element.77.own), channel_id=1, source_target_pairs={{0,31},{1,0},{2,1},{3,2},{4,3},{5,4},{6,5},{7,6},{8,7},{9,8},{10,9... | collective-permute-start | bytes 196616 | tf_op jit(solution)/shard_map/ppermute | solution.py:588
  103.0 1.6 %collective-permute-done.12.above = f32[8,16,128]{2,1,0:T(8,128)S(1)} collective-permute-done((f32[8,16,128]{2,1,0:T(8,128)S(1)}, f32[8,16,128]{2,1,0:T(8,128)S(1)}, u32[]{:S(2)}, u32[]{:S(2)}) %collective-permute-start.12) | collective-permute-done | bytes 65568 | tf_op jit(solution)/shard_map/ppermute | solution.py:587
  104.7 1.6 %collective-permute-start.15 = (f32[8,48,128]{2,1,0:T(8,128)S(1)}, f32[8,48,128]{2,1,0:T(8,128)S(1)}, u32[]{:S(2)}, u32[]{:S(2)}) collective-permute-start(f32[8,48,128]{2,1,0:T(8,128)S(1)} %constant_dynamic-update-slice_fusion.3), channel_id=1, source_target_pairs={{0,224},{32,0},{64,32},{96,64},{128,96},{160,128},{192,160},{224,1... | collective-permute-start | bytes 589832 | tf_op jit(solution)/shard_map/ppermute | solution.py:588
  106.2 0.2 collective-permute-start.14
  106.5 3.6 %collective-permute-done.15.right = f32[8,48,128]{2,1,0:T(8,128)S(1)} collective-permute-done((f32[8,48,128]{2,1,0:T(8,128)S(1)}, f32[8,48,128]{2,1,0:T(8,128)S(1)}, u32[]{:S(2)}, u32[]{:S(2)}) %collective-permute-start.15) | collective-permute-done | bytes 196640 | tf_op jit(solution)/shard_map/ppermute | solution.py:588
  110.1 3.6 %shard_map.65 = (f32[48,48,128]{2,1,0:T(8,128)S(1)}, f32[48,48,128]{2,1,0:T(8,128)S(1)}, f32[24,24,128]{2,1,0:T(8,128)S(1)}, f32[24,24,128]{2,1,0:T(8,128)S(1)}, f32[256,2,128]{2,1,0:T(2,128)S(1)}) custom-call(f32[8,16,128]{2,1,0:T(8,128)S(1)} %get-tuple-element.77.own, f32[8,48,128]{2,1,0:T(8,128)S(1)} %collective-permute-done.14.left, ...), custom_call_target="tpu_custom_call" | custom-call | tf_op jit(solution)/shard_map/pallas_call | solution.py:31
  113.7 25.1 %all_to_all.11 = f32[256,2,128]{2,1,0:T(2,128)S(1)} all-to-all(f32[256,2,128]{2,1,0:T(2,128)S(1)} %get-tuple-element.78), channel_id=1, replica_groups=mesh['grp'=8,'box'=32] {'grp','box'}, dimensions={0} | all-to-all | bytes 524288 | tf_op jit(solution)/shard_map/all_to_all | solution.py:604
  138.8 10.1 %shard_map.66 = (f32[32,32,128]{2,1,0:T(8,128)}, f32[32,32,128]{2,1,0:T(8,128)}) custom-call(f32[512,128]{1,0:T(8,128)S(1)} %bitcast.4, f32[1024,128]{1,0:T(8,128)S(1)} %bitcast.3, f32[48,48,128]{2,1,0:T(8,128)S(1)} %get-tuple-element.67.refs_1_.refs_2_, f32[48,48,128]{2,1,0:T(8,128)S(1)} %get-tuple-element.68.refs_2_.refs_3_, ...), custom_call_target="tpu_custom_call" | custom-call | tf_op jit(solution)/shard_map/pallas_call | solution.py:31
  (19 shorter events, 0.1 us)
Async XLA Ops:
  0.6 19.1 %copy-start = (f32[32,32,128]{2,1,0:T(8,128)S(1)}, f32[32,32,128]{2,1,0:T(8,128)}, u32[]{:S(2)}) copy-start(f32[32,32,128]{2,1,0:T(8,128)} %refs_0_.1) | copy-start | bytes 1572868
  2.6 17.1 %collective-permute-start = (f32[17,32,128]{2,1,0:T(8,128)S(1)}, f32[17,32,128]{2,1,0:T(8,128)S(1)}, u32[]{:S(2)}, u32[]{:S(2)}) collective-permute-start(f32[17,32,128]{2,1,0:T(8,128)S(1)} %get-tuple-element.44), channel_id=1, source_target_pairs={{0,32},{32,64},{64,96},{96,128},{128,160},{160,192},{192,224},{224... | collective-permute-start | bytes 835592 | tf_op jit(solution)/shard_map/ppermute | solution.py:587
  5.2 14.5 %collective-permute-start.1 = (f32[17,32,128]{2,1,0:T(8,128)S(1)}, f32[17,32,128]{2,1,0:T(8,128)S(1)}, u32[]{:S(2)}, u32[]{:S(2)}) collective-permute-start(f32[17,32,128]{2,1,0:T(8,128)S(1)} %get-tuple-element.45), channel_id=1, source_target_pairs={{0,224},{32,0},{64,32},{96,64},{128,96},{160,128},{192,160},{224,1... | collective-permute-start | bytes 835592 | tf_op jit(solution)/shard_map/ppermute | solution.py:588
  5.9 8.7 %collective-permute-start.3 = (f32[8,16,128]{2,1,0:T(8,128)S(1)}, f32[8,16,128]{2,1,0:T(8,128)S(1)}, u32[]{:S(2)}, u32[]{:S(2)}) collective-permute-start(f32[8,16,128]{2,1,0:T(8,128)S(1)} %get-tuple-element.46.refs_0_), channel_id=1, source_target_pairs={{0,31},{1,0},{2,1},{3,2},{4,3},{5,4},{6,5},{7,6},{8,7},{9,8},{10,9... | collective-permute-start | bytes 196616 | tf_op jit(solution)/shard_map/ppermute | solution.py:588
  13.3 6.4 %collective-permute-start.2 = (f32[8,16,128]{2,1,0:T(8,128)S(1)}, f32[8,16,128]{2,1,0:T(8,128)S(1)}, u32[]{:S(2)}, u32[]{:S(2)}) collective-permute-start(f32[8,16,128]{2,1,0:T(8,128)S(1)} %get-tuple-element.46.refs_0_), channel_id=1, source_target_pairs={{0,1},{1,2},{2,3},{3,4},{4,5},{5,6},{6,7},{7,8},{8,9},{9,10},{10,1... | collective-permute-start | bytes 196616 | tf_op jit(solution)/shard_map/ppermute | solution.py:587
  19.9 12.3 %collective-permute-start.4 = (f32[105,8,128]{2,1,0:T(8,128)S(1)}, f32[105,8,128]{2,1,0:T(8,128)S(1)}, u32[]{:S(2)}, u32[]{:S(2)}) collective-permute-start(f32[105,8,128]{2,1,0:T(8,128)S(1)} %get-tuple-element.49), channel_id=1, source_target_pairs={{0,1},{1,2},{2,3},{3,4},{4,5},{5,6},{6,7},{7,8},{8,9},{9,10},{10,1... | collective-permute-start | bytes 1290248 | tf_op jit(solution)/shard_map/ppermute | solution.py:587
  19.9 12.2 %collective-permute-start.5 = (f32[105,8,128]{2,1,0:T(8,128)S(1)}, f32[105,8,128]{2,1,0:T(8,128)S(1)}, u32[]{:S(2)}, u32[]{:S(2)}) collective-permute-start(f32[105,8,128]{2,1,0:T(8,128)S(1)} %get-tuple-element.50), channel_id=1, source_target_pairs={{0,31},{1,0},{2,1},{3,2},{4,3},{5,4},{6,5},{7,6},{8,7},{9,8},{10,9... | collective-permute-start | bytes 1290248 | tf_op jit(solution)/shard_map/ppermute | solution.py:588
  24.7 7.4 %collective-permute-start.7 = (f32[8,48,128]{2,1,0:T(8,128)S(1)}, f32[8,48,128]{2,1,0:T(8,128)S(1)}, u32[]{:S(2)}, u32[]{:S(2)}) collective-permute-start(f32[8,48,128]{2,1,0:T(8,128)S(1)} %pad_maximum_fusion), channel_id=1, source_target_pairs={{0,224},{32,0},{64,32},{96,64},{128,96},{160,128},{192,160},{224,1... | collective-permute-start | bytes 589832 | tf_op jit(solution)/shard_map/ppermute | solution.py:588
  28.6 3.5 %collective-permute-start.6 = (f32[8,48,128]{2,1,0:T(8,128)S(1)}, f32[8,48,128]{2,1,0:T(8,128)S(1)}, u32[]{:S(2)}, u32[]{:S(2)}) collective-permute-start(f32[8,48,128]{2,1,0:T(8,128)S(1)} %pad_maximum_fusion), channel_id=1, source_target_pairs={{0,32},{32,64},{64,96},{96,128},{128,160},{160,192},{192,224},{224... | collective-permute-start | bytes 589832 | tf_op jit(solution)/shard_map/ppermute | solution.py:587
  36.3 6.5 %collective-permute-start.8 = (f32[8,16,128]{2,1,0:T(8,128)S(1)}, f32[8,16,128]{2,1,0:T(8,128)S(1)}, u32[]{:S(2)}, u32[]{:S(2)}) collective-permute-start(f32[8,16,128]{2,1,0:T(8,128)S(1)} %get-tuple-element.54.own), channel_id=1, source_target_pairs={{0,1},{1,2},{2,3},{3,4},{4,5},{5,6},{6,7},{7,8},{8,9},{9,10},{10,1... | collective-permute-start | bytes 196616 | tf_op jit(solution)/shard_map/ppermute | solution.py:587
  36.4 6.4 %collective-permute-start.9 = (f32[8,16,128]{2,1,0:T(8,128)S(1)}, f32[8,16,128]{2,1,0:T(8,128)S(1)}, u32[]{:S(2)}, u32[]{:S(2)}) collective-permute-start(f32[8,16,128]{2,1,0:T(8,128)S(1)} %get-tuple-element.54.own), channel_id=1, source_target_pairs={{0,31},{1,0},{2,1},{3,2},{4,3},{5,4},{6,5},{7,6},{8,7},{9,8},{10,9... | collective-permute-start | bytes 196616 | tf_op jit(solution)/shard_map/ppermute | solution.py:588
  42.8 9.4 %collective-permute-start.11 = (f32[8,48,128]{2,1,0:T(8,128)S(1)}, f32[8,48,128]{2,1,0:T(8,128)S(1)}, u32[]{:S(2)}, u32[]{:S(2)}) collective-permute-start(f32[8,48,128]{2,1,0:T(8,128)S(1)} %constant_dynamic-update-slice_fusion), channel_id=1, source_target_pairs={{0,224},{32,0},{64,32},{96,64},{128,96},{160,128},{192,160},{224,1... | collective-permute-start | bytes 589832 | tf_op jit(solution)/shard_map/ppermute | solution.py:588
  47.5 4.7 %collective-permute-start.10 = (f32[8,48,128]{2,1,0:T(8,128)S(1)}, f32[8,48,128]{2,1,0:T(8,128)S(1)}, u32[]{:S(2)}, u32[]{:S(2)}) collective-permute-start(f32[8,48,128]{2,1,0:T(8,128)S(1)} %constant_dynamic-update-slice_fusion), channel_id=1, source_target_pairs={{0,32},{32,64},{64,96},{96,128},{128,160},{160,192},{192,224},{224... | collective-permute-start | bytes 589832 | tf_op jit(solution)/shard_map/ppermute | solution.py:587
  98.1 6.5 %collective-permute-start.12 = (f32[8,16,128]{2,1,0:T(8,128)S(1)}, f32[8,16,128]{2,1,0:T(8,128)S(1)}, u32[]{:S(2)}, u32[]{:S(2)}) collective-permute-start(f32[8,16,128]{2,1,0:T(8,128)S(1)} %get-tuple-element.77.own), channel_id=1, source_target_pairs={{0,1},{1,2},{2,3},{3,4},{4,5},{5,6},{6,7},{7,8},{8,9},{9,10},{10,1... | collective-permute-start | bytes 196616 | tf_op jit(solution)/shard_map/ppermute | solution.py:587
  98.7 5.9 %collective-permute-start.13 = (f32[8,16,128]{2,1,0:T(8,128)S(1)}, f32[8,16,128]{2,1,0:T(8,128)S(1)}, u32[]{:S(2)}, u32[]{:S(2)}) collective-permute-start(f32[8,16,128]{2,1,0:T(8,128)S(1)} %get-tuple-element.77.own), channel_id=1, source_target_pairs={{0,31},{1,0},{2,1},{3,2},{4,3},{5,4},{6,5},{7,6},{8,7},{9,8},{10,9... | collective-permute-start | bytes 196616 | tf_op jit(solution)/shard_map/ppermute | solution.py:588
  104.7 5.4 %collective-permute-start.15 = (f32[8,48,128]{2,1,0:T(8,128)S(1)}, f32[8,48,128]{2,1,0:T(8,128)S(1)}, u32[]{:S(2)}, u32[]{:S(2)}) collective-permute-start(f32[8,48,128]{2,1,0:T(8,128)S(1)} %constant_dynamic-update-slice_fusion.3), channel_id=1, source_target_pairs={{0,224},{32,0},{64,32},{96,64},{128,96},{160,128},{192,160},{224,1... | collective-permute-start | bytes 589832 | tf_op jit(solution)/shard_map/ppermute | solution.py:588
  106.2 3.8 %collective-permute-start.14 = (f32[8,48,128]{2,1,0:T(8,128)S(1)}, f32[8,48,128]{2,1,0:T(8,128)S(1)}, u32[]{:S(2)}, u32[]{:S(2)}) collective-permute-start(f32[8,48,128]{2,1,0:T(8,128)S(1)} %constant_dynamic-update-slice_fusion.3), channel_id=1, source_target_pairs={{0,32},{32,64},{64,96},{96,128},{128,160},{160,192},{192,224},{224... | collective-permute-start | bytes 589832 | tf_op jit(solution)/shard_map/ppermute | solution.py:587

commit v5 on v4

--- a/solution.py
+++ b/solution.py
@@ -59,6 +59,26 @@
     return jnp.where((k >> 1) == j, F32(1.0), F32(0.0))
 
 
+def halver_at(h):
+    k, j = iota((128, 128), 0), iota((128, 128), 1)
+    return jnp.where((k >> 1) + 64 * h == j, F32(0.5), F32(0.0))
+
+
+def doubler_at(h):
+    j, k = iota((128, 128), 0), iota((128, 128), 1)
+    return jnp.where((k >> 1) + 64 * h == j, F32(1.0), F32(0.0))
+
+
+def folder():
+    k, j = iota((128, 128), 0), iota((128, 128), 1)
+    return jnp.where(((k & 63) >> 1) == j, F32(0.5), F32(0.0))
+
+
+def spreader():
+    j, k = iota((128, 128), 0), iota((128, 128), 1)
+    return jnp.where(((k & 63) >> 1) == j, F32(1.0), F32(0.0))
+
+
 def dot(a, b):
     return lax.dot_general(
         a, b, (((1,), (0,)), ((), ())), precision=lax.Precision.HIGHEST, preferred_element_type=F32
@@ -71,6 +91,16 @@
 
 def down(v, axis):
     return pltpu.roll(v, 1, axis)
+
+
+def two_next(here, after):
+    low = iota(here.shape, 1) < 64
+    return pltpu.roll(jnp.where(low, after, here), 64, 1)
+
+
+def two_prev(here, before):
+    low = iota(here.shape, 1) < 64
+    return pltpu.roll(jnp.where(low, here, before), 64, 1)
 
 
 def near_sum(vc, vn, carry, wxx, wss, wll):
@@ -95,7 +125,7 @@
     return max(1, 384 // ref.shape[1])
 
 
-def sweep(v, f, op, lo, hi):
+def sweep(v, f, op, lo, hi, two=False):
     wx, ws, wl, di = op
 
     def step(x, n, state):
@@ -104,9 +134,12 @@
         new = []
         for i in range(n):
             wxx = wx[x + i]
-            t = near_sum(vs[i], vs[i + 1], carry, wxx, ws[x + i], wl[x + i])
+            after, before = vs[i + 1], carry
+            carry = wxx * vs[i]
+            if two:
+                after, before = two_next(vs[i], after), two_prev(carry, before)
+            t = near_sum(vs[i], after, before, wxx, ws[x + i], wl[x + i])
             new.append(F32(0.2) * vs[i] + di[x + i] * (f[x + i] + t))
-            carry = wxx * vs[i]
         for i in range(n):
             v[x + i] = new[i]
         return carry, vs[n]
@@ -126,14 +159,17 @@
     blocks(lo, hi, block_of(v), step)
 
 
-def resid_slabs(v, f, op, x, n):
+def resid_slabs(v, f, op, x, n, two=False):
     wx, ws, wl, di = op
     vs = [v[x + i - 1] for i in range(n + 2)]
     wxs = [wx[x + i - 1] for i in range(n + 1)]
     out = []
     for i in range(n):
         vc = vs[i + 1]
-        t = near_sum(vc, vs[i + 2], wxs[i] * vs[i], wxs[i + 1], ws[x + i], wl[x + i])
+        after, before = vs[i + 2], wxs[i] * vs[i]
+        if two:
+            after, before = two_next(vc, after), two_prev(wxs[i + 1] * vc, before)
+        t = near_sum(vc, after, before, wxs[i + 1], ws[x + i], wl[x + i])
         dinv = di[x + i]
         inside = dinv > 0
         diag = jnp.where(inside, F32(0.8) / jnp.where(inside, dinv, F32(1.0)), F32(0.0))
@@ -151,6 +187,16 @@
     blocks(0, n, max(1, block_of(v) // 2), step)
 
 
+def resid_each(v, f, op, lo, n, out):
+    def step(j, m, _):
+        rs = resid_slabs(v, f, op, lo + j, m, True)
+        for i in range(m):
+            out[j + i] = rs[i]
+        return 0
+
+    blocks(0, n, block_of(v), step)
+
+
 def sum_pairs(src, lo, n, out):
     def step(j, m, _):
         new = [src[lo + 2 * (j + i)] + src[lo + 2 * (j + i) + 1] for i in range(m)]
@@ -161,7 +207,7 @@
     blocks(0, n, max(1, block_of(out) // 2), step)
 
 
-def weights(c, cbase, op, lo, hi, lane_last, sub_last, edge=None):
+def weights(c, cbase, op, lo, hi, lane_last, sub_last, edge=None, two=False):
     wx, ws, wl, di = op
     ny, nl = c.shape[1:]
     half, zero = F32(0.5), F32(0.0)
@@ -169,11 +215,17 @@
     def step(x, n, _):
         x = x + cbase
         rows, lanes = iota((ny, nl), 0), iota((ny, nl), 1)
+        last, first = lanes >= lane_last, lanes == 0
+        if two:
+            last, first = (lanes & 63) == 63, (lanes & 63) == 0
         hs = [c[x + i - 1] * half for i in range(n + 2)]
         new = []
         for i in range(n):
             ch = hs[i + 1]
-            cp, cm = ch + hs[i + 2], ch + hs[i]
+            after, before = hs[i + 2], hs[i]
+            if two:
+                after, before = two_next(ch, after), two_prev(ch, before)
+            cp, cm = ch + after, ch + before
             s_next, s_prev = up(ch, 0), down(ch, 0)
             if sub_last:
                 s_next = jnp.where(rows == ny - 1, zero, s_next)
@@ -181,14 +233,14 @@
             if edge is not None:
                 s_next = jnp.where(rows == ny - 1, edge[1, pl.ds(x + i, 1), :] * half, s_next)
                 s_prev = jnp.where(rows == 0, edge[0, pl.ds(x + i, 1), :] * half, s_prev)
-            l_next = jnp.where(lanes >= lane_last, zero, up(ch, 1))
-            l_prev = jnp.where(lanes == 0, zero, down(ch, 1))
+            l_next = jnp.where(last, zero, up(ch, 1))
+            l_prev = jnp.where(first, zero, down(ch, 1))
             s_up, l_up = ch + s_next, ch + l_next
             diag = (cp + cm) + (s_up + (ch + s_prev)) + (l_up + (ch + l_prev))
             inside = ch > 0
             dinv = jnp.where(inside, F32(0.8) / jnp.where(inside, diag, F32(1.0)), zero)
             s_up = jnp.where(rows == ny - 1, zero, s_up) if sub_last else s_up
-            new.append((cp, s_up, jnp.where(lanes >= lane_last, zero, l_up), dinv))
+            new.append((cp, s_up, jnp.where(last, zero, l_up), dinv))
         for i in range(n):
             for ref, value in zip(op, new[i]):
                 ref[x - cbase + i] = value
@@ -246,8 +298,7 @@
 
     blocks(0, 32, 8, step)
     sum_pairs(coef, 0, 16, s)
-    c1 = dot(flat(pair_rows(s, 0, 16) * F32(0.25)), halver(128)).reshape(16, 16, 128)
-    packed[...] = pack_halves(c1)
+    packed[...] = to_level1(pair_rows(s, 0, 16) * F32(0.25))
     to_next[8:17] = coef[23:32]
     to_prev[8:17] = coef[0:9]
     for copy in copies[3:]:
@@ -274,28 +325,22 @@
         out[104, 2:8, :] = jnp.zeros((6, 128), F32)
 
 
-def pack_halves(a):
-    return a[0:8] + pltpu.roll(a[8:16], 64, 2)
-
-
-def unpack(dst, own, left, right, above, below, flags=None):
-    lanes = iota((48, 128), 1)
+def to_level1(pairs):
+    halves = pairs.reshape(8, 2, 16, 128)
+    even, odd = halves[:, 0].reshape(128, 128), halves[:, 1].reshape(128, 128)
+    return (dot(even, halver_at(0)) + dot(odd, halver_at(1))).reshape(8, 16, 128)
+
+
+def assemble(dst, own, left, right, above, below, flags=None):
+    one = F32(1.0)
+    gl, gr, bl, br = flags or (one, one, one, one)
     rows = iota((48, 128), 0)
-    for k in range(3):
-        scale = None
+    for k, side in enumerate((left, None, right)):
         if flags is not None:
-            gl, gr, bl, br = flags
-            one = F32(1.0)
             scale = jnp.where(rows < 16, bl, jnp.where(rows < 32, one, br)) * (gl, one, gr)[k]
         for i in range(8):
-            if k == 1:
-                slab = jnp.concatenate([above[i], own[i], below[i]], 0)
-            else:
-                slab = (left, None, right)[k][i]
-            if scale is not None:
-                slab = slab * scale
-            dst[16 * k + i] = jnp.where(lanes < 64, slab, F32(0.0))
-            dst[16 * k + 8 + i] = jnp.where(lanes < 64, pltpu.roll(slab, 64, 1), F32(0.0))
+            slab = jnp.concatenate([above[i], own[i], below[i]], 0) if side is None else side[i]
+            dst[8 * k + i] = slab if flags is None else slab * scale
 
 
 def edge_flags(ng, nb):
@@ -311,8 +356,7 @@
 
 def fine_restrict(v, f, op, s):
     resid_pairs(v, f, op, 8, 16, s)
-    pairs = pair_rows(s, 8, 16)
-    return dot(flat(pairs), halver(128)).reshape(16, 16, 128)
+    return to_level1(pair_rows(s, 8, 16))
 
 
 def start_kernel(
@@ -340,9 +384,7 @@
     weights(cx, 1, op, 0, 48, 127, False, edge)
     first_sweep(v, fx, op, 0, 48)
     sweep(v, fx, op, 1, 47)
-    f1 = fine_restrict(v, fx, op, s)
-
-    packed[...] = pack_halves(f1)
+    packed[...] = fine_restrict(v, fx, op, s)
 
 
 def fold_rows(send):
@@ -353,11 +395,12 @@
 
 
 def mid_down(f1, v1, op1, f2, v2, op2, s, payload, extra):
-    first_sweep(v1, f1, op1, 2, 46)
-    sweep(v1, f1, op1, 3, 45)
-    resid_pairs(v1, f1, op1, 4, 20, s)
+    v1[0] = v1[23] = jnp.zeros((48, 128), F32)
+    first_sweep(v1, f1, op1, 1, 23)
+    sweep(v1, f1, op1, 1, 23, True)
+    resid_each(v1, f1, op1, 2, 20, s)
     half = halver(128)
-    f2[2:22] = dot(flat(pair_rows(s.at[0:20], 0, 24)), half).reshape(20, 24, 128)
+    f2[2:22] = dot(flat(pair_rows(s.at[0:20], 0, 24)), folder()).reshape(20, 24, 128)
     first_sweep(v2, f2, op2, 2, 22)
     sweep(v2, f2, op2, 3, 21)
     resid_pairs(v2, f2, op2, 8, 4, s.at[0:4, 0:24])
@@ -381,11 +424,11 @@
     ng, nb, cown, cleft, cright, cabove, cbelow,
     wx1, ws1, wl1, di1, wx2, ws2, wl2, di2, coarser, c1, c2, s,
 ):
-    unpack(c1, cown, cleft, cright, cabove, cbelow, edge_flags(ng, nb))
-    weights(c1, 0, (wx1, ws1, wl1, di1), 1, 47, 63, False)
-    sum_pairs(c1, 0, 24, s)
+    assemble(c1, cown, cleft, cright, cabove, cbelow, edge_flags(ng, nb))
+    wx1[0] = jnp.zeros((48, 128), F32)
+    weights(c1, 0, (wx1, ws1, wl1, di1), 1, 23, 127, False, None, True)
     half = halver(128)
-    c2[...] = dot(flat(pair_rows(s, 0, 24) * F32(0.25)), half).reshape(24, 24, 128)
+    c2[...] = dot(flat(pair_rows(c1, 0, 24) * F32(0.25)), folder()).reshape(24, 24, 128)
     weights(c2, 0, (wx2, ws2, wl2, di2), 1, 23, 31, False)
     for x in range(4):
         s[x, 0:24] = c2[8 + 2 * x] + c2[9 + 2 * x]
@@ -397,7 +440,7 @@
     own, left, right, above, below, wx1, ws1, wl1, di1, wx2, ws2, wl2, di2, coarser,
     f1, v1, f2, v2, payload, s,
 ):
-    unpack(f1, own, left, right, above, below)
+    assemble(f1, own, left, right, above, below)
     op1, op2 = (wx1, ws1, wl1, di1), (wx2, ws2, wl2, di2)
     mid_down(f1, v1, op1, f2, v2, op2, s, payload, coarser[...])
 
@@ -406,7 +449,7 @@
     own, left, right, above, below, wx1, ws1, wl1, di1, wx2, ws2, wl2, di2,
     f1, v1, f2, v2, payload, s,
 ):
-    unpack(f1, own, left, right, above, below)
+    assemble(f1, own, left, right, above, below)
     op1, op2 = (wx1, ws1, wl1, di1), (wx2, ws2, wl2, di2)
     mid_down(f1, v1, op1, f2, v2, op2, s, payload, None)
 
@@ -526,16 +569,18 @@
     coarse_to_mid(nb, v3, v2, s2, 4 * nb)
     sweep(v2, f2, op2, 4, 20)
     sweep(v2, f2, op2, 5, 19)
-    twice = doubler(128)
-    e = dot(flat(v2[5:19]), twice).reshape(14, 24, 128)
+    e = dot(flat(v2[5:19]), spreader()).reshape(14, 24, 128)
     es[5:19, pl.ds(0, 24, stride=2), :] = e
     es[5:19, pl.ds(1, 24, stride=2), :] = e
     v1, f1 = v1.at[:, 8:40], f1.at[:, 8:40]
     op1 = tuple(ref.at[:, 8:40] for ref in op1)
-    add_double(v1, es.at[:, 8:40], 10, 38)
-    sweep(v1, f1, op1, 11, 37)
-    sweep(v1, f1, op1, 12, 36)
-    e = dot(flat(v1[12:36, 4:28, :]), twice).reshape(24, 24, 128)
+    for i in range(5, 19):
+        v1[i] = v1[i] + es[i, 8:40]
+    sweep(v1, f1, op1, 5, 19, True)
+    sweep(v1, f1, op1, 6, 18, True)
+    rows = flat(v1[6:18, 4:28, :])
+    e = [dot(rows, doubler_at(h)).reshape(12, 1, 24, 128) for h in (0, 1)]
+    e = jnp.concatenate(e, 1).reshape(24, 24, 128)
     es[:, pl.ds(0, 24, stride=2), :] = e
     es[:, pl.ds(1, 24, stride=2), :] = e
 
@@ -553,8 +598,7 @@
     add_double(v0, scr[-1], 0, 48)
     for lo in (2, 3, 4, 5):
         sweep(v0, f0, op0, lo, 48 - lo)
-    f1n = fine_restrict(v0, f0, op0, s)
-    packed[...] = pack_halves(f1n)
+    packed[...] = fine_restrict(v0, f0, op0, s)
 
 
 def end_kernel(ng, nb, *refs):
@@ -606,7 +650,7 @@
 
 
 def make_body(ng, nb):
-    big, mid, low = (48, 48, 128), (48, 48, 128), (24, 24, 128)
+    big, mid, low = (48, 48, 128), (24, 48, 128), (24, 24, 128)
     n3, nl = 4 * ng, 4 * nb
     nd = ng * nb
     pay, pay2 = (nd, 4, 128), (nd, 2, 128)
@@ -627,14 +671,11 @@
             hbm=(0, 1, 2, 3),
         )
         left, right = ring((to_next, to_prev), "grp", ng)
-        coarse_above, coarse_below, tall = tall_of(cpack, nb)
-        left, right, tall = lax.optimization_barrier((left, right, tall))
         to_next, to_prev = call(rows_kernel, (f, coef, left, right), [(105, 8, 128)] * 2)
         above, below = ring((to_next, to_prev), "box", nb)
+        coarse_above, coarse_below, tall = tall_of(cpack, nb)
+        above, below, tall = lax.optimization_barrier((above, below, tall))
         coarse_left, coarse_right = ring((tall, tall), "grp", ng)
-        above, below, coarse_left, coarse_right = lax.optimization_barrier(
-            (above, below, coarse_left, coarse_right)
-        )
         coarse_coef = (cpack, coarse_left, coarse_right, coarse_above, coarse_below)
         v0, f0, wx0, ws0, wl0, di0, packed = call(
             fix(start_kernel), (f, coef, left, right, above, below), [big] * 6 + [(8, 16, 128)],
@@ -643,7 +684,7 @@
         l0 = (f0, wx0, ws0, wl0, di0)
         *ops, coarser = call(
             fix(mid_weights_kernel), coarse_coef, [mid] * 4 + [low] * 4 + [(4, 128)],
-            scratch=[(48, 48, 128), (24, 24, 128), (24, 48, 128)],
+            scratch=[mid, low, mid],
         )
         f1, v1, f2, v2, payload = call(
             mid_kernel, around(packed, ng, nb) + tuple(ops) + (coarser,),

time: 149 us -> 144 us (0.966)
  starting transfers between devices: 36.6 us -> 27.6 us
  waiting for transfers between devices: 17.4 us -> 23.3 us
  Pallas kernels: 38.1 us -> 33.7 us
  blocking collectives: 56 us -> 58.4 us
    ppermute x8, starting transfers between devices: 31.9 us -> 21.3 us  [ring(): after = lax.ppermute(x[1], axis, [(i, (i - 1) % n) for i in range(n)])]
    ppermute x8, waiting for transfers between devices: 8.94 us -> 17.9 us  [ring(): after = lax.ppermute(x[1], axis, [(i, (i - 1) % n) for i in range(n)])]
    pallas_call x8, Pallas kernels: 38.1 us -> 33.7 us  [call(): pl.pallas_call(kernel, out_shape=[shape_of(i, s) for i, s in enumerate(ou...]
    ppermute x8, waiting for transfers between devices: 8.42 us -> 5.39 us  [ring(): before = lax.ppermute(x[0], axis, [(i, (i + 1) % n) for i in range(n)])]
    all_to_all x2, blocking collectives: 56 us -> 58.4 us  [gather_all(): got = lax.all_to_all(payload, ('grp', 'box'), 0, 0, tiled=True)]
    ppermute x8, starting transfers between devices: 4.71 us -> 6.34 us  [ring(): before = lax.ppermute(x[0], axis, [(i, (i + 1) % n) for i in range(n)])]
  transfers between devices with their start and end apart: 16 -> 16, of which waited for: 7 -> 8; matrix products, arithmetic and copies ran while one was open for 0% -> 0% of each run, Pallas kernels for 2% -> 2%
where the time goes in v5:
time: 144 us
  blocking collectives  58.4 us (41%)
  Pallas kernels  33.7 us (23%)
  starting transfers between devices  27.6 us (19%)
  waiting for transfers between devices  23.3 us (16%)
    all_to_all x2, blocking collectives, gather_all(): got = lax.all_to_all(payload, ('grp', 'box'), 0, 0, tiled=True)  58.4 us
    pallas_call x8, Pallas kernels, call(): pl.pallas_call(kernel, out_shape=[shape_of(i, s) for i, s in enumerate(ou...  33.7 us
    ppermute x8, starting transfers between devices, ring(): after = lax.ppermute(x[1], axis, [(i, (i - 1) % n) for i in range(n)])  21.3 us
    ppermute x8, waiting for transfers between devices, ring(): after = lax.ppermute(x[1], axis, [(i, (i - 1) % n) for i in range(n)])  17.9 us
    ppermute x8, starting transfers between devices, ring(): before = lax.ppermute(x[0], axis, [(i, (i + 1) % n) for i in range(n)])  6.34 us
    ppermute x8, waiting for transfers between devices, ring(): before = lax.ppermute(x[0], axis, [(i, (i + 1) % n) for i in range(n)])  5.39 us
  transfers between devices with their start and end apart: 16, of which 8 were waited for; matrix products, arithmetic and copies ran while one was open for 0% of the time, Pallas kernels for 2%

profile of v5, /device:TPU:1, one launch (start us, length us, event | category | flops | bytes accessed | tf_op | source)
XLA Modules:
  0.0 143.8 jit_solution(16603446746317701171)
XLA Ops:
  0.6 1.9 %shard_map.59 = (f32[32,32,128]{2,1,0:T(8,128)S(1)}, f32[17,32,128]{2,1,0:T(8,128)S(1)}, f32[17,32,128]{2,1,0:T(8,128)S(1)}, f32[8,16,128]{2,1,0:T(8,128)S(1)}) custom-call(f32[32,32,128]{2,1,0:T(8,128)} %refs_0_.1, s32[32,32,128]{2,1,0:T(8,128)} %tags_hbm.1, f32[8]{0:T(128)} %table_hbm.1, f32[32,32,128]{2,1,0:T(8,128)} %rough_hbm.1), custom_call_target="tpu_custom_call" | custom-call | tf_op jit(solution)/shard_map/pallas_call | solution.py:31
  2.6 2.6 %collective-permute-start = (f32[17,32,128]{2,1,0:T(8,128)S(1)}, f32[17,32,128]{2,1,0:T(8,128)S(1)}, u32[]{:S(2)}, u32[]{:S(2)}) collective-permute-start(f32[17,32,128]{2,1,0:T(8,128)S(1)} %get-tuple-element.40), channel_id=1, source_target_pairs={{0,32},{32,64},{64,96},{96,128},{128,160},{160,192},{192,224},{224... | collective-permute-start | bytes 835592 | tf_op jit(solution)/shard_map/ppermute | solution.py:631
  5.2 0.7 collective-permute-start.1
  5.9 2.8 %collective-permute-done.left.refs_2_ = f32[17,32,128]{2,1,0:T(8,128)S(1)} collective-permute-done((f32[17,32,128]{2,1,0:T(8,128)S(1)}, f32[17,32,128]{2,1,0:T(8,128)S(1)}, u32[]{:S(2)}, u32[]{:S(2)}) %collective-permute-start) | collective-permute-done | bytes 278560 | tf_op jit(solution)/shard_map/ppermute | solution.py:631
  8.7 2.8 %collective-permute-done.1.right.refs_3_ = f32[17,32,128]{2,1,0:T(8,128)S(1)} collective-permute-done((f32[17,32,128]{2,1,0:T(8,128)S(1)}, f32[17,32,128]{2,1,0:T(8,128)S(1)}, u32[]{:S(2)}, u32[]{:S(2)}) %collective-permute-start.1) | collective-permute-done | bytes 278560 | tf_op jit(solution)/shard_map/ppermute | solution.py:632
  11.5 0.1 shard_map.60
  11.6 1.4 collective-permute-start.2
  13.0 6.5 %collective-permute-start.3 = (f32[105,8,128]{2,1,0:T(8,128)S(1)}, f32[105,8,128]{2,1,0:T(8,128)S(1)}, u32[]{:S(2)}, u32[]{:S(2)}) collective-permute-start(f32[105,8,128]{2,1,0:T(8,128)S(1)} %get-tuple-element.43), channel_id=1, source_target_pairs={{0,31},{1,0},{2,1},{3,2},{4,3},{5,4},{6,5},{7,6},{8,7},{9,8},{10,9... | collective-permute-start | bytes 1290248 | tf_op jit(solution)/shard_map/ppermute | solution.py:632
  19.5 1.4 collective-permute-start.5
  20.9 9.1 %collective-permute-done.5.refs_4_ = f32[8,16,128]{2,1,0:T(8,128)S(1)} collective-permute-done((f32[8,16,128]{2,1,0:T(8,128)S(1)}, f32[8,16,128]{2,1,0:T(8,128)S(1)}, u32[]{:S(2)}, u32[]{:S(2)}) %collective-permute-start.5) | collective-permute-done | bytes 65568 | tf_op jit(solution)/shard_map/ppermute | solution.py:632
  30.0 0.9 collective-permute-done.4.refs_3_
  31.0 3.9 %shard_map.61 = (f32[48,48,128]{2,1,0:T(8,128)S(1)}, f32[48,48,128]{2,1,0:T(8,128)S(1)}, f32[48,48,128]{2,1,0:T(8,128)S(1)}, f32[48,48,128]{2,1,0:T(8,128)S(1)},...) custom-call(f32[32,32,128]{2,1,0:T(8,128)S(1)} %copy-done, ...), custom_call_target="tpu_custom_call" | custom-call | flops 60000000 | bytes 20000000 | tf_op jit(solution)/shard_map/pallas_call | solution.py:31
  35.0 0.7 collective-permute-start.11
  35.7 1.0 collective-permute-start.10
  36.8 4.8 %collective-permute-start.7 = (f32[8,16,128]{2,1,0:T(8,128)S(1)}, f32[8,16,128]{2,1,0:T(8,128)S(1)}, u32[]{:S(2)}, u32[]{:S(2)}) collective-permute-start(f32[8,16,128]{2,1,0:T(8,128)S(1)} %get-tuple-element.47.own), channel_id=1, source_target_pairs={{0,31},{1,0},{2,1},{3,2},{4,3},{5,4},{6,5},{7,6},{8,7},{9,8},{10,9... | collective-permute-start | bytes 196616 | tf_op jit(solution)/shard_map/ppermute | solution.py:632
  41.6 1.3 collective-permute-done.7.below
  42.9 1.5 %collective-permute-start.9 = (f32[8,48,128]{2,1,0:T(8,128)S(1)}, f32[8,48,128]{2,1,0:T(8,128)S(1)}, u32[]{:S(2)}, u32[]{:S(2)}) collective-permute-start(f32[8,48,128]{2,1,0:T(8,128)S(1)} %constant_dynamic-update-slice_fusion), channel_id=1, source_target_pairs={{0,224},{32,0},{64,32},{96,64},{128,96},{160,128},{192,160},{224,1... | collective-permute-start | bytes 589832 | tf_op jit(solution)/shard_map/ppermute | solution.py:632
  44.3 0.3 collective-permute-start.8
  44.6 2.2 %shard_map.62 = (f32[24,48,128]{2,1,0:T(8,128)S(1)}, f32[24,48,128]{2,1,0:T(8,128)S(1)}, f32[24,48,128]{2,1,0:T(8,128)S(1)}, f32[24,48,128]{2,1,0:T(8,128)S(1)},...) custom-call(f32[8,16,128]{2,1,0:T(8,128)S(1)} %get-tuple-element.44., ...), custom_call_target="tpu_custom_call" | custom-call | tf_op jit(solution)/shard_map/pallas_call | solution.py:31
  46.8 1.1 collective-permute-done.9.right
  48.0 2.9 %shard_map.63 = (f32[24,48,128]{2,1,0:T(8,128)S(1)}, f32[24,48,128]{2,1,0:T(8,128)S(1)}, f32[24,24,128]{2,1,0:T(8,128)S(1)}, f32[24,24,128]{2,1,0:T(8,128)S(1)}, f32[256,4,128]{2,1,0:T(4,128)S(1)}) custom-call(f32[8,16,128]{2,1,0:T(8,128)S(1)} %get-tuple-element.47.own, f32[8,48,128]{2,1,0:T(8,128)S(1)} %collective-permute-done.8.left, ...), custom_call_target="tpu_custom_call" | custom-call | tf_op jit(solution)/shard_map/pallas_call | solution.py:31
  50.9 33.2 %all_to_all.10 = f32[256,4,128]{2,1,0:T(4,128)S(1)} all-to-all(f32[256,4,128]{2,1,0:T(4,128)S(1)} %get-tuple-element.58), channel_id=1, replica_groups=mesh['grp'=8,'box'=32] {'grp','box'}, dimensions={0} | all-to-all | bytes 1048576 | tf_op jit(solution)/shard_map/all_to_all | solution.py:648
  84.1 10.2 %shard_map.64 = (f32[48,48,128]{2,1,0:T(8,128)S(1)}, f32[8,16,128]{2,1,0:T(8,128)S(1)}) custom-call(f32[1024,128]{1,0:T(8,128)S(1)} %bitcast.2, f32[48,48,128]{2,1,0:T(8,128)S(1)} %get-tuple-element.59.refs_1_.refs_2_, f32[48,48,128]{2,1,0:T(8,128)S(1)} %get-tuple-element.60.refs_2_.refs_3_, ...), custom_call_target="tpu_custom_call", output_to_operand_aliasing={{0}: (16, {})} | custom-call | tf_op jit(solution)/shard_map/pallas_call | solution.py:31
  94.3 0.6 collective-permute-start.12
  95.0 4.3 %collective-permute-start.13 = (f32[8,16,128]{2,1,0:T(8,128)S(1)}, f32[8,16,128]{2,1,0:T(8,128)S(1)}, u32[]{:S(2)}, u32[]{:S(2)}) collective-permute-start(f32[8,16,128]{2,1,0:T(8,128)S(1)} %get-tuple-element.69.own), channel_id=1, source_target_pairs={{0,31},{1,0},{2,1},{3,2},{4,3},{5,4},{6,5},{7,6},{8,7},{9,8},{10,9... | collective-permute-start | bytes 196616 | tf_op jit(solution)/shard_map/ppermute | solution.py:632
  99.2 1.6 %collective-permute-done.12.above = f32[8,16,128]{2,1,0:T(8,128)S(1)} collective-permute-done((f32[8,16,128]{2,1,0:T(8,128)S(1)}, f32[8,16,128]{2,1,0:T(8,128)S(1)}, u32[]{:S(2)}, u32[]{:S(2)}) %collective-permute-start.12) | collective-permute-done | bytes 65568 | tf_op jit(solution)/shard_map/ppermute | solution.py:631
  100.9 1.6 %collective-permute-start.15 = (f32[8,48,128]{2,1,0:T(8,128)S(1)}, f32[8,48,128]{2,1,0:T(8,128)S(1)}, u32[]{:S(2)}, u32[]{:S(2)}) collective-permute-start(f32[8,48,128]{2,1,0:T(8,128)S(1)} %constant_dynamic-update-slice_fusion.3), channel_id=1, source_target_pairs={{0,224},{32,0},{64,32},{96,64},{128,96},{160,128},{192,160},{224,1... | collective-permute-start | bytes 589832 | tf_op jit(solution)/shard_map/ppermute | solution.py:632
  102.5 0.2 collective-permute-start.14
  102.7 3.6 %collective-permute-done.15.right = f32[8,48,128]{2,1,0:T(8,128)S(1)} collective-permute-done((f32[8,48,128]{2,1,0:T(8,128)S(1)}, f32[8,48,128]{2,1,0:T(8,128)S(1)}, u32[]{:S(2)}, u32[]{:S(2)}) %collective-permute-start.15) | collective-permute-done | bytes 196640 | tf_op jit(solution)/shard_map/ppermute | solution.py:632
  106.3 2.9 %shard_map.65 = (f32[24,48,128]{2,1,0:T(8,128)S(1)}, f32[24,48,128]{2,1,0:T(8,128)S(1)}, f32[24,24,128]{2,1,0:T(8,128)S(1)}, f32[24,24,128]{2,1,0:T(8,128)S(1)}, f32[256,2,128]{2,1,0:T(2,128)S(1)}) custom-call(f32[8,16,128]{2,1,0:T(8,128)S(1)} %get-tuple-element.69.own, f32[8,48,128]{2,1,0:T(8,128)S(1)} %collective-permute-done.14.left, ...), custom_call_target="tpu_custom_call" | custom-call | tf_op jit(solution)/shard_map/pallas_call | solution.py:31
  109.2 25.1 %all_to_all.11 = f32[256,2,128]{2,1,0:T(2,128)S(1)} all-to-all(f32[256,2,128]{2,1,0:T(2,128)S(1)} %get-tuple-element.70), channel_id=1, replica_groups=mesh['grp'=8,'box'=32] {'grp','box'}, dimensions={0} | all-to-all | bytes 524288 | tf_op jit(solution)/shard_map/all_to_all | solution.py:648
  134.3 9.5 %shard_map.66 = (f32[32,32,128]{2,1,0:T(8,128)}, f32[32,32,128]{2,1,0:T(8,128)}) custom-call(f32[512,128]{1,0:T(8,128)S(1)} %bitcast.4, f32[1024,128]{1,0:T(8,128)S(1)} %bitcast.3, f32[48,48,128]{2,1,0:T(8,128)S(1)} %get-tuple-element.59.refs_1_.refs_2_, f32[48,48,128]{2,1,0:T(8,128)S(1)} %get-tuple-element.60.refs_2_.refs_3_, ...), custom_call_target="tpu_custom_call" | custom-call | tf_op jit(solution)/shard_map/pallas_call | solution.py:31
  (19 shorter events, 0.2 us)
Async XLA Ops:
  0.6 10.8 %copy-start = (f32[32,32,128]{2,1,0:T(8,128)S(1)}, f32[32,32,128]{2,1,0:T(8,128)}, u32[]{:S(2)}) copy-start(f32[32,32,128]{2,1,0:T(8,128)} %refs_0_.1) | copy-start | bytes 1572868
  2.6 6.1 %collective-permute-start = (f32[17,32,128]{2,1,0:T(8,128)S(1)}, f32[17,32,128]{2,1,0:T(8,128)S(1)}, u32[]{:S(2)}, u32[]{:S(2)}) collective-permute-start(f32[17,32,128]{2,1,0:T(8,128)S(1)} %get-tuple-element.40), channel_id=1, source_target_pairs={{0,32},{32,64},{64,96},{96,128},{128,160},{160,192},{192,224},{224... | collective-permute-start | bytes 835592 | tf_op jit(solution)/shard_map/ppermute | solution.py:631
  5.2 6.3 %collective-permute-start.1 = (f32[17,32,128]{2,1,0:T(8,128)S(1)}, f32[17,32,128]{2,1,0:T(8,128)S(1)}, u32[]{:S(2)}, u32[]{:S(2)}) collective-permute-start(f32[17,32,128]{2,1,0:T(8,128)S(1)} %get-tuple-element.41), channel_id=1, source_target_pairs={{0,224},{32,0},{64,32},{96,64},{128,96},{160,128},{192,160},{224,1... | collective-permute-start | bytes 835592 | tf_op jit(solution)/shard_map/ppermute | solution.py:632
  11.6 19.4 %collective-permute-start.2 = (f32[105,8,128]{2,1,0:T(8,128)S(1)}, f32[105,8,128]{2,1,0:T(8,128)S(1)}, u32[]{:S(2)}, u32[]{:S(2)}) collective-permute-start(f32[105,8,128]{2,1,0:T(8,128)S(1)} %get-tuple-element.42), channel_id=1, source_target_pairs={{0,1},{1,2},{2,3},{3,4},{4,5},{5,6},{6,7},{7,8},{8,9},{9,10},{10,1... | collective-permute-start | bytes 1290248 | tf_op jit(solution)/shard_map/ppermute | solution.py:631
  13.0 18.0 %collective-permute-start.3 = (f32[105,8,128]{2,1,0:T(8,128)S(1)}, f32[105,8,128]{2,1,0:T(8,128)S(1)}, u32[]{:S(2)}, u32[]{:S(2)}) collective-permute-start(f32[105,8,128]{2,1,0:T(8,128)S(1)} %get-tuple-element.43), channel_id=1, source_target_pairs={{0,31},{1,0},{2,1},{3,2},{4,3},{5,4},{6,5},{7,6},{8,7},{9,8},{10,9... | collective-permute-start | bytes 1290248 | tf_op jit(solution)/shard_map/ppermute | solution.py:632
  19.5 10.6 %collective-permute-start.5 = (f32[8,16,128]{2,1,0:T(8,128)S(1)}, f32[8,16,128]{2,1,0:T(8,128)S(1)}, u32[]{:S(2)}, u32[]{:S(2)}) collective-permute-start(f32[8,16,128]{2,1,0:T(8,128)S(1)} %get-tuple-element.44.refs_0_), channel_id=1, source_target_pairs={{0,31},{1,0},{2,1},{3,2},{4,3},{5,4},{6,5},{7,6},{8,7},{9,8},{10,9... | collective-permute-start | bytes 196616 | tf_op jit(solution)/shard_map/ppermute | solution.py:632
  20.8 10.1 %collective-permute-start.4 = (f32[8,16,128]{2,1,0:T(8,128)S(1)}, f32[8,16,128]{2,1,0:T(8,128)S(1)}, u32[]{:S(2)}, u32[]{:S(2)}) collective-permute-start(f32[8,16,128]{2,1,0:T(8,128)S(1)} %get-tuple-element.44.refs_0_), channel_id=1, source_target_pairs={{0,1},{1,2},{2,3},{3,4},{4,5},{5,6},{6,7},{7,8},{8,9},{9,10},{10,1... | collective-permute-start | bytes 196616 | tf_op jit(solution)/shard_map/ppermute | solution.py:631
  34.9 6.6 %collective-permute-start.6 = (f32[8,16,128]{2,1,0:T(8,128)S(1)}, f32[8,16,128]{2,1,0:T(8,128)S(1)}, u32[]{:S(2)}, u32[]{:S(2)}) collective-permute-start(f32[8,16,128]{2,1,0:T(8,128)S(1)} %get-tuple-element.47.own), channel_id=1, source_target_pairs={{0,1},{1,2},{2,3},{3,4},{4,5},{5,6},{6,7},{7,8},{8,9},{9,10},{10,1... | collective-permute-start | bytes 196616 | tf_op jit(solution)/shard_map/ppermute | solution.py:631
  35.0 9.6 %collective-permute-start.11 = (f32[8,48,128]{2,1,0:T(8,128)S(1)}, f32[8,48,128]{2,1,0:T(8,128)S(1)}, u32[]{:S(2)}, u32[]{:S(2)}) collective-permute-start(f32[8,48,128]{2,1,0:T(8,128)S(1)} %pad_maximum_fusion), channel_id=1, source_target_pairs={{0,224},{32,0},{64,32},{96,64},{128,96},{160,128},{192,160},{224,1... | collective-permute-start | bytes 589832 | tf_op jit(solution)/shard_map/ppermute | solution.py:632
  35.7 8.9 %collective-permute-start.10 = (f32[8,48,128]{2,1,0:T(8,128)S(1)}, f32[8,48,128]{2,1,0:T(8,128)S(1)}, u32[]{:S(2)}, u32[]{:S(2)}) collective-permute-start(f32[8,48,128]{2,1,0:T(8,128)S(1)} %pad_maximum_fusion), channel_id=1, source_target_pairs={{0,32},{32,64},{64,96},{96,128},{128,160},{160,192},{192,224},{224... | collective-permute-start | bytes 589832 | tf_op jit(solution)/shard_map/ppermute | solution.py:631
  36.8 6.1 %collective-permute-start.7 = (f32[8,16,128]{2,1,0:T(8,128)S(1)}, f32[8,16,128]{2,1,0:T(8,128)S(1)}, u32[]{:S(2)}, u32[]{:S(2)}) collective-permute-start(f32[8,16,128]{2,1,0:T(8,128)S(1)} %get-tuple-element.47.own), channel_id=1, source_target_pairs={{0,31},{1,0},{2,1},{3,2},{4,3},{5,4},{6,5},{7,6},{8,7},{9,8},{10,9... | collective-permute-start | bytes 196616 | tf_op jit(solution)/shard_map/ppermute | solution.py:632
  42.9 5.1 %collective-permute-start.9 = (f32[8,48,128]{2,1,0:T(8,128)S(1)}, f32[8,48,128]{2,1,0:T(8,128)S(1)}, u32[]{:S(2)}, u32[]{:S(2)}) collective-permute-start(f32[8,48,128]{2,1,0:T(8,128)S(1)} %constant_dynamic-update-slice_fusion), channel_id=1, source_target_pairs={{0,224},{32,0},{64,32},{96,64},{128,96},{160,128},{192,160},{224,1... | collective-permute-start | bytes 589832 | tf_op jit(solution)/shard_map/ppermute | solution.py:632
  44.3 3.6 %collective-permute-start.8 = (f32[8,48,128]{2,1,0:T(8,128)S(1)}, f32[8,48,128]{2,1,0:T(8,128)S(1)}, u32[]{:S(2)}, u32[]{:S(2)}) collective-permute-start(f32[8,48,128]{2,1,0:T(8,128)S(1)} %constant_dynamic-update-slice_fusion), channel_id=1, source_target_pairs={{0,32},{32,64},{64,96},{96,128},{128,160},{160,192},{192,224},{224... | collective-permute-start | bytes 589832 | tf_op jit(solution)/shard_map/ppermute | solution.py:631
  94.3 6.5 %collective-permute-start.12 = (f32[8,16,128]{2,1,0:T(8,128)S(1)}, f32[8,16,128]{2,1,0:T(8,128)S(1)}, u32[]{:S(2)}, u32[]{:S(2)}) collective-permute-start(f32[8,16,128]{2,1,0:T(8,128)S(1)} %get-tuple-element.69.own), channel_id=1, source_target_pairs={{0,1},{1,2},{2,3},{3,4},{4,5},{5,6},{6,7},{7,8},{8,9},{9,10},{10,1... | collective-permute-start | bytes 196616 | tf_op jit(solution)/shard_map/ppermute | solution.py:631
  95.0 5.9 %collective-permute-start.13 = (f32[8,16,128]{2,1,0:T(8,128)S(1)}, f32[8,16,128]{2,1,0:T(8,128)S(1)}, u32[]{:S(2)}, u32[]{:S(2)}) collective-permute-start(f32[8,16,128]{2,1,0:T(8,128)S(1)} %get-tuple-element.69.own), channel_id=1, source_target_pairs={{0,31},{1,0},{2,1},{3,2},{4,3},{5,4},{6,5},{7,6},{8,7},{9,8},{10,9... | collective-permute-start | bytes 196616 | tf_op jit(solution)/shard_map/ppermute | solution.py:632
  100.9 5.4 %collective-permute-start.15 = (f32[8,48,128]{2,1,0:T(8,128)S(1)}, f32[8,48,128]{2,1,0:T(8,128)S(1)}, u32[]{:S(2)}, u32[]{:S(2)}) collective-permute-start(f32[8,48,128]{2,1,0:T(8,128)S(1)} %constant_dynamic-update-slice_fusion.3), channel_id=1, source_target_pairs={{0,224},{32,0},{64,32},{96,64},{128,96},{160,128},{192,160},{224,1... | collective-permute-start | bytes 589832 | tf_op jit(solution)/shard_map/ppermute | solution.py:632
  102.5 3.8 %collective-permute-start.14 = (f32[8,48,128]{2,1,0:T(8,128)S(1)}, f32[8,48,128]{2,1,0:T(8,128)S(1)}, u32[]{:S(2)}, u32[]{:S(2)}) collective-permute-start(f32[8,48,128]{2,1,0:T(8,128)S(1)} %constant_dynamic-update-slice_fusion.3), channel_id=1, source_target_pairs={{0,32},{32,64},{64,96},{96,128},{128,160},{160,192},{192,224},{224... | collective-permute-start | bytes 589832 | tf_op jit(solution)/shard_map/ppermute | solution.py:631

commit v6 on v5

--- a/solution.py
+++ b/solution.py
@@ -275,8 +275,8 @@
         (table_hbm, table),
         (tags_hbm, tags),
         (rough_hbm, rough),
-        (f_hbm.at[24:32], to_next.at[0:8]),
-        (f_hbm.at[0:8], to_prev.at[0:8]),
+        (f_hbm.at[:, 24:32], to_next.at[0:32]),
+        (f_hbm.at[:, 0:8], to_prev.at[0:32]),
     )
     copies = [pltpu.make_async_copy(a, b, sems.at[i]) for i, (a, b) in enumerate(pairs)]
     for copy in copies:
@@ -298,31 +298,36 @@
 
     blocks(0, 32, 8, step)
     sum_pairs(coef, 0, 16, s)
-    packed[...] = to_level1(pair_rows(s, 0, 16) * F32(0.25))
-    to_next[8:17] = coef[23:32]
-    to_prev[8:17] = coef[0:9]
+    c1 = to_level1(pair_rows(s, 0, 16) * F32(0.25))
+    packed[...] = c1
+    for out, row, extra in ((to_next, 24, 23), (to_prev, 0, 8)):
+        out[32:64] = coef[:, row : row + 8]
+        for x in range(32):
+            out[64 + x // 8, x % 8 : x % 8 + 1, :] = coef[x, extra : extra + 1, :]
+        out[68:84] = c1.reshape(16, 8, 128)
     for copy in copies[3:]:
         copy.wait()
 
 
-def rows_kernel(f, coef, left, right, to_next, to_prev):
-    for out, row, extra in ((to_next, 24, 23), (to_prev, 0, 8)):
-        sl = slice(row, row + 8)
-        out[0:8] = left[0:8, sl]
-        out[8:40] = f[:, sl]
-        out[40:48] = right[0:8, sl]
-        out[48:57] = left[8:17, sl]
-        out[57:89] = coef[:, sl]
-        out[89:98] = right[8:17, sl]
-        for x in range(50):
-            if x < 9:
-                line = left[8 + x, extra : extra + 1, :]
-            elif x < 41:
-                line = coef[x - 9, extra : extra + 1, :]
-            else:
-                line = right[8 + x - 41, extra : extra + 1, :]
-            out[98 + x // 8, x % 8 : x % 8 + 1, :] = line
-        out[104, 2:8, :] = jnp.zeros((6, 128), F32)
+def slabs_kernel(f, coef, packed, above, below, to_next, to_prev):
+    for out, fs, cs in (
+        (to_next, slice(24, 32), slice(23, 32)),
+        (to_prev, slice(0, 8), slice(0, 9)),
+    ):
+        out[0:8, 8:40] = f[fs]
+        out[8:17, 8:40] = coef[cs]
+        out[17] = jnp.zeros((48, 128), F32)
+        for rows, src, line in ((slice(0, 8), above, 0), (slice(40, 48), below, 16)):
+            out[0:8, rows] = src[fs]
+            out[8:17, rows] = src[32 + cs.start : 32 + cs.stop]
+            out[17, line : line + 9] = flat(src[64:68])[cs]
+        for i in range(8):
+            out[18 + i] = tall_slab(packed, above, below, i)
+
+
+def tall_slab(packed, above, below, i):
+    parts = [above[68 + 2 * i], above[69 + 2 * i], packed[i], below[68 + 2 * i], below[69 + 2 * i]]
+    return jnp.concatenate(parts, 0)
 
 
 def to_level1(pairs):
@@ -331,16 +336,11 @@
     return (dot(even, halver_at(0)) + dot(odd, halver_at(1))).reshape(8, 16, 128)
 
 
-def assemble(dst, own, left, right, above, below, flags=None):
-    one = F32(1.0)
-    gl, gr, bl, br = flags or (one, one, one, one)
-    rows = iota((48, 128), 0)
-    for k, side in enumerate((left, None, right)):
-        if flags is not None:
-            scale = jnp.where(rows < 16, bl, jnp.where(rows < 32, one, br)) * (gl, one, gr)[k]
-        for i in range(8):
-            slab = jnp.concatenate([above[i], own[i], below[i]], 0) if side is None else side[i]
-            dst[8 * k + i] = slab if flags is None else slab * scale
+def assemble(dst, own, left, right, above, below):
+    for i in range(8):
+        dst[i] = left[i]
+        dst[8 + i] = jnp.concatenate([above[i], own[i], below[i]], 0)
+        dst[16 + i] = right[i]
 
 
 def edge_flags(ng, nb):
@@ -363,23 +363,23 @@
     ng, nb, f, coef, left, right, above, below, v, fx, wx, ws, wl, di, packed, cx, edge, s
 ):
     gl, gr, bl, br = edge_flags(ng, nb)
-    fx[0:8, 8:40] = left[0:8]
+    fx[0:8] = left[0:8]
     fx[8:40, 8:40] = f[...]
-    fx[40:48, 8:40] = right[0:8]
-    fx[:, 0:8] = above[0:48]
-    fx[:, 40:48] = below[0:48]
-    cx[0:9, 8:40] = left[8:17] * gl
+    fx[8:40, 0:8] = above[0:32]
+    fx[8:40, 40:48] = below[0:32]
+    fx[40:48] = right[0:8]
+    rows = iota((48, 128), 0)
+    tall = jnp.where(rows < 8, bl, jnp.where(rows < 40, F32(1.0), br))
+    cx[0:9] = left[8:17] * (tall * gl)[None]
     cx[9:41, 8:40] = coef[...]
-    cx[41:50, 8:40] = right[8:17] * gr
-    for rows, src, flag in ((slice(0, 8), above, bl), (slice(40, 48), below, br)):
-        cx[0:9, rows] = src[48:57] * (gl * flag)
-        cx[9:41, rows] = src[57:89] * flag
-        cx[41:50, rows] = src[89:98] * (gr * flag)
+    cx[9:41, 0:8] = above[32:64] * bl
+    cx[9:41, 40:48] = below[32:64] * br
+    cx[41:50] = right[8:17] * (tall * gr)[None]
     for i, (src, flag) in enumerate(((above, bl), (below, br))):
-        lines = flat(src[98:105])
-        x = iota(lines.shape, 0)
-        scale = jnp.where(x < 9, gl * flag, jnp.where(x < 41, flag, gr * flag))
-        edge[i] = lines * scale
+        line = 16 * i
+        edge[i, 0:9] = left[17, line : line + 9] * (gl * flag)
+        edge[i, 9:41] = flat(src[64:68]) * flag
+        edge[i, 41:50] = right[17, line : line + 9] * (gr * flag)
     op = (wx, ws, wl, di)
     weights(cx, 1, op, 0, 48, 127, False, edge)
     first_sweep(v, fx, op, 0, 48)
@@ -421,10 +421,16 @@
 
 
 def mid_weights_kernel(
-    ng, nb, cown, cleft, cright, cabove, cbelow,
+    ng, nb, packed, left, right, above, below,
     wx1, ws1, wl1, di1, wx2, ws2, wl2, di2, coarser, c1, c2, s,
 ):
-    assemble(c1, cown, cleft, cright, cabove, cbelow, edge_flags(ng, nb))
+    gl, gr, bl, br = edge_flags(ng, nb)
+    rows = iota((48, 128), 0)
+    scale = jnp.where(rows < 16, bl, jnp.where(rows < 32, F32(1.0), br))
+    for i in range(8):
+        c1[i] = left[18 + i] * (scale * gl)
+        c1[8 + i] = tall_slab(packed, above, below, i) * scale
+        c1[16 + i] = right[18 + i] * (scale * gr)
     wx1[0] = jnp.zeros((48, 128), F32)
     weights(c1, 0, (wx1, ws1, wl1, di1), 1, 23, 127, False, None, True)
     half = halver(128)
@@ -481,7 +487,9 @@
     wl = jnp.where(lanes >= ny4 - 1, o, l_up)
 
     def total(a):
-        return jnp.sum(jnp.sum(a, axis=0))
+        for axis in range(3):
+            a = jnp.sum(a, axis=axis, keepdims=True)
+        return a
 
     v = None
     r = p = f4
@@ -663,27 +671,25 @@
     def body(f, tags, table, rough):
         coef, to_next, to_prev, cpack = call(
             coef_kernel, (f, tags, table, rough),
-            [(32, 32, 128), (17, 32, 128), (17, 32, 128), (8, 16, 128)],
+            [(32, 32, 128), (84, 8, 128), (84, 8, 128), (8, 16, 128)],
             scratch=[
                 pltpu.VMEM((32, 32, 128), jnp.int32), pltpu.SMEM((8,), F32), (32, 32, 128),
                 (16, 32, 128), pltpu.SemaphoreType.DMA((5,)),
             ],
             hbm=(0, 1, 2, 3),
         )
+        above, below = ring((to_next, to_prev), "box", nb)
+        to_next, to_prev = call(
+            slabs_kernel, (f, coef, cpack, above, below), [(26, 48, 128)] * 2
+        )
         left, right = ring((to_next, to_prev), "grp", ng)
-        to_next, to_prev = call(rows_kernel, (f, coef, left, right), [(105, 8, 128)] * 2)
-        above, below = ring((to_next, to_prev), "box", nb)
-        coarse_above, coarse_below, tall = tall_of(cpack, nb)
-        above, below, tall = lax.optimization_barrier((above, below, tall))
-        coarse_left, coarse_right = ring((tall, tall), "grp", ng)
-        coarse_coef = (cpack, coarse_left, coarse_right, coarse_above, coarse_below)
         v0, f0, wx0, ws0, wl0, di0, packed = call(
             fix(start_kernel), (f, coef, left, right, above, below), [big] * 6 + [(8, 16, 128)],
             scratch=[(50, 48, 128), (2, 56, 128), (16, 48, 128)], touched=20_000_000,
         )
         l0 = (f0, wx0, ws0, wl0, di0)
         *ops, coarser = call(
-            fix(mid_weights_kernel), coarse_coef, [mid] * 4 + [low] * 4 + [(4, 128)],
+            fix(mid_weights_kernel), (cpack, left, right, above, below), [mid] * 4 + [low] * 4 + [(4, 128)],
             scratch=[mid, low, mid],
         )
         f1, v1, f2, v2, payload = call(

time: 144 us -> 142 us (0.986)
  starting transfers between devices: 27.6 us -> 24.8 us
  waiting for transfers between devices: 23.3 us -> 26.1 us
    ppermute x8 -> x6, waiting for transfers between devices: 5.39 us -> 18.8 us  [ring(): before = lax.ppermute(x[0], axis, [(i, (i + 1) % n) for i in range(n)])]
    ppermute x8 -> x6, waiting for transfers between devices: 17.9 us -> 7.24 us  [ring(): after = lax.ppermute(x[1], axis, [(i, (i - 1) % n) for i in range(n)])]
    ppermute x8 -> x6, starting transfers between devices: 21.3 us -> 18.1 us  [ring(): after = lax.ppermute(x[1], axis, [(i, (i - 1) % n) for i in range(n)])]
    ppermute x8 -> x6, starting transfers between devices: 6.34 us -> 6.66 us  [ring(): before = lax.ppermute(x[0], axis, [(i, (i + 1) % n) for i in range(n)])]
  transfers between devices with their start and end apart: 16 -> 12, of which waited for: 8 -> 7; matrix products, arithmetic and copies ran while one was open for 0% -> 0% of each run, Pallas kernels for 2% -> 2%
where the time goes in v6:
time: 142 us
  blocking collectives  57 us (40%)
  Pallas kernels  33 us (23%)
  waiting for transfers between devices  26.1 us (18%)
  starting transfers between devices  24.8 us (17%)
    all_to_all x2, blocking collectives, gather_all(): got = lax.all_to_all(payload, ('grp', 'box'), 0, 0, tiled=True)  57 us
    pallas_call x8, Pallas kernels, call(): pl.pallas_call(kernel, out_shape=[shape_of(i, s) for i, s in enumerate(ou...  33 us
    ppermute x6, waiting for transfers between devices, ring(): before = lax.ppermute(x[0], axis, [(i, (i + 1) % n) for i in range(n)])  18.8 us
    ppermute x6, starting transfers between devices, ring(): after = lax.ppermute(x[1], axis, [(i, (i - 1) % n) for i in range(n)])  18.1 us
    ppermute x6, waiting for transfers between devices, ring(): after = lax.ppermute(x[1], axis, [(i, (i - 1) % n) for i in range(n)])  7.24 us
    ppermute x6, starting transfers between devices, ring(): before = lax.ppermute(x[0], axis, [(i, (i + 1) % n) for i in range(n)])  6.66 us
  transfers between devices with their start and end apart: 12, of which 7 were waited for; matrix products, arithmetic and copies ran while one was open for 0% of the time, Pallas kernels for 2%

profile of v6, /device:TPU:1, one launch (start us, length us, event | category | flops | bytes accessed | tf_op | source)
XLA Modules:
  0.0 141.6 jit_solution(10044974405586382955)
XLA Ops:
  0.6 1.9 %shard_map.59 = (f32[32,32,128]{2,1,0:T(8,128)S(1)}, f32[84,8,128]{2,1,0:T(8,128)S(1)}, f32[84,8,128]{2,1,0:T(8,128)S(1)}, f32[8,16,128]{2,1,0:T(8,128)S(1)}) custom-call(f32[32,32,128]{2,1,0:T(8,128)} %refs_0_.1, s32[32,32,128]{2,1,0:T(8,128)} %tags_hbm.1, f32[8]{0:T(128)} %table_hbm.1, f32[32,32,128]{2,1,0:T(8,128)} %rough_hbm.1), custom_call_target="tpu_custom_call" | custom-call | tf_op jit(solution)/shard_map/pallas_call | solution.py:31
  2.6 2.5 %collective-permute-start = (f32[84,8,128]{2,1,0:T(8,128)S(1)}, f32[84,8,128]{2,1,0:T(8,128)S(1)}, u32[]{:S(2)}, u32[]{:S(2)}) collective-permute-start(f32[84,8,128]{2,1,0:T(8,128)S(1)} %get-tuple-element.38), channel_id=1, source_target_pairs={{0,1},{1,2},{2,3},{3,4},{4,5},{5,6},{6,7},{7,8},{8,9},{9,10},{10,1... | collective-permute-start | bytes 1032200 | tf_op jit(solution)/shard_map/ppermute | solution.py:639
  5.1 6.5 %collective-permute-start.1 = (f32[84,8,128]{2,1,0:T(8,128)S(1)}, f32[84,8,128]{2,1,0:T(8,128)S(1)}, u32[]{:S(2)}, u32[]{:S(2)}) collective-permute-start(f32[84,8,128]{2,1,0:T(8,128)S(1)} %get-tuple-element.39), channel_id=1, source_target_pairs={{0,31},{1,0},{2,1},{3,2},{4,3},{5,4},{6,5},{7,6},{8,7},{9,8},{10,9... | collective-permute-start | bytes 1032200 | tf_op jit(solution)/shard_map/ppermute | solution.py:640
  11.6 7.7 %collective-permute-done.above.refs_4_.refs_3_ = f32[84,8,128]{2,1,0:T(8,128)S(1)} collective-permute-done((f32[84,8,128]{2,1,0:T(8,128)S(1)}, f32[84,8,128]{2,1,0:T(8,128)S(1)}, u32[]{:S(2)}, u32[]{:S(2)}) %collective-permute-start) | collective-permute-done | bytes 344096 | tf_op jit(solution)/shard_map/ppermute | solution.py:639
  19.3 0.0 collective-permute-done.1.below.refs_5_.refs_4_
  19.3 0.1 shard_map.60
  19.4 2.3 %collective-permute-start.2 = (f32[26,48,128]{2,1,0:T(8,128)S(1)}, f32[26,48,128]{2,1,0:T(8,128)S(1)}, u32[]{:S(2)}, u32[]{:S(2)}) collective-permute-start(f32[26,48,128]{2,1,0:T(8,128)S(1)} %get-tuple-element.40), channel_id=1, source_target_pairs={{0,32},{32,64},{64,96},{96,128},{128,160},{160,192},{192,224},{224... | collective-permute-start | bytes 1916936 | tf_op jit(solution)/shard_map/ppermute | solution.py:639
  21.7 0.0 collective-permute-start.3
  21.7 7.4 %collective-permute-done.2.refs_2_.refs_1_ = f32[26,48,128]{2,1,0:T(8,128)S(1)} collective-permute-done((f32[26,48,128]{2,1,0:T(8,128)S(1)}, f32[26,48,128]{2,1,0:T(8,128)S(1)}, u32[]{:S(2)}, u32[]{:S(2)}) %collective-permute-start.2) | collective-permute-done | bytes 639008 | tf_op jit(solution)/shard_map/ppermute | solution.py:639
  29.1 2.5 %collective-permute-done.3.refs_3_.refs_2_ = f32[26,48,128]{2,1,0:T(8,128)S(1)} collective-permute-done((f32[26,48,128]{2,1,0:T(8,128)S(1)}, f32[26,48,128]{2,1,0:T(8,128)S(1)}, u32[]{:S(2)}, u32[]{:S(2)}) %collective-permute-start.3) | collective-permute-done | bytes 639008 | tf_op jit(solution)/shard_map/ppermute | solution.py:640
  31.6 3.9 %shard_map.61 = (f32[48,48,128]{2,1,0:T(8,128)S(1)}, f32[48,48,128]{2,1,0:T(8,128)S(1)}, f32[48,48,128]{2,1,0:T(8,128)S(1)}, f32[48,48,128]{2,1,0:T(8,128)S(1)},...) custom-call(f32[32,32,128]{2,1,0:T(8,128)S(1)} %copy-done, ...), custom_call_target="tpu_custom_call" | custom-call | flops 60000000 | bytes 20000000 | tf_op jit(solution)/shard_map/pallas_call | solution.py:31
  35.5 0.1 collective-permute-start.4
  35.6 4.9 %collective-permute-start.5 = (f32[8,16,128]{2,1,0:T(8,128)S(1)}, f32[8,16,128]{2,1,0:T(8,128)S(1)}, u32[]{:S(2)}, u32[]{:S(2)}) collective-permute-start(f32[8,16,128]{2,1,0:T(8,128)S(1)} %get-tuple-element.42.own), channel_id=1, source_target_pairs={{0,31},{1,0},{2,1},{3,2},{4,3},{5,4},{6,5},{7,6},{8,7},{9,8},{10,9... | collective-permute-start | bytes 196616 | tf_op jit(solution)/shard_map/ppermute | solution.py:640
  40.5 2.1 %collective-permute-done.4.above = f32[8,16,128]{2,1,0:T(8,128)S(1)} collective-permute-done((f32[8,16,128]{2,1,0:T(8,128)S(1)}, f32[8,16,128]{2,1,0:T(8,128)S(1)}, u32[]{:S(2)}, u32[]{:S(2)}) %collective-permute-start.4) | collective-permute-done | bytes 65568 | tf_op jit(solution)/shard_map/ppermute | solution.py:639
  42.6 0.0 collective-permute-done.5.below
  42.7 0.9 collective-permute-start.7
  43.5 0.9 collective-permute-start.6
  44.4 2.2 %shard_map.62 = (f32[24,48,128]{2,1,0:T(8,128)S(1)}, f32[24,48,128]{2,1,0:T(8,128)S(1)}, f32[24,48,128]{2,1,0:T(8,128)S(1)}, f32[24,48,128]{2,1,0:T(8,128)S(1)},...) custom-call(f32[8,16,128]{2,1,0:T(8,128)S(1)} %get-tuple-element.37., ...), custom_call_target="tpu_custom_call" | custom-call | tf_op jit(solution)/shard_map/pallas_call | solution.py:31
  46.7 1.1 collective-permute-done.7.right
  47.8 0.0 collective-permute-done.6.left
  47.8 2.9 %shard_map.63 = (f32[24,48,128]{2,1,0:T(8,128)S(1)}, f32[24,48,128]{2,1,0:T(8,128)S(1)}, f32[24,24,128]{2,1,0:T(8,128)S(1)}, f32[24,24,128]{2,1,0:T(8,128)S(1)}, f32[256,4,128]{2,1,0:T(4,128)S(1)}) custom-call(f32[8,16,128]{2,1,0:T(8,128)S(1)} %get-tuple-element.42.own, f32[8,48,128]{2,1,0:T(8,128)S(1)} %collective-permute-done.6.left, ...), custom_call_target="tpu_custom_call" | custom-call | tf_op jit(solution)/shard_map/pallas_call | solution.py:31
  50.7 31.9 %all_to_all.10 = f32[256,4,128]{2,1,0:T(4,128)S(1)} all-to-all(f32[256,4,128]{2,1,0:T(4,128)S(1)} %get-tuple-element.52), channel_id=1, replica_groups=mesh['grp'=8,'box'=32] {'grp','box'}, dimensions={0} | all-to-all | bytes 1048576 | tf_op jit(solution)/shard_map/all_to_all | solution.py:656
  82.6 9.9 %shard_map.64 = (f32[48,48,128]{2,1,0:T(8,128)S(1)}, f32[8,16,128]{2,1,0:T(8,128)S(1)}) custom-call(f32[1024,128]{1,0:T(8,128)S(1)} %bitcast.2, f32[48,48,128]{2,1,0:T(8,128)S(1)} %get-tuple-element.53.refs_1_.refs_2_, f32[48,48,128]{2,1,0:T(8,128)S(1)} %get-tuple-element.54.refs_2_.refs_3_, ...), custom_call_target="tpu_custom_call", output_to_operand_aliasing={{0}: (16, {})} | custom-call | tf_op jit(solution)/shard_map/pallas_call | solution.py:31
  92.5 0.6 collective-permute-start.8
  93.1 4.3 %collective-permute-start.9 = (f32[8,16,128]{2,1,0:T(8,128)S(1)}, f32[8,16,128]{2,1,0:T(8,128)S(1)}, u32[]{:S(2)}, u32[]{:S(2)}) collective-permute-start(f32[8,16,128]{2,1,0:T(8,128)S(1)} %get-tuple-element.63.own), channel_id=1, source_target_pairs={{0,31},{1,0},{2,1},{3,2},{4,3},{5,4},{6,5},{7,6},{8,7},{9,8},{10,9... | collective-permute-start | bytes 196616 | tf_op jit(solution)/shard_map/ppermute | solution.py:640
  97.4 1.6 %collective-permute-done.8.above = f32[8,16,128]{2,1,0:T(8,128)S(1)} collective-permute-done((f32[8,16,128]{2,1,0:T(8,128)S(1)}, f32[8,16,128]{2,1,0:T(8,128)S(1)}, u32[]{:S(2)}, u32[]{:S(2)}) %collective-permute-start.8) | collective-permute-done | bytes 65568 | tf_op jit(solution)/shard_map/ppermute | solution.py:639
  99.0 1.6 %collective-permute-start.11 = (f32[8,48,128]{2,1,0:T(8,128)S(1)}, f32[8,48,128]{2,1,0:T(8,128)S(1)}, u32[]{:S(2)}, u32[]{:S(2)}) collective-permute-start(f32[8,48,128]{2,1,0:T(8,128)S(1)} %constant_dynamic-update-slice_fusion.3), channel_id=1, source_target_pairs={{0,224},{32,0},{64,32},{96,64},{128,96},{160,128},{192,160},{224,1... | collective-permute-start | bytes 589832 | tf_op jit(solution)/shard_map/ppermute | solution.py:640
  100.6 0.2 collective-permute-start.10
  100.8 3.6 %collective-permute-done.11.right = f32[8,48,128]{2,1,0:T(8,128)S(1)} collective-permute-done((f32[8,48,128]{2,1,0:T(8,128)S(1)}, f32[8,48,128]{2,1,0:T(8,128)S(1)}, u32[]{:S(2)}, u32[]{:S(2)}) %collective-permute-start.11) | collective-permute-done | bytes 196640 | tf_op jit(solution)/shard_map/ppermute | solution.py:640
  104.4 2.9 %shard_map.65 = (f32[24,48,128]{2,1,0:T(8,128)S(1)}, f32[24,48,128]{2,1,0:T(8,128)S(1)}, f32[24,24,128]{2,1,0:T(8,128)S(1)}, f32[24,24,128]{2,1,0:T(8,128)S(1)}, f32[256,2,128]{2,1,0:T(2,128)S(1)}) custom-call(f32[8,16,128]{2,1,0:T(8,128)S(1)} %get-tuple-element.63.own, f32[8,48,128]{2,1,0:T(8,128)S(1)} %collective-permute-done.10.left, ...), custom_call_target="tpu_custom_call" | custom-call | tf_op jit(solution)/shard_map/pallas_call | solution.py:31
  107.3 25.1 %all_to_all.11 = f32[256,2,128]{2,1,0:T(2,128)S(1)} all-to-all(f32[256,2,128]{2,1,0:T(2,128)S(1)} %get-tuple-element.64), channel_id=1, replica_groups=mesh['grp'=8,'box'=32] {'grp','box'}, dimensions={0} | all-to-all | bytes 524288 | tf_op jit(solution)/shard_map/all_to_all | solution.py:656
  132.5 9.1 %shard_map.66 = (f32[32,32,128]{2,1,0:T(8,128)}, f32[32,32,128]{2,1,0:T(8,128)}) custom-call(f32[512,128]{1,0:T(8,128)S(1)} %bitcast.4, f32[1024,128]{1,0:T(8,128)S(1)} %bitcast.3, f32[48,48,128]{2,1,0:T(8,128)S(1)} %get-tuple-element.53.refs_1_.refs_2_, f32[48,48,128]{2,1,0:T(8,128)S(1)} %get-tuple-element.54.refs_2_.refs_3_, ...), custom_call_target="tpu_custom_call" | custom-call | tf_op jit(solution)/shard_map/pallas_call | solution.py:31
  (10 shorter events, 0.0 us)
Async XLA Ops:
  0.6 18.7 %copy-start = (f32[32,32,128]{2,1,0:T(8,128)S(1)}, f32[32,32,128]{2,1,0:T(8,128)}, u32[]{:S(2)}) copy-start(f32[32,32,128]{2,1,0:T(8,128)} %refs_0_.1) | copy-start | bytes 1572868
  2.6 16.7 %collective-permute-start = (f32[84,8,128]{2,1,0:T(8,128)S(1)}, f32[84,8,128]{2,1,0:T(8,128)S(1)}, u32[]{:S(2)}, u32[]{:S(2)}) collective-permute-start(f32[84,8,128]{2,1,0:T(8,128)S(1)} %get-tuple-element.38), channel_id=1, source_target_pairs={{0,1},{1,2},{2,3},{3,4},{4,5},{5,6},{6,7},{7,8},{8,9},{9,10},{10,1... | collective-permute-start | bytes 1032200 | tf_op jit(solution)/shard_map/ppermute | solution.py:639
  5.1 14.2 %collective-permute-start.1 = (f32[84,8,128]{2,1,0:T(8,128)S(1)}, f32[84,8,128]{2,1,0:T(8,128)S(1)}, u32[]{:S(2)}, u32[]{:S(2)}) collective-permute-start(f32[84,8,128]{2,1,0:T(8,128)S(1)} %get-tuple-element.39), channel_id=1, source_target_pairs={{0,31},{1,0},{2,1},{3,2},{4,3},{5,4},{6,5},{7,6},{8,7},{9,8},{10,9... | collective-permute-start | bytes 1032200 | tf_op jit(solution)/shard_map/ppermute | solution.py:640
  19.4 9.7 %collective-permute-start.2 = (f32[26,48,128]{2,1,0:T(8,128)S(1)}, f32[26,48,128]{2,1,0:T(8,128)S(1)}, u32[]{:S(2)}, u32[]{:S(2)}) collective-permute-start(f32[26,48,128]{2,1,0:T(8,128)S(1)} %get-tuple-element.40), channel_id=1, source_target_pairs={{0,32},{32,64},{64,96},{96,128},{128,160},{160,192},{192,224},{224... | collective-permute-start | bytes 1916936 | tf_op jit(solution)/shard_map/ppermute | solution.py:639
  21.7 9.8 %collective-permute-start.3 = (f32[26,48,128]{2,1,0:T(8,128)S(1)}, f32[26,48,128]{2,1,0:T(8,128)S(1)}, u32[]{:S(2)}, u32[]{:S(2)}) collective-permute-start(f32[26,48,128]{2,1,0:T(8,128)S(1)} %get-tuple-element.41), channel_id=1, source_target_pairs={{0,224},{32,0},{64,32},{96,64},{128,96},{160,128},{192,160},{224,1... | collective-permute-start | bytes 1916936 | tf_op jit(solution)/shard_map/ppermute | solution.py:640
  35.5 7.1 %collective-permute-start.4 = (f32[8,16,128]{2,1,0:T(8,128)S(1)}, f32[8,16,128]{2,1,0:T(8,128)S(1)}, u32[]{:S(2)}, u32[]{:S(2)}) collective-permute-start(f32[8,16,128]{2,1,0:T(8,128)S(1)} %get-tuple-element.42.own), channel_id=1, source_target_pairs={{0,1},{1,2},{2,3},{3,4},{4,5},{5,6},{6,7},{7,8},{8,9},{9,10},{10,1... | collective-permute-start | bytes 196616 | tf_op jit(solution)/shard_map/ppermute | solution.py:639
  35.6 7.1 %collective-permute-start.5 = (f32[8,16,128]{2,1,0:T(8,128)S(1)}, f32[8,16,128]{2,1,0:T(8,128)S(1)}, u32[]{:S(2)}, u32[]{:S(2)}) collective-permute-start(f32[8,16,128]{2,1,0:T(8,128)S(1)} %get-tuple-element.42.own), channel_id=1, source_target_pairs={{0,31},{1,0},{2,1},{3,2},{4,3},{5,4},{6,5},{7,6},{8,7},{9,8},{10,9... | collective-permute-start | bytes 196616 | tf_op jit(solution)/shard_map/ppermute | solution.py:640
  42.7 5.1 %collective-permute-start.7 = (f32[8,48,128]{2,1,0:T(8,128)S(1)}, f32[8,48,128]{2,1,0:T(8,128)S(1)}, u32[]{:S(2)}, u32[]{:S(2)}) collective-permute-start(f32[8,48,128]{2,1,0:T(8,128)S(1)} %constant_dynamic-update-slice_fusion), channel_id=1, source_target_pairs={{0,224},{32,0},{64,32},{96,64},{128,96},{160,128},{192,160},{224,1... | collective-permute-start | bytes 589832 | tf_op jit(solution)/shard_map/ppermute | solution.py:640
  43.5 4.2 %collective-permute-start.6 = (f32[8,48,128]{2,1,0:T(8,128)S(1)}, f32[8,48,128]{2,1,0:T(8,128)S(1)}, u32[]{:S(2)}, u32[]{:S(2)}) collective-permute-start(f32[8,48,128]{2,1,0:T(8,128)S(1)} %constant_dynamic-update-slice_fusion), channel_id=1, source_target_pairs={{0,32},{32,64},{64,96},{96,128},{128,160},{160,192},{192,224},{224... | collective-permute-start | bytes 589832 | tf_op jit(solution)/shard_map/ppermute | solution.py:639
  92.5 6.5 %collective-permute-start.8 = (f32[8,16,128]{2,1,0:T(8,128)S(1)}, f32[8,16,128]{2,1,0:T(8,128)S(1)}, u32[]{:S(2)}, u32[]{:S(2)}) collective-permute-start(f32[8,16,128]{2,1,0:T(8,128)S(1)} %get-tuple-element.63.own), channel_id=1, source_target_pairs={{0,1},{1,2},{2,3},{3,4},{4,5},{5,6},{6,7},{7,8},{8,9},{9,10},{10,1... | collective-permute-start | bytes 196616 | tf_op jit(solution)/shard_map/ppermute | solution.py:639
  93.1 5.9 %collective-permute-start.9 = (f32[8,16,128]{2,1,0:T(8,128)S(1)}, f32[8,16,128]{2,1,0:T(8,128)S(1)}, u32[]{:S(2)}, u32[]{:S(2)}) collective-permute-start(f32[8,16,128]{2,1,0:T(8,128)S(1)} %get-tuple-element.63.own), channel_id=1, source_target_pairs={{0,31},{1,0},{2,1},{3,2},{4,3},{5,4},{6,5},{7,6},{8,7},{9,8},{10,9... | collective-permute-start | bytes 196616 | tf_op jit(solution)/shard_map/ppermute | solution.py:640
  99.0 5.4 %collective-permute-start.11 = (f32[8,48,128]{2,1,0:T(8,128)S(1)}, f32[8,48,128]{2,1,0:T(8,128)S(1)}, u32[]{:S(2)}, u32[]{:S(2)}) collective-permute-start(f32[8,48,128]{2,1,0:T(8,128)S(1)} %constant_dynamic-update-slice_fusion.3), channel_id=1, source_target_pairs={{0,224},{32,0},{64,32},{96,64},{128,96},{160,128},{192,160},{224,1... | collective-permute-start | bytes 589832 | tf_op jit(solution)/shard_map/ppermute | solution.py:640
  100.6 3.8 %collective-permute-start.10 = (f32[8,48,128]{2,1,0:T(8,128)S(1)}, f32[8,48,128]{2,1,0:T(8,128)S(1)}, u32[]{:S(2)}, u32[]{:S(2)}) collective-permute-start(f32[8,48,128]{2,1,0:T(8,128)S(1)} %constant_dynamic-update-slice_fusion.3), channel_id=1, source_target_pairs={{0,32},{32,64},{64,96},{96,128},{128,160},{160,192},{192,224},{224... | collective-permute-start | bytes 589832 | tf_op jit(solution)/shard_map/ppermute | solution.py:639

commit v7 on v6

--- a/solution.py
+++ b/solution.py
@@ -268,7 +268,7 @@
 
 
 def coef_kernel(
-    f_hbm, tags_hbm, table_hbm, rough_hbm, coef, to_next, to_prev, packed,
+    f_hbm, tags_hbm, table_hbm, rough_hbm, coef, to_next, to_prev, x_next, x_prev, packed,
     tags, table, rough, s, sems,
 ):
     pairs = (
@@ -277,6 +277,8 @@
         (rough_hbm, rough),
         (f_hbm.at[:, 24:32], to_next.at[0:32]),
         (f_hbm.at[:, 0:8], to_prev.at[0:32]),
+        (f_hbm.at[24:32], x_next.at[0:8]),
+        (f_hbm.at[0:8], x_prev.at[0:8]),
     )
     copies = [pltpu.make_async_copy(a, b, sems.at[i]) for i, (a, b) in enumerate(pairs)]
     for copy in copies:
@@ -305,29 +307,25 @@
         for x in range(32):
             out[64 + x // 8, x % 8 : x % 8 + 1, :] = coef[x, extra : extra + 1, :]
         out[68:84] = c1.reshape(16, 8, 128)
+    for out, first in ((x_next, 23), (x_prev, 0)):
+        out[8:17] = coef[first : first + 9]
+        out[17:21] = c1.reshape(4, 32, 128)
     for copy in copies[3:]:
         copy.wait()
 
 
-def slabs_kernel(f, coef, packed, above, below, to_next, to_prev):
+def corners_kernel(above, below, to_next, to_prev):
     for out, fs, cs in (
         (to_next, slice(24, 32), slice(23, 32)),
         (to_prev, slice(0, 8), slice(0, 9)),
     ):
-        out[0:8, 8:40] = f[fs]
-        out[8:17, 8:40] = coef[cs]
-        out[17] = jnp.zeros((48, 128), F32)
-        for rows, src, line in ((slice(0, 8), above, 0), (slice(40, 48), below, 16)):
+        for i, src in enumerate((above, below)):
+            rows = slice(8 * i, 8 * i + 8)
             out[0:8, rows] = src[fs]
             out[8:17, rows] = src[32 + cs.start : 32 + cs.stop]
-            out[17, line : line + 9] = flat(src[64:68])[cs]
-        for i in range(8):
-            out[18 + i] = tall_slab(packed, above, below, i)
-
-
-def tall_slab(packed, above, below, i):
-    parts = [above[68 + 2 * i], above[69 + 2 * i], packed[i], below[68 + 2 * i], below[69 + 2 * i]]
-    return jnp.concatenate(parts, 0)
+            out[17 + i] = jnp.zeros((16, 128), F32)
+            out[17 + i, 0:9] = flat(src[64:68])[cs]
+            out[19 + 8 * i : 27 + 8 * i] = src[68:84].reshape(8, 16, 128)
 
 
 def to_level1(pairs):
@@ -360,26 +358,27 @@
 
 
 def start_kernel(
-    ng, nb, f, coef, left, right, above, below, v, fx, wx, ws, wl, di, packed, cx, edge, s
+    ng, nb, f, coef, left, right, above, below, cleft, cright, v, fx, wx, ws, wl, di, packed, cx, edge, s
 ):
     gl, gr, bl, br = edge_flags(ng, nb)
-    fx[0:8] = left[0:8]
     fx[8:40, 8:40] = f[...]
     fx[8:40, 0:8] = above[0:32]
     fx[8:40, 40:48] = below[0:32]
-    fx[40:48] = right[0:8]
-    rows = iota((48, 128), 0)
-    tall = jnp.where(rows < 8, bl, jnp.where(rows < 40, F32(1.0), br))
-    cx[0:9] = left[8:17] * (tall * gl)[None]
     cx[9:41, 8:40] = coef[...]
     cx[9:41, 0:8] = above[32:64] * bl
     cx[9:41, 40:48] = below[32:64] * br
-    cx[41:50] = right[8:17] * (tall * gr)[None]
-    for i, (src, flag) in enumerate(((above, bl), (below, br))):
-        line = 16 * i
-        edge[i, 0:9] = left[17, line : line + 9] * (gl * flag)
-        edge[i, 9:41] = flat(src[64:68]) * flag
-        edge[i, 41:50] = right[17, line : line + 9] * (gr * flag)
+    for x, side, corner, flag in ((0, left, cleft, gl), (40, right, cright, gr)):
+        fx[x : x + 8, 8:40] = side[0:8]
+        fx[x : x + 8, 0:8] = corner[0:8, 0:8]
+        fx[x : x + 8, 40:48] = corner[0:8, 8:16]
+        x = 41 if x else 0
+        cx[x : x + 9, 8:40] = side[8:17] * flag
+        cx[x : x + 9, 0:8] = corner[8:17, 0:8] * (flag * bl)
+        cx[x : x + 9, 40:48] = corner[8:17, 8:16] * (flag * br)
+        edge[0, x : x + 9] = corner[17, 0:9] * (flag * bl)
+        edge[1, x : x + 9] = corner[18, 0:9] * (flag * br)
+    edge[0, 9:41] = flat(above[64:68]) * bl
+    edge[1, 9:41] = flat(below[64:68]) * br
     op = (wx, ws, wl, di)
     weights(cx, 1, op, 0, 48, 127, False, edge)
     first_sweep(v, fx, op, 0, 48)
@@ -421,16 +420,20 @@
 
 
 def mid_weights_kernel(
-    ng, nb, packed, left, right, above, below,
+    ng, nb, packed, left, right, above, below, cleft, cright,
     wx1, ws1, wl1, di1, wx2, ws2, wl2, di2, coarser, c1, c2, s,
 ):
     gl, gr, bl, br = edge_flags(ng, nb)
     rows = iota((48, 128), 0)
     scale = jnp.where(rows < 16, bl, jnp.where(rows < 32, F32(1.0), br))
     for i in range(8):
-        c1[i] = left[18 + i] * (scale * gl)
-        c1[8 + i] = tall_slab(packed, above, below, i) * scale
-        c1[16 + i] = right[18 + i] * (scale * gr)
+        parts = [above[68 + 2 * i], above[69 + 2 * i], packed[i]]
+        parts += [below[68 + 2 * i], below[69 + 2 * i]]
+        c1[8 + i] = jnp.concatenate(parts, 0) * scale
+        own = slice(16 * (i % 2), 16 * (i % 2) + 16)
+        for at, side, corner, flag in ((0, left, cleft, gl), (16, right, cright, gr)):
+            parts = [corner[19 + i], side[17 + i // 2, own], corner[27 + i]]
+            c1[at + i] = jnp.concatenate(parts, 0) * (scale * flag)
     wx1[0] = jnp.zeros((48, 128), F32)
     weights(c1, 0, (wx1, ws1, wl1, di1), 1, 23, 127, False, None, True)
     half = halver(128)
@@ -669,27 +672,26 @@
         return lambda *refs: kernel(ng, nb, *refs)
 
     def body(f, tags, table, rough):
-        coef, to_next, to_prev, cpack = call(
+        coef, to_next, to_prev, x_next, x_prev, cpack = call(
             coef_kernel, (f, tags, table, rough),
-            [(32, 32, 128), (84, 8, 128), (84, 8, 128), (8, 16, 128)],
+            [(32, 32, 128)] + [(84, 8, 128)] * 2 + [(21, 32, 128)] * 2 + [(8, 16, 128)],
             scratch=[
                 pltpu.VMEM((32, 32, 128), jnp.int32), pltpu.SMEM((8,), F32), (32, 32, 128),
-                (16, 32, 128), pltpu.SemaphoreType.DMA((5,)),
+                (16, 32, 128), pltpu.SemaphoreType.DMA((7,)),
             ],
             hbm=(0, 1, 2, 3),
         )
         above, below = ring((to_next, to_prev), "box", nb)
-        to_next, to_prev = call(
-            slabs_kernel, (f, coef, cpack, above, below), [(26, 48, 128)] * 2
-        )
-        left, right = ring((to_next, to_prev), "grp", ng)
+        left, right = ring((x_next, x_prev), "grp", ng)
+        corners = call(corners_kernel, (above, below), [(35, 16, 128)] * 2)
+        halo = (left, right, above, below) + ring(corners, "grp", ng)
         v0, f0, wx0, ws0, wl0, di0, packed = call(
-            fix(start_kernel), (f, coef, left, right, above, below), [big] * 6 + [(8, 16, 128)],
+            fix(start_kernel), (f, coef) + halo, [big] * 6 + [(8, 16, 128)],
             scratch=[(50, 48, 128), (2, 56, 128), (16, 48, 128)], touched=20_000_000,
         )
         l0 = (f0, wx0, ws0, wl0, di0)
         *ops, coarser = call(
-            fix(mid_weights_kernel), (cpack, left, right, above, below), [mid] * 4 + [low] * 4 + [(4, 128)],
+            fix(mid_weights_kernel), (cpack,) + halo, [mid] * 4 + [low] * 4 + [(4, 128)],
             scratch=[mid, low, mid],
         )
         f1, v1, f2, v2, payload = call(

time: 142 us -> 138 us (0.972)
  waiting for transfers between devices: 26.1 us -> 20.2 us
  starting transfers between devices: 24.8 us -> 26.8 us
    ppermute x6 -> x7, waiting for transfers between devices: 18.8 us -> 13 us  [ring(): before = lax.ppermute(x[0], axis, [(i, (i + 1) % n) for i in range(n)])]
    ppermute x6 -> x7, starting transfers between devices: 6.66 us -> 8.72 us  [ring(): before = lax.ppermute(x[0], axis, [(i, (i + 1) % n) for i in range(n)])]
    ppermute x6 -> x7, waiting for transfers between devices: 7.24 us -> 7.24 us  [ring(): after = lax.ppermute(x[1], axis, [(i, (i - 1) % n) for i in range(n)])]
    ppermute x6 -> x7, starting transfers between devices: 18.1 us -> 18.1 us  [ring(): after = lax.ppermute(x[1], axis, [(i, (i - 1) % n) for i in range(n)])]
  transfers between devices with their start and end apart: 12 -> 14, of which waited for: 7 -> 7; matrix products, arithmetic and copies ran while one was open for 0% -> 0% of each run, Pallas kernels for 2% -> 2%
where the time goes in v7:
time: 138 us
  blocking collectives  57 us (41%)
  Pallas kernels  32.9 us (24%)
  starting transfers between devices  26.8 us (19%)
  waiting for transfers between devices  20.2 us (15%)
    all_to_all x2, blocking collectives, gather_all(): got = lax.all_to_all(payload, ('grp', 'box'), 0, 0, tiled=True)  57 us
    pallas_call x8, Pallas kernels, call(): pl.pallas_call(kernel, out_shape=[shape_of(i, s) for i, s in enumerate(ou...  32.9 us
    ppermute x7, starting transfers between devices, ring(): after = lax.ppermute(x[1], axis, [(i, (i - 1) % n) for i in range(n)])  18.1 us
    ppermute x7, waiting for transfers between devices, ring(): before = lax.ppermute(x[0], axis, [(i, (i + 1) % n) for i in range(n)])  13 us
    ppermute x7, starting transfers between devices, ring(): before = lax.ppermute(x[0], axis, [(i, (i + 1) % n) for i in range(n)])  8.72 us
    ppermute x7, waiting for transfers between devices, ring(): after = lax.ppermute(x[1], axis, [(i, (i - 1) % n) for i in range(n)])  7.24 us
  transfers between devices with their start and end apart: 14, of which 7 were waited for; matrix products, arithmetic and copies ran while one was open for 0% of the time, Pallas kernels for 2%

profile of v7, /device:TPU:1, one launch (start us, length us, event | category | flops | bytes accessed | tf_op | source)
XLA Modules:
  0.0 137.8 jit_solution(748266953668150162)
XLA Ops:
  0.6 2.0 %shard_map.59 = (f32[32,32,128]{2,1,0:T(8,128)S(1)}, f32[84,8,128]{2,1,0:T(8,128)S(1)}, f32[84,8,128]{2,1,0:T(8,128)S(1)}, f32[21,32,128]{2,1,0:T(8,128)S(1)}, f...) custom-call(f32[32,32,128]{2,1,0:T(8,128)} %refs_0_.1, s32[32,32,128]{2,1,0:T(8,128)} %tags_hbm.1, f32[8]{0:T(128)} %table_hbm.1, ...), custom_call_target="tpu_custom_call" | custom-call | tf_op jit(solution)/shard_map/pallas_call | solution.py:31
  2.6 2.5 %collective-permute-start.2 = (f32[84,8,128]{2,1,0:T(8,128)S(1)}, f32[84,8,128]{2,1,0:T(8,128)S(1)}, u32[]{:S(2)}, u32[]{:S(2)}) collective-permute-start(f32[84,8,128]{2,1,0:T(8,128)S(1)} %get-tuple-element.41), channel_id=1, source_target_pairs={{0,1},{1,2},{2,3},{3,4},{4,5},{5,6},{6,7},{7,8},{8,9},{9,10},{10,1... | collective-permute-start | bytes 1032200 | tf_op jit(solution)/shard_map/ppermute | solution.py:642
  5.2 6.5 %collective-permute-start.3 = (f32[84,8,128]{2,1,0:T(8,128)S(1)}, f32[84,8,128]{2,1,0:T(8,128)S(1)}, u32[]{:S(2)}, u32[]{:S(2)}) collective-permute-start(f32[84,8,128]{2,1,0:T(8,128)S(1)} %get-tuple-element.42), channel_id=1, source_target_pairs={{0,31},{1,0},{2,1},{3,2},{4,3},{5,4},{6,5},{7,6},{8,7},{9,8},{10,9... | collective-permute-start | bytes 1032200 | tf_op jit(solution)/shard_map/ppermute | solution.py:643
  11.6 2.1 %collective-permute-start = (f32[21,32,128]{2,1,0:T(8,128)S(1)}, f32[21,32,128]{2,1,0:T(8,128)S(1)}, u32[]{:S(2)}, u32[]{:S(2)}) collective-permute-start(f32[21,32,128]{2,1,0:T(8,128)S(1)} %get-tuple-element.39), channel_id=1, source_target_pairs={{0,32},{32,64},{64,96},{96,128},{128,160},{160,192},{192,224},{224... | collective-permute-start | bytes 1032200 | tf_op jit(solution)/shard_map/ppermute | solution.py:642
  13.7 5.6 %collective-permute-done.2.above.refs_4_.refs_3_ = f32[84,8,128]{2,1,0:T(8,128)S(1)} collective-permute-done((f32[84,8,128]{2,1,0:T(8,128)S(1)}, f32[84,8,128]{2,1,0:T(8,128)S(1)}, u32[]{:S(2)}, u32[]{:S(2)}) %collective-permute-start.2) | collective-permute-done | bytes 344096 | tf_op jit(solution)/shard_map/ppermute | solution.py:642
  19.4 2.3 %collective-permute-start.4 = (f32[35,16,128]{2,1,0:T(8,128)S(1)}, f32[35,16,128]{2,1,0:T(8,128)S(1)}, u32[]{:S(2)}, u32[]{:S(2)}) collective-permute-start(f32[35,16,128]{2,1,0:T(8,128)S(1)} %get-tuple-element.43), channel_id=1, source_target_pairs={{0,32},{32,64},{64,96},{96,128},{128,160},{160,192},{192,224},{224... | collective-permute-start | bytes 860168 | tf_op jit(solution)/shard_map/ppermute | solution.py:642
  21.7 0.0 collective-permute-start.5
  21.7 3.6 %collective-permute-done.4.refs_6_.refs_5_ = f32[35,16,128]{2,1,0:T(8,128)S(1)} collective-permute-done((f32[35,16,128]{2,1,0:T(8,128)S(1)}, f32[35,16,128]{2,1,0:T(8,128)S(1)}, u32[]{:S(2)}, u32[]{:S(2)}) %collective-permute-start.4) | collective-permute-done | bytes 286752 | tf_op jit(solution)/shard_map/ppermute | solution.py:642
  25.3 2.5 %collective-permute-done.5.refs_7_.refs_6_ = f32[35,16,128]{2,1,0:T(8,128)S(1)} collective-permute-done((f32[35,16,128]{2,1,0:T(8,128)S(1)}, f32[35,16,128]{2,1,0:T(8,128)S(1)}, u32[]{:S(2)}, u32[]{:S(2)}) %collective-permute-start.5) | collective-permute-done | bytes 286752 | tf_op jit(solution)/shard_map/ppermute | solution.py:643
  27.8 3.9 %shard_map.61 = (f32[48,48,128]{2,1,0:T(8,128)S(1)}, f32[48,48,128]{2,1,0:T(8,128)S(1)}, f32[48,48,128]{2,1,0:T(8,128)S(1)}, f32[48,48,128]{2,1,0:T(8,128)S(1)},...) custom-call(f32[32,32,128]{2,1,0:T(8,128)S(1)} %copy-done, ...), custom_call_target="tpu_custom_call" | custom-call | flops 60000000 | bytes 20000000 | tf_op jit(solution)/shard_map/pallas_call | solution.py:31
  31.7 0.1 collective-permute-start.6
  31.8 4.9 %collective-permute-start.7 = (f32[8,16,128]{2,1,0:T(8,128)S(1)}, f32[8,16,128]{2,1,0:T(8,128)S(1)}, u32[]{:S(2)}, u32[]{:S(2)}) collective-permute-start(f32[8,16,128]{2,1,0:T(8,128)S(1)} %get-tuple-element.45.own), channel_id=1, source_target_pairs={{0,31},{1,0},{2,1},{3,2},{4,3},{5,4},{6,5},{7,6},{8,7},{9,8},{10,9... | collective-permute-start | bytes 196616 | tf_op jit(solution)/shard_map/ppermute | solution.py:643
  36.7 2.1 %collective-permute-done.6.above = f32[8,16,128]{2,1,0:T(8,128)S(1)} collective-permute-done((f32[8,16,128]{2,1,0:T(8,128)S(1)}, f32[8,16,128]{2,1,0:T(8,128)S(1)}, u32[]{:S(2)}, u32[]{:S(2)}) %collective-permute-start.6) | collective-permute-done | bytes 65568 | tf_op jit(solution)/shard_map/ppermute | solution.py:642
  38.9 0.0 collective-permute-done.7.below
  38.9 0.9 collective-permute-start.9
  39.7 0.9 collective-permute-start.8
  40.6 2.2 %shard_map.62 = (f32[24,48,128]{2,1,0:T(8,128)S(1)}, f32[24,48,128]{2,1,0:T(8,128)S(1)}, f32[24,48,128]{2,1,0:T(8,128)S(1)}, f32[24,48,128]{2,1,0:T(8,128)S(1)},...) custom-call(f32[8,16,128]{2,1,0:T(8,128)S(1)} %get-tuple-element.46., ...), custom_call_target="tpu_custom_call" | custom-call | tf_op jit(solution)/shard_map/pallas_call | solution.py:31
  42.9 1.1 collective-permute-done.9.right
  44.0 0.0 collective-permute-done.8.left
  44.0 2.9 %shard_map.63 = (f32[24,48,128]{2,1,0:T(8,128)S(1)}, f32[24,48,128]{2,1,0:T(8,128)S(1)}, f32[24,24,128]{2,1,0:T(8,128)S(1)}, f32[24,24,128]{2,1,0:T(8,128)S(1)}, f32[256,4,128]{2,1,0:T(4,128)S(1)}) custom-call(f32[8,16,128]{2,1,0:T(8,128)S(1)} %get-tuple-element.45.own, f32[8,48,128]{2,1,0:T(8,128)S(1)} %collective-permute-done.8.left, ...), custom_call_target="tpu_custom_call" | custom-call | tf_op jit(solution)/shard_map/pallas_call | solution.py:31
  46.9 31.9 %all_to_all.10 = f32[256,4,128]{2,1,0:T(4,128)S(1)} all-to-all(f32[256,4,128]{2,1,0:T(4,128)S(1)} %get-tuple-element.56), channel_id=1, replica_groups=mesh['grp'=8,'box'=32] {'grp','box'}, dimensions={0} | all-to-all | bytes 1048576 | tf_op jit(solution)/shard_map/all_to_all | solution.py:659
  78.8 9.9 %shard_map.64 = (f32[48,48,128]{2,1,0:T(8,128)S(1)}, f32[8,16,128]{2,1,0:T(8,128)S(1)}) custom-call(f32[1024,128]{1,0:T(8,128)S(1)} %bitcast.2, f32[48,48,128]{2,1,0:T(8,128)S(1)} %get-tuple-element.57.refs_1_.refs_2_, f32[48,48,128]{2,1,0:T(8,128)S(1)} %get-tuple-element.58.refs_2_.refs_3_, ...), custom_call_target="tpu_custom_call", output_to_operand_aliasing={{0}: (16, {})} | custom-call | tf_op jit(solution)/shard_map/pallas_call | solution.py:31
  88.7 0.6 collective-permute-start.10
  89.3 4.3 %collective-permute-start.11 = (f32[8,16,128]{2,1,0:T(8,128)S(1)}, f32[8,16,128]{2,1,0:T(8,128)S(1)}, u32[]{:S(2)}, u32[]{:S(2)}) collective-permute-start(f32[8,16,128]{2,1,0:T(8,128)S(1)} %get-tuple-element.67.own), channel_id=1, source_target_pairs={{0,31},{1,0},{2,1},{3,2},{4,3},{5,4},{6,5},{7,6},{8,7},{9,8},{10,9... | collective-permute-start | bytes 196616 | tf_op jit(solution)/shard_map/ppermute | solution.py:643
  93.6 1.6 %collective-permute-done.10.above = f32[8,16,128]{2,1,0:T(8,128)S(1)} collective-permute-done((f32[8,16,128]{2,1,0:T(8,128)S(1)}, f32[8,16,128]{2,1,0:T(8,128)S(1)}, u32[]{:S(2)}, u32[]{:S(2)}) %collective-permute-start.10) | collective-permute-done | bytes 65568 | tf_op jit(solution)/shard_map/ppermute | solution.py:642
  95.2 0.0 collective-permute-done.11.below
  95.2 1.6 %collective-permute-start.13 = (f32[8,48,128]{2,1,0:T(8,128)S(1)}, f32[8,48,128]{2,1,0:T(8,128)S(1)}, u32[]{:S(2)}, u32[]{:S(2)}) collective-permute-start(f32[8,48,128]{2,1,0:T(8,128)S(1)} %constant_dynamic-update-slice_fusion.3), channel_id=1, source_target_pairs={{0,224},{32,0},{64,32},{96,64},{128,96},{160,128},{192,160},{224,1... | collective-permute-start | bytes 589832 | tf_op jit(solution)/shard_map/ppermute | solution.py:643
  96.8 0.2 collective-permute-start.12
  97.0 3.6 %collective-permute-done.13.right = f32[8,48,128]{2,1,0:T(8,128)S(1)} collective-permute-done((f32[8,48,128]{2,1,0:T(8,128)S(1)}, f32[8,48,128]{2,1,0:T(8,128)S(1)}, u32[]{:S(2)}, u32[]{:S(2)}) %collective-permute-start.13) | collective-permute-done | bytes 196640 | tf_op jit(solution)/shard_map/ppermute | solution.py:643
  100.7 2.9 %shard_map.65 = (f32[24,48,128]{2,1,0:T(8,128)S(1)}, f32[24,48,128]{2,1,0:T(8,128)S(1)}, f32[24,24,128]{2,1,0:T(8,128)S(1)}, f32[24,24,128]{2,1,0:T(8,128)S(1)}, f32[256,2,128]{2,1,0:T(2,128)S(1)}) custom-call(f32[8,16,128]{2,1,0:T(8,128)S(1)} %get-tuple-element.67.own, f32[8,48,128]{2,1,0:T(8,128)S(1)} %collective-permute-done.12.left, ...), custom_call_target="tpu_custom_call" | custom-call | tf_op jit(solution)/shard_map/pallas_call | solution.py:31
  103.5 25.1 %all_to_all.11 = f32[256,2,128]{2,1,0:T(2,128)S(1)} all-to-all(f32[256,2,128]{2,1,0:T(2,128)S(1)} %get-tuple-element.68), channel_id=1, replica_groups=mesh['grp'=8,'box'=32] {'grp','box'}, dimensions={0} | all-to-all | bytes 524288 | tf_op jit(solution)/shard_map/all_to_all | solution.py:659
  128.7 9.1 %shard_map.66 = (f32[32,32,128]{2,1,0:T(8,128)}, f32[32,32,128]{2,1,0:T(8,128)}) custom-call(f32[512,128]{1,0:T(8,128)S(1)} %bitcast.4, f32[1024,128]{1,0:T(8,128)S(1)} %bitcast.3, f32[48,48,128]{2,1,0:T(8,128)S(1)} %get-tuple-element.57.refs_1_.refs_2_, f32[48,48,128]{2,1,0:T(8,128)S(1)} %get-tuple-element.58.refs_2_.refs_3_, ...), custom_call_target="tpu_custom_call" | custom-call | tf_op jit(solution)/shard_map/pallas_call | solution.py:31
  (14 shorter events, 0.1 us)
Async XLA Ops:
  0.6 27.1 %copy-start = (f32[32,32,128]{2,1,0:T(8,128)S(1)}, f32[32,32,128]{2,1,0:T(8,128)}, u32[]{:S(2)}) copy-start(f32[32,32,128]{2,1,0:T(8,128)} %refs_0_.1) | copy-start | bytes 1572868
  2.6 16.7 %collective-permute-start.2 = (f32[84,8,128]{2,1,0:T(8,128)S(1)}, f32[84,8,128]{2,1,0:T(8,128)S(1)}, u32[]{:S(2)}, u32[]{:S(2)}) collective-permute-start(f32[84,8,128]{2,1,0:T(8,128)S(1)} %get-tuple-element.41), channel_id=1, source_target_pairs={{0,1},{1,2},{2,3},{3,4},{4,5},{5,6},{6,7},{7,8},{8,9},{9,10},{10,1... | collective-permute-start | bytes 1032200 | tf_op jit(solution)/shard_map/ppermute | solution.py:642
  5.2 14.2 %collective-permute-start.3 = (f32[84,8,128]{2,1,0:T(8,128)S(1)}, f32[84,8,128]{2,1,0:T(8,128)S(1)}, u32[]{:S(2)}, u32[]{:S(2)}) collective-permute-start(f32[84,8,128]{2,1,0:T(8,128)S(1)} %get-tuple-element.42), channel_id=1, source_target_pairs={{0,31},{1,0},{2,1},{3,2},{4,3},{5,4},{6,5},{7,6},{8,7},{9,8},{10,9... | collective-permute-start | bytes 1032200 | tf_op jit(solution)/shard_map/ppermute | solution.py:643
  11.6 10.1 %collective-permute-start = (f32[21,32,128]{2,1,0:T(8,128)S(1)}, f32[21,32,128]{2,1,0:T(8,128)S(1)}, u32[]{:S(2)}, u32[]{:S(2)}) collective-permute-start(f32[21,32,128]{2,1,0:T(8,128)S(1)} %get-tuple-element.39), channel_id=1, source_target_pairs={{0,32},{32,64},{64,96},{96,128},{128,160},{160,192},{192,224},{224... | collective-permute-start | bytes 1032200 | tf_op jit(solution)/shard_map/ppermute | solution.py:642
  13.7 8.0 %collective-permute-start.1 = (f32[21,32,128]{2,1,0:T(8,128)S(1)}, f32[21,32,128]{2,1,0:T(8,128)S(1)}, u32[]{:S(2)}, u32[]{:S(2)}) collective-permute-start(f32[21,32,128]{2,1,0:T(8,128)S(1)} %get-tuple-element.40), channel_id=1, source_target_pairs={{0,224},{32,0},{64,32},{96,64},{128,96},{160,128},{192,160},{224,1... | collective-permute-start | bytes 1032200 | tf_op jit(solution)/shard_map/ppermute | solution.py:643
  19.4 5.9 %collective-permute-start.4 = (f32[35,16,128]{2,1,0:T(8,128)S(1)}, f32[35,16,128]{2,1,0:T(8,128)S(1)}, u32[]{:S(2)}, u32[]{:S(2)}) collective-permute-start(f32[35,16,128]{2,1,0:T(8,128)S(1)} %get-tuple-element.43), channel_id=1, source_target_pairs={{0,32},{32,64},{64,96},{96,128},{128,160},{160,192},{192,224},{224... | collective-permute-start | bytes 860168 | tf_op jit(solution)/shard_map/ppermute | solution.py:642
  21.7 6.1 %collective-permute-start.5 = (f32[35,16,128]{2,1,0:T(8,128)S(1)}, f32[35,16,128]{2,1,0:T(8,128)S(1)}, u32[]{:S(2)}, u32[]{:S(2)}) collective-permute-start(f32[35,16,128]{2,1,0:T(8,128)S(1)} %get-tuple-element.44), channel_id=1, source_target_pairs={{0,224},{32,0},{64,32},{96,64},{128,96},{160,128},{192,160},{224,1... | collective-permute-start | bytes 860168 | tf_op jit(solution)/shard_map/ppermute | solution.py:643
  31.7 7.1 %collective-permute-start.6 = (f32[8,16,128]{2,1,0:T(8,128)S(1)}, f32[8,16,128]{2,1,0:T(8,128)S(1)}, u32[]{:S(2)}, u32[]{:S(2)}) collective-permute-start(f32[8,16,128]{2,1,0:T(8,128)S(1)} %get-tuple-element.45.own), channel_id=1, source_target_pairs={{0,1},{1,2},{2,3},{3,4},{4,5},{5,6},{6,7},{7,8},{8,9},{9,10},{10,1... | collective-permute-start | bytes 196616 | tf_op jit(solution)/shard_map/ppermute | solution.py:642
  31.8 7.1 %collective-permute-start.7 = (f32[8,16,128]{2,1,0:T(8,128)S(1)}, f32[8,16,128]{2,1,0:T(8,128)S(1)}, u32[]{:S(2)}, u32[]{:S(2)}) collective-permute-start(f32[8,16,128]{2,1,0:T(8,128)S(1)} %get-tuple-element.45.own), channel_id=1, source_target_pairs={{0,31},{1,0},{2,1},{3,2},{4,3},{5,4},{6,5},{7,6},{8,7},{9,8},{10,9... | collective-permute-start | bytes 196616 | tf_op jit(solution)/shard_map/ppermute | solution.py:643
  38.9 5.1 %collective-permute-start.9 = (f32[8,48,128]{2,1,0:T(8,128)S(1)}, f32[8,48,128]{2,1,0:T(8,128)S(1)}, u32[]{:S(2)}, u32[]{:S(2)}) collective-permute-start(f32[8,48,128]{2,1,0:T(8,128)S(1)} %constant_dynamic-update-slice_fusion), channel_id=1, source_target_pairs={{0,224},{32,0},{64,32},{96,64},{128,96},{160,128},{192,160},{224,1... | collective-permute-start | bytes 589832 | tf_op jit(solution)/shard_map/ppermute | solution.py:643
  39.7 4.2 %collective-permute-start.8 = (f32[8,48,128]{2,1,0:T(8,128)S(1)}, f32[8,48,128]{2,1,0:T(8,128)S(1)}, u32[]{:S(2)}, u32[]{:S(2)}) collective-permute-start(f32[8,48,128]{2,1,0:T(8,128)S(1)} %constant_dynamic-update-slice_fusion), channel_id=1, source_target_pairs={{0,32},{32,64},{64,96},{96,128},{128,160},{160,192},{192,224},{224... | collective-permute-start | bytes 589832 | tf_op jit(solution)/shard_map/ppermute | solution.py:642
  88.7 6.5 %collective-permute-start.10 = (f32[8,16,128]{2,1,0:T(8,128)S(1)}, f32[8,16,128]{2,1,0:T(8,128)S(1)}, u32[]{:S(2)}, u32[]{:S(2)}) collective-permute-start(f32[8,16,128]{2,1,0:T(8,128)S(1)} %get-tuple-element.67.own), channel_id=1, source_target_pairs={{0,1},{1,2},{2,3},{3,4},{4,5},{5,6},{6,7},{7,8},{8,9},{9,10},{10,1... | collective-permute-start | bytes 196616 | tf_op jit(solution)/shard_map/ppermute | solution.py:642
  89.3 5.9 %collective-permute-start.11 = (f32[8,16,128]{2,1,0:T(8,128)S(1)}, f32[8,16,128]{2,1,0:T(8,128)S(1)}, u32[]{:S(2)}, u32[]{:S(2)}) collective-permute-start(f32[8,16,128]{2,1,0:T(8,128)S(1)} %get-tuple-element.67.own), channel_id=1, source_target_pairs={{0,31},{1,0},{2,1},{3,2},{4,3},{5,4},{6,5},{7,6},{8,7},{9,8},{10,9... | collective-permute-start | bytes 196616 | tf_op jit(solution)/shard_map/ppermute | solution.py:643
  95.2 5.4 %collective-permute-start.13 = (f32[8,48,128]{2,1,0:T(8,128)S(1)}, f32[8,48,128]{2,1,0:T(8,128)S(1)}, u32[]{:S(2)}, u32[]{:S(2)}) collective-permute-start(f32[8,48,128]{2,1,0:T(8,128)S(1)} %constant_dynamic-update-slice_fusion.3), channel_id=1, source_target_pairs={{0,224},{32,0},{64,32},{96,64},{128,96},{160,128},{192,160},{224,1... | collective-permute-start | bytes 589832 | tf_op jit(solution)/shard_map/ppermute | solution.py:643
  96.8 3.8 %collective-permute-start.12 = (f32[8,48,128]{2,1,0:T(8,128)S(1)}, f32[8,48,128]{2,1,0:T(8,128)S(1)}, u32[]{:S(2)}, u32[]{:S(2)}) collective-permute-start(f32[8,48,128]{2,1,0:T(8,128)S(1)} %constant_dynamic-update-slice_fusion.3), channel_id=1, source_target_pairs={{0,32},{32,64},{64,96},{96,128},{128,160},{160,192},{192,224},{224... | collective-permute-start | bytes 589832 | tf_op jit(solution)/shard_map/ppermute | solution.py:642

commit v8 on v7

--- a/solution.py
+++ b/solution.py
@@ -357,9 +357,7 @@
     return to_level1(pair_rows(s, 8, 16))
 
 
-def start_kernel(
-    ng, nb, f, coef, left, right, above, below, cleft, cright, v, fx, wx, ws, wl, di, packed, cx, edge, s
-):
+def inner_kernel(ng, nb, f, coef, above, below, v, fx, wx, ws, wl, di, cx, edge):
     gl, gr, bl, br = edge_flags(ng, nb)
     fx[8:40, 8:40] = f[...]
     fx[8:40, 0:8] = above[0:32]
@@ -367,6 +365,16 @@
     cx[9:41, 8:40] = coef[...]
     cx[9:41, 0:8] = above[32:64] * bl
     cx[9:41, 40:48] = below[32:64] * br
+    edge[0, 9:41] = flat(above[64:68]) * bl
+    edge[1, 9:41] = flat(below[64:68]) * br
+    op = (wx, ws, wl, di)
+    weights(cx, 1, op, 9, 39, 127, False, edge)
+    first_sweep(v, fx, op, 9, 39)
+
+
+def start_kernel(ng, nb, left, right, cleft, cright, *refs):
+    v, fx, wx, ws, wl, di, cx, edge, packed, s = refs[8:]
+    gl, gr, bl, br = edge_flags(ng, nb)
     for x, side, corner, flag in ((0, left, cleft, gl), (40, right, cright, gr)):
         fx[x : x + 8, 8:40] = side[0:8]
         fx[x : x + 8, 0:8] = corner[0:8, 0:8]
@@ -377,11 +385,10 @@
         cx[x : x + 9, 40:48] = corner[8:17, 8:16] * (flag * br)
         edge[0, x : x + 9] = corner[17, 0:9] * (flag * bl)
         edge[1, x : x + 9] = corner[18, 0:9] * (flag * br)
-    edge[0, 9:41] = flat(above[64:68]) * bl
-    edge[1, 9:41] = flat(below[64:68]) * br
     op = (wx, ws, wl, di)
-    weights(cx, 1, op, 0, 48, 127, False, edge)
-    first_sweep(v, fx, op, 0, 48)
+    for lo, hi in ((0, 9), (39, 48)):
+        weights(cx, 1, op, lo, hi, 127, False, edge)
+        first_sweep(v, fx, op, lo, hi)
     sweep(v, fx, op, 1, 47)
     packed[...] = fine_restrict(v, fx, op, s)
 
@@ -509,15 +516,27 @@
     return v
 
 
-def coarse(ng, nb, got, got_c, v3, f3, op3, c3, s3):
+def coarse_weights(ng, nb, got, op3, c4, c3, s3):
     n3, nl = 4 * ng, 4 * nb
     for g in range(ng):
-        slabs = slice(4 + 4 * g, 8 + 4 * g)
-        t = got_c[g * nl : (g + 1) * nl, :].T
-        c3[slabs] = t[64:128].reshape(4, 16, nl)
-        if got is None:
-            f3[slabs] = t[0:64].reshape(4, 16, nl)
-    if got is not None:
+        t = got[g * nl : (g + 1) * nl, :].T
+        c3[4 + 4 * g : 8 + 4 * g] = t[64:128].reshape(4, 16, nl)
+    pad = jnp.zeros((4, 16, nl), F32)
+    for ref in (c3, op3[0]):
+        ref[0:4] = pad
+        ref[4 + n3 : 8 + n3] = pad
+    weights(c3, 0, op3, 4, 4 + n3, nl - 1, True)
+    sum_pairs(c3, 4, n3 // 2, s3)
+    c4[...] = dot(flat(pair_rows(s3, 0, 8) * F32(0.25)), halver(nl)).reshape(n3 // 2, 8, nl)
+
+
+def coarse(ng, nb, got, v3, f3, op3, c4, s3):
+    n3, nl = 4 * ng, 4 * nb
+    if got.shape[0] == ng * nl:
+        for g in range(ng):
+            t = got[g * nl : (g + 1) * nl, :].T
+            f3[4 + 4 * g : 8 + 4 * g] = t[0:64].reshape(4, 16, nl)
+    else:
         k, y = iota((nl // 2, nl), 0), iota((nl // 2, nl), 1)
         even = jnp.where(y == 2 * k, F32(1.0), F32(0.0))
         odd = jnp.where(y == 2 * k + 1, F32(1.0), F32(0.0))
@@ -526,20 +545,16 @@
         lhs1 = jnp.concatenate([t[64:128] for t in ts], 0)
         f3[4 : 4 + n3] = (dot(lhs0, even) + dot(lhs1, odd)).reshape(n3, 16, nl)
     pad = jnp.zeros((4, 16, nl), F32)
-    for ref in (v3, c3, op3[0]):
-        ref[0:4] = pad
-        ref[4 + n3 : 8 + n3] = pad
-    weights(c3, 0, op3, 4, 4 + n3, nl - 1, True)
+    v3[0:4] = pad
+    v3[4 + n3 : 8 + n3] = pad
     lo, hi = 4, 4 + n3
     first_sweep(v3, f3, op3, lo, hi)
     sweep(v3, f3, op3, lo, hi)
     half = halver(nl)
 
-    sum_pairs(c3, 4, n3 // 2, s3)
-    c4 = dot(flat(pair_rows(s3, 0, 8) * F32(0.25)), half).reshape(n3 // 2, 8, nl)
     resid_pairs(v3, f3, op3, 4, n3 // 2, s3)
     f4 = dot(flat(pair_rows(s3, 0, 8)), half).reshape(n3 // 2, 8, nl)
-    v4 = bottom(f4, c4, nl // 2)
+    v4 = bottom(f4, c4[...], nl // 2)
     e = dot(flat(v4), doubler(nl)).reshape(n3 // 2, 8, nl)
     s3[:, pl.ds(0, 8, stride=2), :] = e
     s3[:, pl.ds(1, 8, stride=2), :] = e
@@ -573,10 +588,9 @@
             v2[x + 1] = v2[x + 1] + part
 
 
-def climb(ng, nb, got, got_c, v0, f0, op0, v1, f1, op1, v2, f2, op2, scr):
-    v3, f3, c3, wx3, ws3, wl3, di3, s3, s2, es = scr
-    op3 = (wx3, ws3, wl3, di3)
-    coarse(ng, nb, got, got_c, v3, f3, op3, c3, s3)
+def climb(ng, nb, got, op3, c4, v1, f1, op1, v2, f2, op2, scr):
+    v3, f3, s3, s2, es = scr
+    coarse(ng, nb, got, v3, f3, op3, c4, s3)
     coarse_to_mid(nb, v3, v2, s2, 4 * nb)
     sweep(v2, f2, op2, 4, 20)
     sweep(v2, f2, op2, 5, 19)
@@ -600,12 +614,14 @@
     got, f0, wx0, ws0, wl0, di0, f1, wx1, ws1, wl1, di1, f2, wx2, ws2, wl2, di2 = refs[:16]
     v0i, v1i, v2i = refs[16:19]
     v0, packed = refs[19:21]
-    v1, v2, s = refs[21:24]
-    scr = refs[24:]
+    op3, c4 = refs[21:25], refs[25]
+    v1, v2, s, c3 = refs[26:30]
+    scr = refs[30:]
+    coarse_weights(ng, nb, got, op3, c4, c3, scr[2])
     v1[...] = v1i[...]
     v2[...] = v2i[...]
     op0, op1, op2 = (wx0, ws0, wl0, di0), (wx1, ws1, wl1, di1), (wx2, ws2, wl2, di2)
-    climb(ng, nb, None, got, v0, f0, op0, v1, f1, op1, v2, f2, op2, scr)
+    climb(ng, nb, got, op3, c4, v1, f1, op1, v2, f2, op2, scr)
     add_double(v0, scr[-1], 0, 48)
     for lo in (2, 3, 4, 5):
         sweep(v0, f0, op0, lo, 48 - lo)
@@ -613,17 +629,17 @@
 
 
 def end_kernel(ng, nb, *refs):
-    got, got_c = refs[:2]
-    f0, wx0, ws0, wl0, di0, f1, wx1, ws1, wl1, di1, f2, wx2, ws2, wl2, di2 = refs[2:17]
-    v0i, v1i, v2i = refs[17:20]
-    sol, res = refs[20:22]
-    v0, v1, v2 = refs[22:25]
-    scr = refs[25:]
+    got, op3, c4 = refs[0], refs[1:5], refs[5]
+    f0, wx0, ws0, wl0, di0, f1, wx1, ws1, wl1, di1, f2, wx2, ws2, wl2, di2 = refs[6:21]
+    v0i, v1i, v2i = refs[21:24]
+    sol, res = refs[24:26]
+    v0, v1, v2 = refs[26:29]
+    scr = refs[29:]
     v0[...] = v0i[...]
     v1[...] = v1i[...]
     v2[...] = v2i[...]
     op0, op1, op2 = (wx0, ws0, wl0, di0), (wx1, ws1, wl1, di1), (wx2, ws2, wl2, di2)
-    climb(ng, nb, got, got_c, v0, f0, op0, v1, f1, op1, v2, f2, op2, scr)
+    climb(ng, nb, got, op3, c4, v1, f1, op1, v2, f2, op2, scr)
     add_double(v0, scr[-1], 4, 44)
     sweep(v0, f0, op0, 6, 42)
     sweep(v0, f0, op0, 7, 41)
@@ -666,7 +682,7 @@
     nd = ng * nb
     pay, pay2 = (nd, 4, 128), (nd, 2, 128)
     lev3 = (n3 + 8, 16, nl)
-    climb_scratch = [lev3] * 7 + [(n3 // 2, 16, nl), (12, 32, nl), (24, 48, 128)]
+    climb_scratch = [lev3] * 2 + [(n3 // 2, 16, nl), (12, 32, nl), (24, 48, 128)]
 
     def fix(kernel):
         return lambda *refs: kernel(ng, nb, *refs)
@@ -685,9 +701,13 @@
         left, right = ring((x_next, x_prev), "grp", ng)
         corners = call(corners_kernel, (above, below), [(35, 16, 128)] * 2)
         halo = (left, right, above, below) + ring(corners, "grp", ng)
-        v0, f0, wx0, ws0, wl0, di0, packed = call(
-            fix(start_kernel), (f, coef) + halo, [big] * 6 + [(8, 16, 128)],
-            scratch=[(50, 48, 128), (2, 56, 128), (16, 48, 128)], touched=20_000_000,
+        inner = call(
+            fix(inner_kernel), (f, coef, above, below), [big] * 6 + [(50, 48, 128), (2, 56, 128)],
+        )
+        v0, f0, wx0, ws0, wl0, di0, _, _, packed = call(
+            fix(start_kernel), halo[:2] + halo[4:] + tuple(inner),
+            [big] * 6 + [(50, 48, 128), (2, 56, 128), (8, 16, 128)],
+            scratch=[(16, 48, 128)], aliases={4 + i: i for i in range(8)},
         )
         l0 = (f0, wx0, ws0, wl0, di0)
         *ops, coarser = call(
@@ -700,9 +720,10 @@
         )
         got_c = gather_all(payload)
         l1, l2 = (f1, *ops[:4]), (f2, *ops[4:])
-        v0, packed = call(
-            fix(turn_kernel), (got_c,) + l0 + l1 + l2 + (v0, v1, v2), [big, (8, 16, 128)],
-            aliases={16: 0}, scratch=[mid, low, (16, 48, 128)] + climb_scratch,
+        v0, packed, *level3 = call(
+            fix(turn_kernel), (got_c,) + l0 + l1 + l2 + (v0, v1, v2),
+            [big, (8, 16, 128)] + [lev3] * 4 + [(n3 // 2, 8, nl)],
+            aliases={16: 0}, scratch=[mid, low, (16, 48, 128), lev3] + climb_scratch,
         )
         f1, v1, f2, v2, payload = call(
             mid2_kernel, around(packed, ng, nb) + l1[1:] + l2[1:],
@@ -711,7 +732,7 @@
         got = gather_all(payload)
         l1, l2 = (f1,) + l1[1:], (f2,) + l2[1:]
         return tuple(call(
-            fix(end_kernel), (got, got_c) + l0 + l1 + l2 + (v0, v1, v2), [(32, 32, 128)] * 2,
+            fix(end_kernel), (got, *level3) + l0 + l1 + l2 + (v0, v1, v2), [(32, 32, 128)] * 2,
             scratch=[big, mid, low] + climb_scratch, leave=(0, 1),
         ))
 

time: 138 us -> 140 us (1.014)
  waiting for transfers between devices: 20.2 us -> 22.4 us
    ppermute x7, starting transfers between devices: 18.1 us -> 16 us  [ring(): after = lax.ppermute(x[1], axis, [(i, (i - 1) % n) for i in range(n)])]
    pallas_call x8 -> x9, Pallas kernels: 32.9 us -> 33 us  [call(): pl.pallas_call(kernel, out_shape=[shape_of(i, s) for i, s in enumerate(ou...]
  transfers between devices with their start and end apart: 14 -> 14, of which waited for: 7 -> 8; matrix products, arithmetic and copies ran while one was open for 0% -> 0% of each run, Pallas kernels for 2% -> 2%
where the time goes in v8:
time: 140 us
  blocking collectives  57.6 us (41%)
  Pallas kernels  33 us (24%)
  starting transfers between devices  25.9 us (18%)
  waiting for transfers between devices  22.4 us (16%)
    all_to_all x2, blocking collectives, gather_all(): got = lax.all_to_all(payload, ('grp', 'box'), 0, 0, tiled=True)  57.6 us
    pallas_call x9, Pallas kernels, call(): pl.pallas_call(kernel, out_shape=[shape_of(i, s) for i, s in enumerate(ou...  33 us
    ppermute x7, starting transfers between devices, ring(): after = lax.ppermute(x[1], axis, [(i, (i - 1) % n) for i in range(n)])  16 us
    ppermute x7, waiting for transfers between devices, ring(): before = lax.ppermute(x[0], axis, [(i, (i + 1) % n) for i in range(n)])  14.3 us
    ppermute x7, starting transfers between devices, ring(): before = lax.ppermute(x[0], axis, [(i, (i + 1) % n) for i in range(n)])  9.89 us
    ppermute x7, waiting for transfers between devices, ring(): after = lax.ppermute(x[1], axis, [(i, (i - 1) % n) for i in range(n)])  8.07 us
  transfers between devices with their start and end apart: 14, of which 8 were waited for; matrix products, arithmetic and copies ran while one was open for 0% of the time, Pallas kernels for 2%

profile of v8, /device:TPU:1, one launch (start us, length us, event | category | flops | bytes accessed | tf_op | source)
XLA Modules:
  0.0 139.7 jit_solution(14752384936270177382)
XLA Ops:
  0.6 2.0 %shard_map.59 = (f32[32,32,128]{2,1,0:T(8,128)S(1)}, f32[84,8,128]{2,1,0:T(8,128)S(1)}, f32[84,8,128]{2,1,0:T(8,128)S(1)}, f32[21,32,128]{2,1,0:T(8,128)S(1)}, f...) custom-call(f32[32,32,128]{2,1,0:T(8,128)} %refs_0_.1, s32[32,32,128]{2,1,0:T(8,128)} %tags_hbm.1, f32[8]{0:T(128)} %table_hbm.1, ...), custom_call_target="tpu_custom_call" | custom-call | tf_op jit(solution)/shard_map/pallas_call | solution.py:31
  2.6 2.5 %collective-permute-start.2 = (f32[84,8,128]{2,1,0:T(8,128)S(1)}, f32[84,8,128]{2,1,0:T(8,128)S(1)}, u32[]{:S(2)}, u32[]{:S(2)}) collective-permute-start(f32[84,8,128]{2,1,0:T(8,128)S(1)} %get-tuple-element.53), channel_id=1, source_target_pairs={{0,1},{1,2},{2,3},{3,4},{4,5},{5,6},{6,7},{7,8},{8,9},{9,10},{10,1... | collective-permute-start | bytes 1032200 | tf_op jit(solution)/shard_map/ppermute | solution.py:658
  5.2 6.5 %collective-permute-start.3 = (f32[84,8,128]{2,1,0:T(8,128)S(1)}, f32[84,8,128]{2,1,0:T(8,128)S(1)}, u32[]{:S(2)}, u32[]{:S(2)}) collective-permute-start(f32[84,8,128]{2,1,0:T(8,128)S(1)} %get-tuple-element.54), channel_id=1, source_target_pairs={{0,31},{1,0},{2,1},{3,2},{4,3},{5,4},{6,5},{7,6},{8,7},{9,8},{10,9... | collective-permute-start | bytes 1032200 | tf_op jit(solution)/shard_map/ppermute | solution.py:659
  11.6 2.1 %collective-permute-start = (f32[21,32,128]{2,1,0:T(8,128)S(1)}, f32[21,32,128]{2,1,0:T(8,128)S(1)}, u32[]{:S(2)}, u32[]{:S(2)}) collective-permute-start(f32[21,32,128]{2,1,0:T(8,128)S(1)} %get-tuple-element.51), channel_id=1, source_target_pairs={{0,32},{32,64},{64,96},{96,128},{128,160},{160,192},{192,224},{224... | collective-permute-start | bytes 1032200 | tf_op jit(solution)/shard_map/ppermute | solution.py:658
  13.7 0.0 collective-permute-start.1
  13.7 5.6 %collective-permute-done.2.above.refs_2_.refs_3_ = f32[84,8,128]{2,1,0:T(8,128)S(1)} collective-permute-done((f32[84,8,128]{2,1,0:T(8,128)S(1)}, f32[84,8,128]{2,1,0:T(8,128)S(1)}, u32[]{:S(2)}, u32[]{:S(2)}) %collective-permute-start.2) | collective-permute-done | bytes 344096 | tf_op jit(solution)/shard_map/ppermute | solution.py:658
  19.3 0.0 collective-permute-done.3.below.refs_3_.refs_4_
  19.4 2.3 %collective-permute-start.4 = (f32[35,16,128]{2,1,0:T(8,128)S(1)}, f32[35,16,128]{2,1,0:T(8,128)S(1)}, u32[]{:S(2)}, u32[]{:S(2)}) collective-permute-start(f32[35,16,128]{2,1,0:T(8,128)S(1)} %get-tuple-element.55), channel_id=1, source_target_pairs={{0,32},{32,64},{64,96},{96,128},{128,160},{160,192},{192,224},{224... | collective-permute-start | bytes 860168 | tf_op jit(solution)/shard_map/ppermute | solution.py:658
  21.7 1.2 shard_map.61
  22.9 0.0 collective-permute-done.refs_0_.refs_1_
  23.0 2.3 %collective-permute-done.4.refs_2_.refs_5_ = f32[35,16,128]{2,1,0:T(8,128)S(1)} collective-permute-done((f32[35,16,128]{2,1,0:T(8,128)S(1)}, f32[35,16,128]{2,1,0:T(8,128)S(1)}, u32[]{:S(2)}, u32[]{:S(2)}) %collective-permute-start.4) | collective-permute-done | bytes 286752 | tf_op jit(solution)/shard_map/ppermute | solution.py:658
  25.3 2.5 %collective-permute-done.5.refs_3_.refs_6_ = f32[35,16,128]{2,1,0:T(8,128)S(1)} collective-permute-done((f32[35,16,128]{2,1,0:T(8,128)S(1)}, f32[35,16,128]{2,1,0:T(8,128)S(1)}, u32[]{:S(2)}, u32[]{:S(2)}) %collective-permute-start.5) | collective-permute-done | bytes 286752 | tf_op jit(solution)/shard_map/ppermute | solution.py:659
  27.8 2.8 %shard_map.62 = (f32[48,48,128]{2,1,0:T(8,128)S(1)}, f32[48,48,128]{2,1,0:T(8,128)S(1)}, f32[48,48,128]{2,1,0:T(8,128)S(1)}, f32[48,48,128]{2,1,0:T(8,128)S(1)},...) custom-call(f32[21,32,128]{2,1,0:T(8,128)S(1)} %collective-permute-d, ...), custom_call_target="tpu_custom_call", output_to_operand_aliasing={{0}: (4, {}), {1}: (5, {}), {2}: (6, {}), {3}: (7, {}), {4}... | custom-call | tf_op jit(solution)/shard_map/pallas_call | solution.py:31
  30.6 0.1 collective-permute-start.6
  30.7 4.9 %collective-permute-start.7 = (f32[8,16,128]{2,1,0:T(8,128)S(1)}, f32[8,16,128]{2,1,0:T(8,128)S(1)}, u32[]{:S(2)}, u32[]{:S(2)}) collective-permute-start(f32[8,16,128]{2,1,0:T(8,128)S(1)} %get-tuple-element.66.own), channel_id=1, source_target_pairs={{0,31},{1,0},{2,1},{3,2},{4,3},{5,4},{6,5},{7,6},{8,7},{9,8},{10,9... | collective-permute-start | bytes 196616 | tf_op jit(solution)/shard_map/ppermute | solution.py:659
  35.6 2.1 %collective-permute-done.6.above = f32[8,16,128]{2,1,0:T(8,128)S(1)} collective-permute-done((f32[8,16,128]{2,1,0:T(8,128)S(1)}, f32[8,16,128]{2,1,0:T(8,128)S(1)}, u32[]{:S(2)}, u32[]{:S(2)}) %collective-permute-start.6) | collective-permute-done | bytes 65568 | tf_op jit(solution)/shard_map/ppermute | solution.py:658
  37.7 0.5 collective-permute-start.8
  38.3 0.3 collective-permute-start.9
  38.6 2.2 %shard_map.63 = (f32[24,48,128]{2,1,0:T(8,128)S(1)}, f32[24,48,128]{2,1,0:T(8,128)S(1)}, f32[24,48,128]{2,1,0:T(8,128)S(1)}, f32[24,48,128]{2,1,0:T(8,128)S(1)},...) custom-call(f32[8,16,128]{2,1,0:T(8,128)S(1)} %get-tuple-element.67., ...), custom_call_target="tpu_custom_call" | custom-call | tf_op jit(solution)/shard_map/pallas_call | solution.py:31
  40.9 2.8 %collective-permute-done.9.right = f32[8,48,128]{2,1,0:T(8,128)S(1)} collective-permute-done((f32[8,48,128]{2,1,0:T(8,128)S(1)}, f32[8,48,128]{2,1,0:T(8,128)S(1)}, u32[]{:S(2)}, u32[]{:S(2)}) %collective-permute-start.9) | collective-permute-done | bytes 196640 | tf_op jit(solution)/shard_map/ppermute | solution.py:659
  43.7 2.9 %shard_map.64 = (f32[24,48,128]{2,1,0:T(8,128)S(1)}, f32[24,48,128]{2,1,0:T(8,128)S(1)}, f32[24,24,128]{2,1,0:T(8,128)S(1)}, f32[24,24,128]{2,1,0:T(8,128)S(1)}, f32[256,4,128]{2,1,0:T(4,128)S(1)}) custom-call(f32[8,16,128]{2,1,0:T(8,128)S(1)} %get-tuple-element.66.own, f32[8,48,128]{2,1,0:T(8,128)S(1)} %collective-permute-done.8.left, ...), custom_call_target="tpu_custom_call" | custom-call | tf_op jit(solution)/shard_map/pallas_call | solution.py:31
  46.6 31.8 %all_to_all.10 = f32[256,4,128]{2,1,0:T(4,128)S(1)} all-to-all(f32[256,4,128]{2,1,0:T(4,128)S(1)} %get-tuple-element.77), channel_id=1, replica_groups=mesh['grp'=8,'box'=32] {'grp','box'}, dimensions={0} | all-to-all | bytes 1048576 | tf_op jit(solution)/shard_map/all_to_all | solution.py:675
  78.4 10.0 %shard_map.65 = (f32[48,48,128]{2,1,0:T(8,128)S(1)}, f32[8,16,128]{2,1,0:T(8,128)S(1)}, f32[40,16,128]{2,1,0:T(8,128)S(1)}, f32[40,16,128]{2,1,0:T(8,128)S(1)}, ...) custom-call(f32[1024,128]{1,0:T(8,128)S(1)} %bitcast.2, ...), custom_call_target="tpu_custom_call", output_to_operand_aliasing={{0}: (16, {})} | custom-call | tf_op jit(solution)/shard_map/pallas_call | solution.py:31
  88.4 0.6 collective-permute-start.10
  89.0 4.3 %collective-permute-start.11 = (f32[8,16,128]{2,1,0:T(8,128)S(1)}, f32[8,16,128]{2,1,0:T(8,128)S(1)}, u32[]{:S(2)}, u32[]{:S(2)}) collective-permute-start(f32[8,16,128]{2,1,0:T(8,128)S(1)} %get-tuple-element.88.own), channel_id=1, source_target_pairs={{0,31},{1,0},{2,1},{3,2},{4,3},{5,4},{6,5},{7,6},{8,7},{9,8},{10,9... | collective-permute-start | bytes 196616 | tf_op jit(solution)/shard_map/ppermute | solution.py:659
  93.3 1.6 %collective-permute-done.10.above = f32[8,16,128]{2,1,0:T(8,128)S(1)} collective-permute-done((f32[8,16,128]{2,1,0:T(8,128)S(1)}, f32[8,16,128]{2,1,0:T(8,128)S(1)}, u32[]{:S(2)}, u32[]{:S(2)}) %collective-permute-start.10) | collective-permute-done | bytes 65568 | tf_op jit(solution)/shard_map/ppermute | solution.py:658
  95.0 1.7 %collective-permute-start.12 = (f32[8,48,128]{2,1,0:T(8,128)S(1)}, f32[8,48,128]{2,1,0:T(8,128)S(1)}, u32[]{:S(2)}, u32[]{:S(2)}) collective-permute-start(f32[8,48,128]{2,1,0:T(8,128)S(1)} %constant_dynamic-update-slice_fusion.3), channel_id=1, source_target_pairs={{0,32},{32,64},{64,96},{96,128},{128,160},{160,192},{192,224},{224... | collective-permute-start | bytes 589832 | tf_op jit(solution)/shard_map/ppermute | solution.py:658
  96.7 2.6 %collective-permute-done.12.left = f32[8,48,128]{2,1,0:T(8,128)S(1)} collective-permute-done((f32[8,48,128]{2,1,0:T(8,128)S(1)}, f32[8,48,128]{2,1,0:T(8,128)S(1)}, u32[]{:S(2)}, u32[]{:S(2)}) %collective-permute-start.12) | collective-permute-done | bytes 196640 | tf_op jit(solution)/shard_map/ppermute | solution.py:658
  99.4 2.8 %collective-permute-done.13.right = f32[8,48,128]{2,1,0:T(8,128)S(1)} collective-permute-done((f32[8,48,128]{2,1,0:T(8,128)S(1)}, f32[8,48,128]{2,1,0:T(8,128)S(1)}, u32[]{:S(2)}, u32[]{:S(2)}) %collective-permute-start.13) | collective-permute-done | bytes 196640 | tf_op jit(solution)/shard_map/ppermute | solution.py:659
  102.1 3.0 %shard_map.66 = (f32[24,48,128]{2,1,0:T(8,128)S(1)}, f32[24,48,128]{2,1,0:T(8,128)S(1)}, f32[24,24,128]{2,1,0:T(8,128)S(1)}, f32[24,24,128]{2,1,0:T(8,128)S(1)}, f32[256,2,128]{2,1,0:T(2,128)S(1)}) custom-call(f32[8,16,128]{2,1,0:T(8,128)S(1)} %get-tuple-element.88.own, f32[8,48,128]{2,1,0:T(8,128)S(1)} %collective-permute-done.12.left, ...), custom_call_target="tpu_custom_call" | custom-call | tf_op jit(solution)/shard_map/pallas_call | solution.py:31
  105.1 25.8 %all_to_all.11 = f32[256,2,128]{2,1,0:T(2,128)S(1)} all-to-all(f32[256,2,128]{2,1,0:T(2,128)S(1)} %get-tuple-element.89), channel_id=1, replica_groups=mesh['grp'=8,'box'=32] {'grp','box'}, dimensions={0} | all-to-all | bytes 524288 | tf_op jit(solution)/shard_map/all_to_all | solution.py:675
  130.9 8.8 %shard_map.67 = (f32[32,32,128]{2,1,0:T(8,128)}, f32[32,32,128]{2,1,0:T(8,128)}) custom-call(f32[512,128]{1,0:T(8,128)S(1)} %bitcast.3, f32[40,16,128]{2,1,0:T(8,128)S(1)} %get-tuple-element.90.refs_1_, f32[40,16,128]{2,1,0:T(8,128)S(1)} %get-tuple-element.91.refs_2_, f32[40,16,128]{2,1,0:T(8,128)S(1)} %get-tuple-element.92.refs_3_, ...), custom_call_target="tpu_custom_call" | custom-call | tf_op jit(solution)/shard_map/pallas_call | solution.py:31
  (15 shorter events, 0.1 us)
Async XLA Ops:
  0.6 21.1 %copy-start = (f32[32,32,128]{2,1,0:T(8,128)S(1)}, f32[32,32,128]{2,1,0:T(8,128)}, u32[]{:S(2)}) copy-start(f32[32,32,128]{2,1,0:T(8,128)} %refs_0_.1) | copy-start | bytes 1572868
  2.6 16.7 %collective-permute-start.2 = (f32[84,8,128]{2,1,0:T(8,128)S(1)}, f32[84,8,128]{2,1,0:T(8,128)S(1)}, u32[]{:S(2)}, u32[]{:S(2)}) collective-permute-start(f32[84,8,128]{2,1,0:T(8,128)S(1)} %get-tuple-element.53), channel_id=1, source_target_pairs={{0,1},{1,2},{2,3},{3,4},{4,5},{5,6},{6,7},{7,8},{8,9},{9,10},{10,1... | collective-permute-start | bytes 1032200 | tf_op jit(solution)/shard_map/ppermute | solution.py:658
  5.2 14.2 %collective-permute-start.3 = (f32[84,8,128]{2,1,0:T(8,128)S(1)}, f32[84,8,128]{2,1,0:T(8,128)S(1)}, u32[]{:S(2)}, u32[]{:S(2)}) collective-permute-start(f32[84,8,128]{2,1,0:T(8,128)S(1)} %get-tuple-element.54), channel_id=1, source_target_pairs={{0,31},{1,0},{2,1},{3,2},{4,3},{5,4},{6,5},{7,6},{8,7},{9,8},{10,9... | collective-permute-start | bytes 1032200 | tf_op jit(solution)/shard_map/ppermute | solution.py:659
  11.6 11.3 %collective-permute-start = (f32[21,32,128]{2,1,0:T(8,128)S(1)}, f32[21,32,128]{2,1,0:T(8,128)S(1)}, u32[]{:S(2)}, u32[]{:S(2)}) collective-permute-start(f32[21,32,128]{2,1,0:T(8,128)S(1)} %get-tuple-element.51), channel_id=1, source_target_pairs={{0,32},{32,64},{64,96},{96,128},{128,160},{160,192},{192,224},{224... | collective-permute-start | bytes 1032200 | tf_op jit(solution)/shard_map/ppermute | solution.py:658
  13.7 9.3 %collective-permute-start.1 = (f32[21,32,128]{2,1,0:T(8,128)S(1)}, f32[21,32,128]{2,1,0:T(8,128)S(1)}, u32[]{:S(2)}, u32[]{:S(2)}) collective-permute-start(f32[21,32,128]{2,1,0:T(8,128)S(1)} %get-tuple-element.52), channel_id=1, source_target_pairs={{0,224},{32,0},{64,32},{96,64},{128,96},{160,128},{192,160},{224,1... | collective-permute-start | bytes 1032200 | tf_op jit(solution)/shard_map/ppermute | solution.py:659
  19.4 5.9 %collective-permute-start.4 = (f32[35,16,128]{2,1,0:T(8,128)S(1)}, f32[35,16,128]{2,1,0:T(8,128)S(1)}, u32[]{:S(2)}, u32[]{:S(2)}) collective-permute-start(f32[35,16,128]{2,1,0:T(8,128)S(1)} %get-tuple-element.55), channel_id=1, source_target_pairs={{0,32},{32,64},{64,96},{96,128},{128,160},{160,192},{192,224},{224... | collective-permute-start | bytes 860168 | tf_op jit(solution)/shard_map/ppermute | solution.py:658
  21.7 6.1 %collective-permute-start.5 = (f32[35,16,128]{2,1,0:T(8,128)S(1)}, f32[35,16,128]{2,1,0:T(8,128)S(1)}, u32[]{:S(2)}, u32[]{:S(2)}) collective-permute-start(f32[35,16,128]{2,1,0:T(8,128)S(1)} %get-tuple-element.56), channel_id=1, source_target_pairs={{0,224},{32,0},{64,32},{96,64},{128,96},{160,128},{192,160},{224,1... | collective-permute-start | bytes 860168 | tf_op jit(solution)/shard_map/ppermute | solution.py:659
  30.6 7.1 %collective-permute-start.6 = (f32[8,16,128]{2,1,0:T(8,128)S(1)}, f32[8,16,128]{2,1,0:T(8,128)S(1)}, u32[]{:S(2)}, u32[]{:S(2)}) collective-permute-start(f32[8,16,128]{2,1,0:T(8,128)S(1)} %get-tuple-element.66.own), channel_id=1, source_target_pairs={{0,1},{1,2},{2,3},{3,4},{4,5},{5,6},{6,7},{7,8},{8,9},{9,10},{10,1... | collective-permute-start | bytes 196616 | tf_op jit(solution)/shard_map/ppermute | solution.py:658
  30.7 7.1 %collective-permute-start.7 = (f32[8,16,128]{2,1,0:T(8,128)S(1)}, f32[8,16,128]{2,1,0:T(8,128)S(1)}, u32[]{:S(2)}, u32[]{:S(2)}) collective-permute-start(f32[8,16,128]{2,1,0:T(8,128)S(1)} %get-tuple-element.66.own), channel_id=1, source_target_pairs={{0,31},{1,0},{2,1},{3,2},{4,3},{5,4},{6,5},{7,6},{8,7},{9,8},{10,9... | collective-permute-start | bytes 196616 | tf_op jit(solution)/shard_map/ppermute | solution.py:659
  37.7 3.1 %collective-permute-start.8 = (f32[8,48,128]{2,1,0:T(8,128)S(1)}, f32[8,48,128]{2,1,0:T(8,128)S(1)}, u32[]{:S(2)}, u32[]{:S(2)}) collective-permute-start(f32[8,48,128]{2,1,0:T(8,128)S(1)} %constant_dynamic-update-slice_fusion), channel_id=1, source_target_pairs={{0,32},{32,64},{64,96},{96,128},{128,160},{160,192},{192,224},{224... | collective-permute-start | bytes 589832 | tf_op jit(solution)/shard_map/ppermute | solution.py:658
  38.3 5.4 %collective-permute-start.9 = (f32[8,48,128]{2,1,0:T(8,128)S(1)}, f32[8,48,128]{2,1,0:T(8,128)S(1)}, u32[]{:S(2)}, u32[]{:S(2)}) collective-permute-start(f32[8,48,128]{2,1,0:T(8,128)S(1)} %constant_dynamic-update-slice_fusion), channel_id=1, source_target_pairs={{0,224},{32,0},{64,32},{96,64},{128,96},{160,128},{192,160},{224,1... | collective-permute-start | bytes 589832 | tf_op jit(solution)/shard_map/ppermute | solution.py:659
  88.4 6.5 %collective-permute-start.10 = (f32[8,16,128]{2,1,0:T(8,128)S(1)}, f32[8,16,128]{2,1,0:T(8,128)S(1)}, u32[]{:S(2)}, u32[]{:S(2)}) collective-permute-start(f32[8,16,128]{2,1,0:T(8,128)S(1)} %get-tuple-element.88.own), channel_id=1, source_target_pairs={{0,1},{1,2},{2,3},{3,4},{4,5},{5,6},{6,7},{7,8},{8,9},{9,10},{10,1... | collective-permute-start | bytes 196616 | tf_op jit(solution)/shard_map/ppermute | solution.py:658
  89.0 5.9 %collective-permute-start.11 = (f32[8,16,128]{2,1,0:T(8,128)S(1)}, f32[8,16,128]{2,1,0:T(8,128)S(1)}, u32[]{:S(2)}, u32[]{:S(2)}) collective-permute-start(f32[8,16,128]{2,1,0:T(8,128)S(1)} %get-tuple-element.88.own), channel_id=1, source_target_pairs={{0,31},{1,0},{2,1},{3,2},{4,3},{5,4},{6,5},{7,6},{8,7},{9,8},{10,9... | collective-permute-start | bytes 196616 | tf_op jit(solution)/shard_map/ppermute | solution.py:659
  95.0 4.4 %collective-permute-start.12 = (f32[8,48,128]{2,1,0:T(8,128)S(1)}, f32[8,48,128]{2,1,0:T(8,128)S(1)}, u32[]{:S(2)}, u32[]{:S(2)}) collective-permute-start(f32[8,48,128]{2,1,0:T(8,128)S(1)} %constant_dynamic-update-slice_fusion.3), channel_id=1, source_target_pairs={{0,32},{32,64},{64,96},{96,128},{128,160},{160,192},{192,224},{224... | collective-permute-start | bytes 589832 | tf_op jit(solution)/shard_map/ppermute | solution.py:658
  96.7 5.4 %collective-permute-start.13 = (f32[8,48,128]{2,1,0:T(8,128)S(1)}, f32[8,48,128]{2,1,0:T(8,128)S(1)}, u32[]{:S(2)}, u32[]{:S(2)}) collective-permute-start(f32[8,48,128]{2,1,0:T(8,128)S(1)} %constant_dynamic-update-slice_fusion.3), channel_id=1, source_target_pairs={{0,224},{32,0},{64,32},{96,64},{128,96},{160,128},{192,160},{224,1... | collective-permute-start | bytes 589832 | tf_op jit(solution)/shard_map/ppermute | solution.py:659

commit v9 on v8

--- a/solution.py
+++ b/solution.py
@@ -453,7 +453,7 @@
 
 
 def mid_kernel(
-    own, left, right, above, below, wx1, ws1, wl1, di1, wx2, ws2, wl2, di2, coarser,
+    own, right, left, above, below, wx1, ws1, wl1, di1, wx2, ws2, wl2, di2, coarser,
     f1, v1, f2, v2, payload, s,
 ):
     assemble(f1, own, left, right, above, below)
@@ -462,7 +462,7 @@
 
 
 def mid2_kernel(
-    own, left, right, above, below, wx1, ws1, wl1, di1, wx2, ws2, wl2, di2,
+    own, right, left, above, below, wx1, ws1, wl1, di1, wx2, ws2, wl2, di2,
     f1, v1, f2, v2, payload, s,
 ):
     assemble(f1, own, left, right, above, below)
@@ -668,7 +668,7 @@
 def around(packed, ng, nb):
     above, below, tall = tall_of(packed, nb)
     left, right = ring((tall, tall), "grp", ng)
-    return packed, left, right, above, below
+    return packed, right, left, above, below
 
 
 def gather_all(payload):

time: 140 us -> 137 us (0.979)
  waiting for transfers between devices: 22.4 us -> 19 us
    ppermute x7, waiting for transfers between devices: 14.3 us -> 11.7 us  [ring(): before = lax.ppermute(x[0], axis, [(i, (i + 1) % n) for i in range(n)])]
    ppermute x7, starting transfers between devices: 16 us -> 18.1 us  [ring(): after = lax.ppermute(x[1], axis, [(i, (i - 1) % n) for i in range(n)])]
  transfers between devices with their start and end apart: 14 -> 14, of which waited for: 8 -> 7; matrix products, arithmetic and copies ran while one was open for 0% -> 0% of each run, Pallas kernels for 2% -> 3%
where the time goes in v9:
time: 137 us
  blocking collectives  57 us (42%)
  Pallas kernels  33 us (24%)
  starting transfers between devices  26.8 us (20%)
  waiting for transfers between devices  19 us (14%)
    all_to_all x2, blocking collectives, gather_all(): got = lax.all_to_all(payload, ('grp', 'box'), 0, 0, tiled=True)  57 us
    pallas_call x9, Pallas kernels, call(): pl.pallas_call(kernel, out_shape=[shape_of(i, s) for i, s in enumerate(ou...  33 us
    ppermute x7, starting transfers between devices, ring(): after = lax.ppermute(x[1], axis, [(i, (i - 1) % n) for i in range(n)])  18.1 us
    ppermute x7, waiting for transfers between devices, ring(): before = lax.ppermute(x[0], axis, [(i, (i + 1) % n) for i in range(n)])  11.7 us
    ppermute x7, starting transfers between devices, ring(): before = lax.ppermute(x[0], axis, [(i, (i + 1) % n) for i in range(n)])  8.72 us
    ppermute x7, waiting for transfers between devices, ring(): after = lax.ppermute(x[1], axis, [(i, (i - 1) % n) for i in range(n)])  7.24 us
  transfers between devices with their start and end apart: 14, of which 7 were waited for; matrix products, arithmetic and copies ran while one was open for 0% of the time, Pallas kernels for 3%

profile of v9, /device:TPU:1, one launch (start us, length us, event | category | flops | bytes accessed | tf_op | source)
XLA Modules:
  0.0 136.6 jit_solution(9256858845172682705)
XLA Ops:
  0.6 2.0 %shard_map.59 = (f32[32,32,128]{2,1,0:T(8,128)S(1)}, f32[84,8,128]{2,1,0:T(8,128)S(1)}, f32[84,8,128]{2,1,0:T(8,128)S(1)}, f32[21,32,128]{2,1,0:T(8,128)S(1)}, f...) custom-call(f32[32,32,128]{2,1,0:T(8,128)} %refs_0_.1, s32[32,32,128]{2,1,0:T(8,128)} %tags_hbm.1, f32[8]{0:T(128)} %table_hbm.1, ...), custom_call_target="tpu_custom_call" | custom-call | tf_op jit(solution)/shard_map/pallas_call | solution.py:31
  2.6 2.5 %collective-permute-start.2 = (f32[84,8,128]{2,1,0:T(8,128)S(1)}, f32[84,8,128]{2,1,0:T(8,128)S(1)}, u32[]{:S(2)}, u32[]{:S(2)}) collective-permute-start(f32[84,8,128]{2,1,0:T(8,128)S(1)} %get-tuple-element.53), channel_id=1, source_target_pairs={{0,1},{1,2},{2,3},{3,4},{4,5},{5,6},{6,7},{7,8},{8,9},{9,10},{10,1... | collective-permute-start | bytes 1032200 | tf_op jit(solution)/shard_map/ppermute | solution.py:658
  5.2 6.5 %collective-permute-start.3 = (f32[84,8,128]{2,1,0:T(8,128)S(1)}, f32[84,8,128]{2,1,0:T(8,128)S(1)}, u32[]{:S(2)}, u32[]{:S(2)}) collective-permute-start(f32[84,8,128]{2,1,0:T(8,128)S(1)} %get-tuple-element.54), channel_id=1, source_target_pairs={{0,31},{1,0},{2,1},{3,2},{4,3},{5,4},{6,5},{7,6},{8,7},{9,8},{10,9... | collective-permute-start | bytes 1032200 | tf_op jit(solution)/shard_map/ppermute | solution.py:659
  11.6 2.1 %collective-permute-start = (f32[21,32,128]{2,1,0:T(8,128)S(1)}, f32[21,32,128]{2,1,0:T(8,128)S(1)}, u32[]{:S(2)}, u32[]{:S(2)}) collective-permute-start(f32[21,32,128]{2,1,0:T(8,128)S(1)} %get-tuple-element.51), channel_id=1, source_target_pairs={{0,32},{32,64},{64,96},{96,128},{128,160},{160,192},{192,224},{224... | collective-permute-start | bytes 1032200 | tf_op jit(solution)/shard_map/ppermute | solution.py:658
  13.7 5.6 %collective-permute-done.2.above.refs_2_.refs_3_ = f32[84,8,128]{2,1,0:T(8,128)S(1)} collective-permute-done((f32[84,8,128]{2,1,0:T(8,128)S(1)}, f32[84,8,128]{2,1,0:T(8,128)S(1)}, u32[]{:S(2)}, u32[]{:S(2)}) %collective-permute-start.2) | collective-permute-done | bytes 344096 | tf_op jit(solution)/shard_map/ppermute | solution.py:658
  19.3 0.0 collective-permute-done.3.below.refs_3_.refs_4_
  19.4 2.3 %collective-permute-start.4 = (f32[35,16,128]{2,1,0:T(8,128)S(1)}, f32[35,16,128]{2,1,0:T(8,128)S(1)}, u32[]{:S(2)}, u32[]{:S(2)}) collective-permute-start(f32[35,16,128]{2,1,0:T(8,128)S(1)} %get-tuple-element.55), channel_id=1, source_target_pairs={{0,32},{32,64},{64,96},{96,128},{128,160},{160,192},{192,224},{224... | collective-permute-start | bytes 860168 | tf_op jit(solution)/shard_map/ppermute | solution.py:658
  21.7 0.0 collective-permute-start.5
  21.7 1.2 shard_map.61
  23.0 0.0 collective-permute-done.1.refs_1_.refs_2_
  23.0 2.3 %collective-permute-done.4.refs_2_.refs_5_ = f32[35,16,128]{2,1,0:T(8,128)S(1)} collective-permute-done((f32[35,16,128]{2,1,0:T(8,128)S(1)}, f32[35,16,128]{2,1,0:T(8,128)S(1)}, u32[]{:S(2)}, u32[]{:S(2)}) %collective-permute-start.4) | collective-permute-done | bytes 286752 | tf_op jit(solution)/shard_map/ppermute | solution.py:658
  25.3 2.5 %collective-permute-done.5.refs_3_.refs_6_ = f32[35,16,128]{2,1,0:T(8,128)S(1)} collective-permute-done((f32[35,16,128]{2,1,0:T(8,128)S(1)}, f32[35,16,128]{2,1,0:T(8,128)S(1)}, u32[]{:S(2)}, u32[]{:S(2)}) %collective-permute-start.5) | collective-permute-done | bytes 286752 | tf_op jit(solution)/shard_map/ppermute | solution.py:659
  27.8 2.8 %shard_map.62 = (f32[48,48,128]{2,1,0:T(8,128)S(1)}, f32[48,48,128]{2,1,0:T(8,128)S(1)}, f32[48,48,128]{2,1,0:T(8,128)S(1)}, f32[48,48,128]{2,1,0:T(8,128)S(1)},...) custom-call(f32[21,32,128]{2,1,0:T(8,128)S(1)} %collective-permute-d, ...), custom_call_target="tpu_custom_call", output_to_operand_aliasing={{0}: (4, {}), {1}: (5, {}), {2}: (6, {}), {3}: (7, {}), {4}... | custom-call | tf_op jit(solution)/shard_map/pallas_call | solution.py:31
  30.6 0.1 collective-permute-start.6
  30.7 4.9 %collective-permute-start.7 = (f32[8,16,128]{2,1,0:T(8,128)S(1)}, f32[8,16,128]{2,1,0:T(8,128)S(1)}, u32[]{:S(2)}, u32[]{:S(2)}) collective-permute-start(f32[8,16,128]{2,1,0:T(8,128)S(1)} %get-tuple-element.66.own), channel_id=1, source_target_pairs={{0,31},{1,0},{2,1},{3,2},{4,3},{5,4},{6,5},{7,6},{8,7},{9,8},{10,9... | collective-permute-start | bytes 196616 | tf_op jit(solution)/shard_map/ppermute | solution.py:659
  35.6 2.1 %collective-permute-done.6.above = f32[8,16,128]{2,1,0:T(8,128)S(1)} collective-permute-done((f32[8,16,128]{2,1,0:T(8,128)S(1)}, f32[8,16,128]{2,1,0:T(8,128)S(1)}, u32[]{:S(2)}, u32[]{:S(2)}) %collective-permute-start.6) | collective-permute-done | bytes 65568 | tf_op jit(solution)/shard_map/ppermute | solution.py:658
  37.7 0.9 collective-permute-start.8
  38.6 0.9 collective-permute-start.9
  39.5 2.2 %shard_map.63 = (f32[24,48,128]{2,1,0:T(8,128)S(1)}, f32[24,48,128]{2,1,0:T(8,128)S(1)}, f32[24,48,128]{2,1,0:T(8,128)S(1)}, f32[24,48,128]{2,1,0:T(8,128)S(1)},...) custom-call(f32[8,16,128]{2,1,0:T(8,128)S(1)} %get-tuple-element.67., ...), custom_call_target="tpu_custom_call" | custom-call | tf_op jit(solution)/shard_map/pallas_call | solution.py:31
  41.7 1.1 collective-permute-done.8.right
  42.9 2.9 %shard_map.64 = (f32[24,48,128]{2,1,0:T(8,128)S(1)}, f32[24,48,128]{2,1,0:T(8,128)S(1)}, f32[24,24,128]{2,1,0:T(8,128)S(1)}, f32[24,24,128]{2,1,0:T(8,128)S(1)}, f32[256,4,128]{2,1,0:T(4,128)S(1)}) custom-call(f32[8,16,128]{2,1,0:T(8,128)S(1)} %get-tuple-element.66.own, f32[8,48,128]{2,1,0:T(8,128)S(1)} %collective-permute-done.8.right, ...), custom_call_target="tpu_custom_call" | custom-call | tf_op jit(solution)/shard_map/pallas_call | solution.py:31
  45.8 31.9 %all_to_all.10 = f32[256,4,128]{2,1,0:T(4,128)S(1)} all-to-all(f32[256,4,128]{2,1,0:T(4,128)S(1)} %get-tuple-element.77), channel_id=1, replica_groups=mesh['grp'=8,'box'=32] {'grp','box'}, dimensions={0} | all-to-all | bytes 1048576 | tf_op jit(solution)/shard_map/all_to_all | solution.py:675
  77.7 10.0 %shard_map.65 = (f32[48,48,128]{2,1,0:T(8,128)S(1)}, f32[8,16,128]{2,1,0:T(8,128)S(1)}, f32[40,16,128]{2,1,0:T(8,128)S(1)}, f32[40,16,128]{2,1,0:T(8,128)S(1)}, ...) custom-call(f32[1024,128]{1,0:T(8,128)S(1)} %bitcast.2, ...), custom_call_target="tpu_custom_call", output_to_operand_aliasing={{0}: (16, {})} | custom-call | tf_op jit(solution)/shard_map/pallas_call | solution.py:31
  87.7 0.6 collective-permute-start.10
  88.3 4.3 %collective-permute-start.11 = (f32[8,16,128]{2,1,0:T(8,128)S(1)}, f32[8,16,128]{2,1,0:T(8,128)S(1)}, u32[]{:S(2)}, u32[]{:S(2)}) collective-permute-start(f32[8,16,128]{2,1,0:T(8,128)S(1)} %get-tuple-element.88.own), channel_id=1, source_target_pairs={{0,31},{1,0},{2,1},{3,2},{4,3},{5,4},{6,5},{7,6},{8,7},{9,8},{10,9... | collective-permute-start | bytes 196616 | tf_op jit(solution)/shard_map/ppermute | solution.py:659
  92.6 1.6 %collective-permute-done.10.above = f32[8,16,128]{2,1,0:T(8,128)S(1)} collective-permute-done((f32[8,16,128]{2,1,0:T(8,128)S(1)}, f32[8,16,128]{2,1,0:T(8,128)S(1)}, u32[]{:S(2)}, u32[]{:S(2)}) %collective-permute-start.10) | collective-permute-done | bytes 65568 | tf_op jit(solution)/shard_map/ppermute | solution.py:658
  94.3 1.6 %collective-permute-start.12 = (f32[8,48,128]{2,1,0:T(8,128)S(1)}, f32[8,48,128]{2,1,0:T(8,128)S(1)}, u32[]{:S(2)}, u32[]{:S(2)}) collective-permute-start(f32[8,48,128]{2,1,0:T(8,128)S(1)} %constant_dynamic-update-slice_fusion.3), channel_id=1, source_target_pairs={{0,224},{32,0},{64,32},{96,64},{128,96},{160,128},{192,160},{224,1... | collective-permute-start | bytes 589832 | tf_op jit(solution)/shard_map/ppermute | solution.py:659
  95.8 0.2 collective-permute-start.13
  96.0 3.6 %collective-permute-done.12.right = f32[8,48,128]{2,1,0:T(8,128)S(1)} collective-permute-done((f32[8,48,128]{2,1,0:T(8,128)S(1)}, f32[8,48,128]{2,1,0:T(8,128)S(1)}, u32[]{:S(2)}, u32[]{:S(2)}) %collective-permute-start.12) | collective-permute-done | bytes 196640 | tf_op jit(solution)/shard_map/ppermute | solution.py:659
  99.7 3.0 %shard_map.66 = (f32[24,48,128]{2,1,0:T(8,128)S(1)}, f32[24,48,128]{2,1,0:T(8,128)S(1)}, f32[24,24,128]{2,1,0:T(8,128)S(1)}, f32[24,24,128]{2,1,0:T(8,128)S(1)}, f32[256,2,128]{2,1,0:T(2,128)S(1)}) custom-call(f32[8,16,128]{2,1,0:T(8,128)S(1)} %get-tuple-element.88.own, f32[8,48,128]{2,1,0:T(8,128)S(1)} %collective-permute-done.12.right, ...), custom_call_target="tpu_custom_call" | custom-call | tf_op jit(solution)/shard_map/pallas_call | solution.py:31
  102.7 25.1 %all_to_all.11 = f32[256,2,128]{2,1,0:T(2,128)S(1)} all-to-all(f32[256,2,128]{2,1,0:T(2,128)S(1)} %get-tuple-element.89), channel_id=1, replica_groups=mesh['grp'=8,'box'=32] {'grp','box'}, dimensions={0} | all-to-all | bytes 524288 | tf_op jit(solution)/shard_map/all_to_all | solution.py:675
  127.8 8.8 %shard_map.67 = (f32[32,32,128]{2,1,0:T(8,128)}, f32[32,32,128]{2,1,0:T(8,128)}) custom-call(f32[512,128]{1,0:T(8,128)S(1)} %bitcast.3, f32[40,16,128]{2,1,0:T(8,128)S(1)} %get-tuple-element.90.refs_1_, f32[40,16,128]{2,1,0:T(8,128)S(1)} %get-tuple-element.91.refs_2_, f32[40,16,128]{2,1,0:T(8,128)S(1)} %get-tuple-element.92.refs_3_, ...), custom_call_target="tpu_custom_call" | custom-call | tf_op jit(solution)/shard_map/pallas_call | solution.py:31
  (15 shorter events, 0.1 us)
Async XLA Ops:
  0.6 21.1 %copy-start = (f32[32,32,128]{2,1,0:T(8,128)S(1)}, f32[32,32,128]{2,1,0:T(8,128)}, u32[]{:S(2)}) copy-start(f32[32,32,128]{2,1,0:T(8,128)} %refs_0_.1) | copy-start | bytes 1572868
  2.6 16.7 %collective-permute-start.2 = (f32[84,8,128]{2,1,0:T(8,128)S(1)}, f32[84,8,128]{2,1,0:T(8,128)S(1)}, u32[]{:S(2)}, u32[]{:S(2)}) collective-permute-start(f32[84,8,128]{2,1,0:T(8,128)S(1)} %get-tuple-element.53), channel_id=1, source_target_pairs={{0,1},{1,2},{2,3},{3,4},{4,5},{5,6},{6,7},{7,8},{8,9},{9,10},{10,1... | collective-permute-start | bytes 1032200 | tf_op jit(solution)/shard_map/ppermute | solution.py:658
  5.2 14.2 %collective-permute-start.3 = (f32[84,8,128]{2,1,0:T(8,128)S(1)}, f32[84,8,128]{2,1,0:T(8,128)S(1)}, u32[]{:S(2)}, u32[]{:S(2)}) collective-permute-start(f32[84,8,128]{2,1,0:T(8,128)S(1)} %get-tuple-element.54), channel_id=1, source_target_pairs={{0,31},{1,0},{2,1},{3,2},{4,3},{5,4},{6,5},{7,6},{8,7},{9,8},{10,9... | collective-permute-start | bytes 1032200 | tf_op jit(solution)/shard_map/ppermute | solution.py:659
  11.6 11.3 %collective-permute-start = (f32[21,32,128]{2,1,0:T(8,128)S(1)}, f32[21,32,128]{2,1,0:T(8,128)S(1)}, u32[]{:S(2)}, u32[]{:S(2)}) collective-permute-start(f32[21,32,128]{2,1,0:T(8,128)S(1)} %get-tuple-element.51), channel_id=1, source_target_pairs={{0,32},{32,64},{64,96},{96,128},{128,160},{160,192},{192,224},{224... | collective-permute-start | bytes 1032200 | tf_op jit(solution)/shard_map/ppermute | solution.py:658
  13.7 9.3 %collective-permute-start.1 = (f32[21,32,128]{2,1,0:T(8,128)S(1)}, f32[21,32,128]{2,1,0:T(8,128)S(1)}, u32[]{:S(2)}, u32[]{:S(2)}) collective-permute-start(f32[21,32,128]{2,1,0:T(8,128)S(1)} %get-tuple-element.52), channel_id=1, source_target_pairs={{0,224},{32,0},{64,32},{96,64},{128,96},{160,128},{192,160},{224,1... | collective-permute-start | bytes 1032200 | tf_op jit(solution)/shard_map/ppermute | solution.py:659
  19.4 5.9 %collective-permute-start.4 = (f32[35,16,128]{2,1,0:T(8,128)S(1)}, f32[35,16,128]{2,1,0:T(8,128)S(1)}, u32[]{:S(2)}, u32[]{:S(2)}) collective-permute-start(f32[35,16,128]{2,1,0:T(8,128)S(1)} %get-tuple-element.55), channel_id=1, source_target_pairs={{0,32},{32,64},{64,96},{96,128},{128,160},{160,192},{192,224},{224... | collective-permute-start | bytes 860168 | tf_op jit(solution)/shard_map/ppermute | solution.py:658
  21.7 6.1 %collective-permute-start.5 = (f32[35,16,128]{2,1,0:T(8,128)S(1)}, f32[35,16,128]{2,1,0:T(8,128)S(1)}, u32[]{:S(2)}, u32[]{:S(2)}) collective-permute-start(f32[35,16,128]{2,1,0:T(8,128)S(1)} %get-tuple-element.56), channel_id=1, source_target_pairs={{0,224},{32,0},{64,32},{96,64},{128,96},{160,128},{192,160},{224,1... | collective-permute-start | bytes 860168 | tf_op jit(solution)/shard_map/ppermute | solution.py:659
  30.6 7.1 %collective-permute-start.6 = (f32[8,16,128]{2,1,0:T(8,128)S(1)}, f32[8,16,128]{2,1,0:T(8,128)S(1)}, u32[]{:S(2)}, u32[]{:S(2)}) collective-permute-start(f32[8,16,128]{2,1,0:T(8,128)S(1)} %get-tuple-element.66.own), channel_id=1, source_target_pairs={{0,1},{1,2},{2,3},{3,4},{4,5},{5,6},{6,7},{7,8},{8,9},{9,10},{10,1... | collective-permute-start | bytes 196616 | tf_op jit(solution)/shard_map/ppermute | solution.py:658
  30.7 7.1 %collective-permute-start.7 = (f32[8,16,128]{2,1,0:T(8,128)S(1)}, f32[8,16,128]{2,1,0:T(8,128)S(1)}, u32[]{:S(2)}, u32[]{:S(2)}) collective-permute-start(f32[8,16,128]{2,1,0:T(8,128)S(1)} %get-tuple-element.66.own), channel_id=1, source_target_pairs={{0,31},{1,0},{2,1},{3,2},{4,3},{5,4},{6,5},{7,6},{8,7},{9,8},{10,9... | collective-permute-start | bytes 196616 | tf_op jit(solution)/shard_map/ppermute | solution.py:659
  37.7 5.1 %collective-permute-start.8 = (f32[8,48,128]{2,1,0:T(8,128)S(1)}, f32[8,48,128]{2,1,0:T(8,128)S(1)}, u32[]{:S(2)}, u32[]{:S(2)}) collective-permute-start(f32[8,48,128]{2,1,0:T(8,128)S(1)} %constant_dynamic-update-slice_fusion), channel_id=1, source_target_pairs={{0,224},{32,0},{64,32},{96,64},{128,96},{160,128},{192,160},{224,1... | collective-permute-start | bytes 589832 | tf_op jit(solution)/shard_map/ppermute | solution.py:659
  38.6 4.2 %collective-permute-start.9 = (f32[8,48,128]{2,1,0:T(8,128)S(1)}, f32[8,48,128]{2,1,0:T(8,128)S(1)}, u32[]{:S(2)}, u32[]{:S(2)}) collective-permute-start(f32[8,48,128]{2,1,0:T(8,128)S(1)} %constant_dynamic-update-slice_fusion), channel_id=1, source_target_pairs={{0,32},{32,64},{64,96},{96,128},{128,160},{160,192},{192,224},{224... | collective-permute-start | bytes 589832 | tf_op jit(solution)/shard_map/ppermute | solution.py:658
  87.7 6.5 %collective-permute-start.10 = (f32[8,16,128]{2,1,0:T(8,128)S(1)}, f32[8,16,128]{2,1,0:T(8,128)S(1)}, u32[]{:S(2)}, u32[]{:S(2)}) collective-permute-start(f32[8,16,128]{2,1,0:T(8,128)S(1)} %get-tuple-element.88.own), channel_id=1, source_target_pairs={{0,1},{1,2},{2,3},{3,4},{4,5},{5,6},{6,7},{7,8},{8,9},{9,10},{10,1... | collective-permute-start | bytes 196616 | tf_op jit(solution)/shard_map/ppermute | solution.py:658
  88.3 5.9 %collective-permute-start.11 = (f32[8,16,128]{2,1,0:T(8,128)S(1)}, f32[8,16,128]{2,1,0:T(8,128)S(1)}, u32[]{:S(2)}, u32[]{:S(2)}) collective-permute-start(f32[8,16,128]{2,1,0:T(8,128)S(1)} %get-tuple-element.88.own), channel_id=1, source_target_pairs={{0,31},{1,0},{2,1},{3,2},{4,3},{5,4},{6,5},{7,6},{8,7},{9,8},{10,9... | collective-permute-start | bytes 196616 | tf_op jit(solution)/shard_map/ppermute | solution.py:659
  94.3 5.4 %collective-permute-start.12 = (f32[8,48,128]{2,1,0:T(8,128)S(1)}, f32[8,48,128]{2,1,0:T(8,128)S(1)}, u32[]{:S(2)}, u32[]{:S(2)}) collective-permute-start(f32[8,48,128]{2,1,0:T(8,128)S(1)} %constant_dynamic-update-slice_fusion.3), channel_id=1, source_target_pairs={{0,224},{32,0},{64,32},{96,64},{128,96},{160,128},{192,160},{224,1... | collective-permute-start | bytes 589832 | tf_op jit(solution)/shard_map/ppermute | solution.py:659
  95.8 3.8 %collective-permute-start.13 = (f32[8,48,128]{2,1,0:T(8,128)S(1)}, f32[8,48,128]{2,1,0:T(8,128)S(1)}, u32[]{:S(2)}, u32[]{:S(2)}) collective-permute-start(f32[8,48,128]{2,1,0:T(8,128)S(1)} %constant_dynamic-update-slice_fusion.3), channel_id=1, source_target_pairs={{0,32},{32,64},{64,96},{96,128},{128,160},{160,192},{192,224},{224... | collective-permute-start | bytes 589832 | tf_op jit(solution)/shard_map/ppermute | solution.py:658

commit v10 on v9

--- a/solution.py
+++ b/solution.py
@@ -372,7 +372,7 @@
     first_sweep(v, fx, op, 9, 39)
 
 
-def start_kernel(ng, nb, left, right, cleft, cright, *refs):
+def start_kernel(ng, nb, right, left, cright, cleft, *refs):
     v, fx, wx, ws, wl, di, cx, edge, packed, s = refs[8:]
     gl, gr, bl, br = edge_flags(ng, nb)
     for x, side, corner, flag in ((0, left, cleft, gl), (40, right, cright, gr)):
@@ -427,7 +427,7 @@
 
 
 def mid_weights_kernel(
-    ng, nb, packed, left, right, above, below, cleft, cright,
+    ng, nb, packed, right, left, above, below, cright, cleft,
     wx1, ws1, wl1, di1, wx2, ws2, wl2, di2, coarser, c1, c2, s,
 ):
     gl, gr, bl, br = edge_flags(ng, nb)
@@ -700,7 +700,8 @@
         above, below = ring((to_next, to_prev), "box", nb)
         left, right = ring((x_next, x_prev), "grp", ng)
         corners = call(corners_kernel, (above, below), [(35, 16, 128)] * 2)
-        halo = (left, right, above, below) + ring(corners, "grp", ng)
+        corner_left, corner_right = ring(corners, "grp", ng)
+        halo = (right, left, above, below, corner_right, corner_left)
         inner = call(
             fix(inner_kernel), (f, coef, above, below), [big] * 6 + [(50, 48, 128), (2, 56, 128)],
         )

time: 137 us -> 137 us (level)
  waiting for transfers between devices: 19 us -> 16.2 us
  starting transfers between devices: 26.8 us -> 29.4 us
    ppermute x7, starting transfers between devices: 18.1 us -> 23.7 us  [ring(): after = lax.ppermute(x[1], axis, [(i, (i - 1) % n) for i in range(n)])]
    ppermute x7, starting transfers between devices: 8.72 us -> 5.66 us  [ring(): before = lax.ppermute(x[0], axis, [(i, (i + 1) % n) for i in range(n)])]
    ppermute x7, waiting for transfers between devices: 11.7 us -> 9.24 us  [ring(): before = lax.ppermute(x[0], axis, [(i, (i + 1) % n) for i in range(n)])]
  transfers between devices with their start and end apart: 14 -> 14, of which waited for: 7 -> 6; matrix products, arithmetic and copies ran while one was open for 0% -> 0% of each run, Pallas kernels for 3% -> 3%
where the time goes in v10:
time: 137 us
  blocking collectives  57.2 us (42%)
  Pallas kernels  33 us (24%)
  starting transfers between devices  29.4 us (21%)
  waiting for transfers between devices  16.2 us (12%)
    all_to_all x2, blocking collectives, gather_all(): got = lax.all_to_all(payload, ('grp', 'box'), 0, 0, tiled=True)  57.2 us
    pallas_call x9, Pallas kernels, call(): pl.pallas_call(kernel, out_shape=[shape_of(i, s) for i, s in enumerate(ou...  33 us
    ppermute x7, starting transfers between devices, ring(): after = lax.ppermute(x[1], axis, [(i, (i - 1) % n) for i in range(n)])  23.7 us
    ppermute x7, waiting for transfers between devices, ring(): before = lax.ppermute(x[0], axis, [(i, (i + 1) % n) for i in range(n)])  9.24 us
    ppermute x7, waiting for transfers between devices, ring(): after = lax.ppermute(x[1], axis, [(i, (i - 1) % n) for i in range(n)])  6.99 us
    ppermute x7, starting transfers between devices, ring(): before = lax.ppermute(x[0], axis, [(i, (i + 1) % n) for i in range(n)])  5.66 us
  transfers between devices with their start and end apart: 14, of which 6 were waited for; matrix products, arithmetic and copies ran while one was open for 0% of the time, Pallas kernels for 3%

profile of v10, /device:TPU:1, one launch (start us, length us, event | category | flops | bytes accessed | tf_op | source)
XLA Modules:
  0.0 136.6 jit_solution(7194135645120488773)
XLA Ops:
  0.6 2.0 %shard_map.59 = (f32[32,32,128]{2,1,0:T(8,128)S(1)}, f32[84,8,128]{2,1,0:T(8,128)S(1)}, f32[84,8,128]{2,1,0:T(8,128)S(1)}, f32[21,32,128]{2,1,0:T(8,128)S(1)}, f...) custom-call(f32[32,32,128]{2,1,0:T(8,128)} %refs_0_.1, s32[32,32,128]{2,1,0:T(8,128)} %tags_hbm.1, f32[8]{0:T(128)} %table_hbm.1, ...), custom_call_target="tpu_custom_call" | custom-call | tf_op jit(solution)/shard_map/pallas_call | solution.py:31
  2.6 2.5 %collective-permute-start.2 = (f32[84,8,128]{2,1,0:T(8,128)S(1)}, f32[84,8,128]{2,1,0:T(8,128)S(1)}, u32[]{:S(2)}, u32[]{:S(2)}) collective-permute-start(f32[84,8,128]{2,1,0:T(8,128)S(1)} %get-tuple-element.53), channel_id=1, source_target_pairs={{0,1},{1,2},{2,3},{3,4},{4,5},{5,6},{6,7},{7,8},{8,9},{9,10},{10,1... | collective-permute-start | bytes 1032200 | tf_op jit(solution)/shard_map/ppermute | solution.py:658
  5.2 6.5 %collective-permute-start.3 = (f32[84,8,128]{2,1,0:T(8,128)S(1)}, f32[84,8,128]{2,1,0:T(8,128)S(1)}, u32[]{:S(2)}, u32[]{:S(2)}) collective-permute-start(f32[84,8,128]{2,1,0:T(8,128)S(1)} %get-tuple-element.54), channel_id=1, source_target_pairs={{0,31},{1,0},{2,1},{3,2},{4,3},{5,4},{6,5},{7,6},{8,7},{9,8},{10,9... | collective-permute-start | bytes 1032200 | tf_op jit(solution)/shard_map/ppermute | solution.py:659
  11.6 1.0 collective-permute-start
  12.6 1.1 collective-permute-start.1
  13.7 5.6 %collective-permute-done.2.above.refs_2_.refs_3_ = f32[84,8,128]{2,1,0:T(8,128)S(1)} collective-permute-done((f32[84,8,128]{2,1,0:T(8,128)S(1)}, f32[84,8,128]{2,1,0:T(8,128)S(1)}, u32[]{:S(2)}, u32[]{:S(2)}) %collective-permute-start.2) | collective-permute-done | bytes 344096 | tf_op jit(solution)/shard_map/ppermute | solution.py:658
  19.3 0.0 collective-permute-done.3.below.refs_3_.refs_4_
  19.4 1.2 collective-permute-start.4
  20.6 1.1 collective-permute-start.5
  21.7 1.2 shard_map.61
  23.0 0.0 collective-permute-done.1.refs_1_.refs_2_
  23.0 3.3 %collective-permute-done.4.refs_2_.refs_5_ = f32[35,16,128]{2,1,0:T(8,128)S(1)} collective-permute-done((f32[35,16,128]{2,1,0:T(8,128)S(1)}, f32[35,16,128]{2,1,0:T(8,128)S(1)}, u32[]{:S(2)}, u32[]{:S(2)}) %collective-permute-start.4) | collective-permute-done | bytes 286752 | tf_op jit(solution)/shard_map/ppermute | solution.py:659
  26.3 0.0 collective-permute-done.5.refs_3_.refs_6_
  26.3 2.8 %shard_map.62 = (f32[48,48,128]{2,1,0:T(8,128)S(1)}, f32[48,48,128]{2,1,0:T(8,128)S(1)}, f32[48,48,128]{2,1,0:T(8,128)S(1)}, f32[48,48,128]{2,1,0:T(8,128)S(1)},...) custom-call(f32[21,32,128]{2,1,0:T(8,128)S(1)} %collective-permute-d, ...), custom_call_target="tpu_custom_call", output_to_operand_aliasing={{0}: (4, {}), {1}: (5, {}), {2}: (6, {}), {3}: (7, {}), {4}... | custom-call | tf_op jit(solution)/shard_map/pallas_call | solution.py:31
  29.1 0.1 collective-permute-start.6
  29.2 4.9 %collective-permute-start.7 = (f32[8,16,128]{2,1,0:T(8,128)S(1)}, f32[8,16,128]{2,1,0:T(8,128)S(1)}, u32[]{:S(2)}, u32[]{:S(2)}) collective-permute-start(f32[8,16,128]{2,1,0:T(8,128)S(1)} %get-tuple-element.66.own), channel_id=1, source_target_pairs={{0,31},{1,0},{2,1},{3,2},{4,3},{5,4},{6,5},{7,6},{8,7},{9,8},{10,9... | collective-permute-start | bytes 196616 | tf_op jit(solution)/shard_map/ppermute | solution.py:659
  34.2 1.6 %collective-permute-done.6.above = f32[8,16,128]{2,1,0:T(8,128)S(1)} collective-permute-done((f32[8,16,128]{2,1,0:T(8,128)S(1)}, f32[8,16,128]{2,1,0:T(8,128)S(1)}, u32[]{:S(2)}, u32[]{:S(2)}) %collective-permute-start.6) | collective-permute-done | bytes 65568 | tf_op jit(solution)/shard_map/ppermute | solution.py:658
  35.8 4.3 %collective-permute-start.8 = (f32[8,48,128]{2,1,0:T(8,128)S(1)}, f32[8,48,128]{2,1,0:T(8,128)S(1)}, u32[]{:S(2)}, u32[]{:S(2)}) collective-permute-start(f32[8,48,128]{2,1,0:T(8,128)S(1)} %constant_dynamic-update-slice_fusion), channel_id=1, source_target_pairs={{0,224},{32,0},{64,32},{96,64},{128,96},{160,128},{192,160},{224,1... | collective-permute-start | bytes 589832 | tf_op jit(solution)/shard_map/ppermute | solution.py:659
  40.0 2.2 %shard_map.63 = (f32[24,48,128]{2,1,0:T(8,128)S(1)}, f32[24,48,128]{2,1,0:T(8,128)S(1)}, f32[24,48,128]{2,1,0:T(8,128)S(1)}, f32[24,48,128]{2,1,0:T(8,128)S(1)},...) custom-call(f32[8,16,128]{2,1,0:T(8,128)S(1)} %get-tuple-element.67., ...), custom_call_target="tpu_custom_call" | custom-call | tf_op jit(solution)/shard_map/pallas_call | solution.py:31
  42.3 0.4 collective-permute-done.9.left
  42.7 2.9 %shard_map.64 = (f32[24,48,128]{2,1,0:T(8,128)S(1)}, f32[24,48,128]{2,1,0:T(8,128)S(1)}, f32[24,24,128]{2,1,0:T(8,128)S(1)}, f32[24,24,128]{2,1,0:T(8,128)S(1)}, f32[256,4,128]{2,1,0:T(4,128)S(1)}) custom-call(f32[8,16,128]{2,1,0:T(8,128)S(1)} %get-tuple-element.66.own, f32[8,48,128]{2,1,0:T(8,128)S(1)} %collective-permute-done.8.right, ...), custom_call_target="tpu_custom_call" | custom-call | tf_op jit(solution)/shard_map/pallas_call | solution.py:31
  45.6 32.1 %all_to_all.10 = f32[256,4,128]{2,1,0:T(4,128)S(1)} all-to-all(f32[256,4,128]{2,1,0:T(4,128)S(1)} %get-tuple-element.77), channel_id=1, replica_groups=mesh['grp'=8,'box'=32] {'grp','box'}, dimensions={0} | all-to-all | bytes 1048576 | tf_op jit(solution)/shard_map/all_to_all | solution.py:675
  77.6 10.0 %shard_map.65 = (f32[48,48,128]{2,1,0:T(8,128)S(1)}, f32[8,16,128]{2,1,0:T(8,128)S(1)}, f32[40,16,128]{2,1,0:T(8,128)S(1)}, f32[40,16,128]{2,1,0:T(8,128)S(1)}, ...) custom-call(f32[1024,128]{1,0:T(8,128)S(1)} %bitcast.2, ...), custom_call_target="tpu_custom_call", output_to_operand_aliasing={{0}: (16, {})} | custom-call | tf_op jit(solution)/shard_map/pallas_call | solution.py:31
  87.7 0.6 collective-permute-start.10
  88.3 4.3 %collective-permute-start.11 = (f32[8,16,128]{2,1,0:T(8,128)S(1)}, f32[8,16,128]{2,1,0:T(8,128)S(1)}, u32[]{:S(2)}, u32[]{:S(2)}) collective-permute-start(f32[8,16,128]{2,1,0:T(8,128)S(1)} %get-tuple-element.88.own), channel_id=1, source_target_pairs={{0,31},{1,0},{2,1},{3,2},{4,3},{5,4},{6,5},{7,6},{8,7},{9,8},{10,9... | collective-permute-start | bytes 196616 | tf_op jit(solution)/shard_map/ppermute | solution.py:659
  92.5 1.6 %collective-permute-done.10.above = f32[8,16,128]{2,1,0:T(8,128)S(1)} collective-permute-done((f32[8,16,128]{2,1,0:T(8,128)S(1)}, f32[8,16,128]{2,1,0:T(8,128)S(1)}, u32[]{:S(2)}, u32[]{:S(2)}) %collective-permute-start.10) | collective-permute-done | bytes 65568 | tf_op jit(solution)/shard_map/ppermute | solution.py:658
  94.2 1.6 %collective-permute-start.12 = (f32[8,48,128]{2,1,0:T(8,128)S(1)}, f32[8,48,128]{2,1,0:T(8,128)S(1)}, u32[]{:S(2)}, u32[]{:S(2)}) collective-permute-start(f32[8,48,128]{2,1,0:T(8,128)S(1)} %constant_dynamic-update-slice_fusion.3), channel_id=1, source_target_pairs={{0,224},{32,0},{64,32},{96,64},{128,96},{160,128},{192,160},{224,1... | collective-permute-start | bytes 589832 | tf_op jit(solution)/shard_map/ppermute | solution.py:659
  95.8 0.2 collective-permute-start.13
  96.0 3.6 %collective-permute-done.12.right = f32[8,48,128]{2,1,0:T(8,128)S(1)} collective-permute-done((f32[8,48,128]{2,1,0:T(8,128)S(1)}, f32[8,48,128]{2,1,0:T(8,128)S(1)}, u32[]{:S(2)}, u32[]{:S(2)}) %collective-permute-start.12) | collective-permute-done | bytes 196640 | tf_op jit(solution)/shard_map/ppermute | solution.py:659
  99.6 3.0 %shard_map.66 = (f32[24,48,128]{2,1,0:T(8,128)S(1)}, f32[24,48,128]{2,1,0:T(8,128)S(1)}, f32[24,24,128]{2,1,0:T(8,128)S(1)}, f32[24,24,128]{2,1,0:T(8,128)S(1)}, f32[256,2,128]{2,1,0:T(2,128)S(1)}) custom-call(f32[8,16,128]{2,1,0:T(8,128)S(1)} %get-tuple-element.88.own, f32[8,48,128]{2,1,0:T(8,128)S(1)} %collective-permute-done.12.right, ...), custom_call_target="tpu_custom_call" | custom-call | tf_op jit(solution)/shard_map/pallas_call | solution.py:31
  102.6 25.1 %all_to_all.11 = f32[256,2,128]{2,1,0:T(2,128)S(1)} all-to-all(f32[256,2,128]{2,1,0:T(2,128)S(1)} %get-tuple-element.89), channel_id=1, replica_groups=mesh['grp'=8,'box'=32] {'grp','box'}, dimensions={0} | all-to-all | bytes 524288 | tf_op jit(solution)/shard_map/all_to_all | solution.py:675
  127.8 8.8 %shard_map.67 = (f32[32,32,128]{2,1,0:T(8,128)}, f32[32,32,128]{2,1,0:T(8,128)}) custom-call(f32[512,128]{1,0:T(8,128)S(1)} %bitcast.3, f32[40,16,128]{2,1,0:T(8,128)S(1)} %get-tuple-element.90.refs_1_, f32[40,16,128]{2,1,0:T(8,128)S(1)} %get-tuple-element.91.refs_2_, f32[40,16,128]{2,1,0:T(8,128)S(1)} %get-tuple-element.92.refs_3_, ...), custom_call_target="tpu_custom_call" | custom-call | tf_op jit(solution)/shard_map/pallas_call | solution.py:31
  (15 shorter events, 0.1 us)
Async XLA Ops:
  0.6 21.1 %copy-start = (f32[32,32,128]{2,1,0:T(8,128)S(1)}, f32[32,32,128]{2,1,0:T(8,128)}, u32[]{:S(2)}) copy-start(f32[32,32,128]{2,1,0:T(8,128)} %refs_0_.1) | copy-start | bytes 1572868
  2.6 16.7 %collective-permute-start.2 = (f32[84,8,128]{2,1,0:T(8,128)S(1)}, f32[84,8,128]{2,1,0:T(8,128)S(1)}, u32[]{:S(2)}, u32[]{:S(2)}) collective-permute-start(f32[84,8,128]{2,1,0:T(8,128)S(1)} %get-tuple-element.53), channel_id=1, source_target_pairs={{0,1},{1,2},{2,3},{3,4},{4,5},{5,6},{6,7},{7,8},{8,9},{9,10},{10,1... | collective-permute-start | bytes 1032200 | tf_op jit(solution)/shard_map/ppermute | solution.py:658
  5.2 14.2 %collective-permute-start.3 = (f32[84,8,128]{2,1,0:T(8,128)S(1)}, f32[84,8,128]{2,1,0:T(8,128)S(1)}, u32[]{:S(2)}, u32[]{:S(2)}) collective-permute-start(f32[84,8,128]{2,1,0:T(8,128)S(1)} %get-tuple-element.54), channel_id=1, source_target_pairs={{0,31},{1,0},{2,1},{3,2},{4,3},{5,4},{6,5},{7,6},{8,7},{9,8},{10,9... | collective-permute-start | bytes 1032200 | tf_op jit(solution)/shard_map/ppermute | solution.py:659
  11.6 11.3 %collective-permute-start = (f32[21,32,128]{2,1,0:T(8,128)S(1)}, f32[21,32,128]{2,1,0:T(8,128)S(1)}, u32[]{:S(2)}, u32[]{:S(2)}) collective-permute-start(f32[21,32,128]{2,1,0:T(8,128)S(1)} %get-tuple-element.51), channel_id=1, source_target_pairs={{0,224},{32,0},{64,32},{96,64},{128,96},{160,128},{192,160},{224,1... | collective-permute-start | bytes 1032200 | tf_op jit(solution)/shard_map/ppermute | solution.py:659
  12.6 10.4 %collective-permute-start.1 = (f32[21,32,128]{2,1,0:T(8,128)S(1)}, f32[21,32,128]{2,1,0:T(8,128)S(1)}, u32[]{:S(2)}, u32[]{:S(2)}) collective-permute-start(f32[21,32,128]{2,1,0:T(8,128)S(1)} %get-tuple-element.52), channel_id=1, source_target_pairs={{0,32},{32,64},{64,96},{96,128},{128,160},{160,192},{192,224},{224... | collective-permute-start | bytes 1032200 | tf_op jit(solution)/shard_map/ppermute | solution.py:658
  19.4 7.0 %collective-permute-start.4 = (f32[35,16,128]{2,1,0:T(8,128)S(1)}, f32[35,16,128]{2,1,0:T(8,128)S(1)}, u32[]{:S(2)}, u32[]{:S(2)}) collective-permute-start(f32[35,16,128]{2,1,0:T(8,128)S(1)} %get-tuple-element.55), channel_id=1, source_target_pairs={{0,224},{32,0},{64,32},{96,64},{128,96},{160,128},{192,160},{224,1... | collective-permute-start | bytes 860168 | tf_op jit(solution)/shard_map/ppermute | solution.py:659
  20.6 5.7 %collective-permute-start.5 = (f32[35,16,128]{2,1,0:T(8,128)S(1)}, f32[35,16,128]{2,1,0:T(8,128)S(1)}, u32[]{:S(2)}, u32[]{:S(2)}) collective-permute-start(f32[35,16,128]{2,1,0:T(8,128)S(1)} %get-tuple-element.56), channel_id=1, source_target_pairs={{0,32},{32,64},{64,96},{96,128},{128,160},{160,192},{192,224},{224... | collective-permute-start | bytes 860168 | tf_op jit(solution)/shard_map/ppermute | solution.py:658
  29.1 6.6 %collective-permute-start.6 = (f32[8,16,128]{2,1,0:T(8,128)S(1)}, f32[8,16,128]{2,1,0:T(8,128)S(1)}, u32[]{:S(2)}, u32[]{:S(2)}) collective-permute-start(f32[8,16,128]{2,1,0:T(8,128)S(1)} %get-tuple-element.66.own), channel_id=1, source_target_pairs={{0,1},{1,2},{2,3},{3,4},{4,5},{5,6},{6,7},{7,8},{8,9},{9,10},{10,1... | collective-permute-start | bytes 196616 | tf_op jit(solution)/shard_map/ppermute | solution.py:658
  29.2 6.5 %collective-permute-start.7 = (f32[8,16,128]{2,1,0:T(8,128)S(1)}, f32[8,16,128]{2,1,0:T(8,128)S(1)}, u32[]{:S(2)}, u32[]{:S(2)}) collective-permute-start(f32[8,16,128]{2,1,0:T(8,128)S(1)} %get-tuple-element.66.own), channel_id=1, source_target_pairs={{0,31},{1,0},{2,1},{3,2},{4,3},{5,4},{6,5},{7,6},{8,7},{9,8},{10,9... | collective-permute-start | bytes 196616 | tf_op jit(solution)/shard_map/ppermute | solution.py:659
  35.8 6.5 %collective-permute-start.8 = (f32[8,48,128]{2,1,0:T(8,128)S(1)}, f32[8,48,128]{2,1,0:T(8,128)S(1)}, u32[]{:S(2)}, u32[]{:S(2)}) collective-permute-start(f32[8,48,128]{2,1,0:T(8,128)S(1)} %constant_dynamic-update-slice_fusion), channel_id=1, source_target_pairs={{0,224},{32,0},{64,32},{96,64},{128,96},{160,128},{192,160},{224,1... | collective-permute-start | bytes 589832 | tf_op jit(solution)/shard_map/ppermute | solution.py:659
  40.0 2.6 %collective-permute-start.9 = (f32[8,48,128]{2,1,0:T(8,128)S(1)}, f32[8,48,128]{2,1,0:T(8,128)S(1)}, u32[]{:S(2)}, u32[]{:S(2)}) collective-permute-start(f32[8,48,128]{2,1,0:T(8,128)S(1)} %constant_dynamic-update-slice_fusion), channel_id=1, source_target_pairs={{0,32},{32,64},{64,96},{96,128},{128,160},{160,192},{192,224},{224... | collective-permute-start | bytes 589832 | tf_op jit(solution)/shard_map/ppermute | solution.py:658
  87.7 6.5 %collective-permute-start.10 = (f32[8,16,128]{2,1,0:T(8,128)S(1)}, f32[8,16,128]{2,1,0:T(8,128)S(1)}, u32[]{:S(2)}, u32[]{:S(2)}) collective-permute-start(f32[8,16,128]{2,1,0:T(8,128)S(1)} %get-tuple-element.88.own), channel_id=1, source_target_pairs={{0,1},{1,2},{2,3},{3,4},{4,5},{5,6},{6,7},{7,8},{8,9},{9,10},{10,1... | collective-permute-start | bytes 196616 | tf_op jit(solution)/shard_map/ppermute | solution.py:658
  88.3 5.9 %collective-permute-start.11 = (f32[8,16,128]{2,1,0:T(8,128)S(1)}, f32[8,16,128]{2,1,0:T(8,128)S(1)}, u32[]{:S(2)}, u32[]{:S(2)}) collective-permute-start(f32[8,16,128]{2,1,0:T(8,128)S(1)} %get-tuple-element.88.own), channel_id=1, source_target_pairs={{0,31},{1,0},{2,1},{3,2},{4,3},{5,4},{6,5},{7,6},{8,7},{9,8},{10,9... | collective-permute-start | bytes 196616 | tf_op jit(solution)/shard_map/ppermute | solution.py:659
  94.2 5.4 %collective-permute-start.12 = (f32[8,48,128]{2,1,0:T(8,128)S(1)}, f32[8,48,128]{2,1,0:T(8,128)S(1)}, u32[]{:S(2)}, u32[]{:S(2)}) collective-permute-start(f32[8,48,128]{2,1,0:T(8,128)S(1)} %constant_dynamic-update-slice_fusion.3), channel_id=1, source_target_pairs={{0,224},{32,0},{64,32},{96,64},{128,96},{160,128},{192,160},{224,1... | collective-permute-start | bytes 589832 | tf_op jit(solution)/shard_map/ppermute | solution.py:659
  95.8 3.8 %collective-permute-start.13 = (f32[8,48,128]{2,1,0:T(8,128)S(1)}, f32[8,48,128]{2,1,0:T(8,128)S(1)}, u32[]{:S(2)}, u32[]{:S(2)}) collective-permute-start(f32[8,48,128]{2,1,0:T(8,128)S(1)} %constant_dynamic-update-slice_fusion.3), channel_id=1, source_target_pairs={{0,32},{32,64},{64,96},{96,128},{128,160},{160,192},{192,224},{224... | collective-permute-start | bytes 589832 | tf_op jit(solution)/shard_map/ppermute | solution.py:658

commit v11 on v10

--- a/solution.py
+++ b/solution.py
@@ -334,11 +334,11 @@
     return (dot(even, halver_at(0)) + dot(odd, halver_at(1))).reshape(8, 16, 128)
 
 
-def assemble(dst, own, left, right, above, below):
+def assemble(dst, own, right, left, above, below, corner_right, corner_left):
     for i in range(8):
-        dst[i] = left[i]
         dst[8 + i] = jnp.concatenate([above[i], own[i], below[i]], 0)
-        dst[16 + i] = right[i]
+        for at, side, corner in ((0, left, corner_left), (16, right, corner_right)):
+            dst[at + i] = jnp.concatenate([corner[i, 0:16], side[i], corner[i, 16:32]], 0)
 
 
 def edge_flags(ng, nb):
@@ -453,19 +453,21 @@
 
 
 def mid_kernel(
-    own, right, left, above, below, wx1, ws1, wl1, di1, wx2, ws2, wl2, di2, coarser,
+    own, right, left, above, below, corner_right, corner_left,
+    wx1, ws1, wl1, di1, wx2, ws2, wl2, di2, coarser,
     f1, v1, f2, v2, payload, s,
 ):
-    assemble(f1, own, left, right, above, below)
+    assemble(f1, own, right, left, above, below, corner_right, corner_left)
     op1, op2 = (wx1, ws1, wl1, di1), (wx2, ws2, wl2, di2)
     mid_down(f1, v1, op1, f2, v2, op2, s, payload, coarser[...])
 
 
 def mid2_kernel(
-    own, right, left, above, below, wx1, ws1, wl1, di1, wx2, ws2, wl2, di2,
+    own, right, left, above, below, corner_right, corner_left,
+    wx1, ws1, wl1, di1, wx2, ws2, wl2, di2,
     f1, v1, f2, v2, payload, s,
 ):
-    assemble(f1, own, left, right, above, below)
+    assemble(f1, own, right, left, above, below, corner_right, corner_left)
     op1, op2 = (wx1, ws1, wl1, di1), (wx2, ws2, wl2, di2)
     mid_down(f1, v1, op1, f2, v2, op2, s, payload, None)
 
@@ -660,15 +662,13 @@
     return before, after
 
 
-def tall_of(packed, nb):
+def around(packed, ng, nb):
     above, below = ring((packed, packed), "box", nb)
-    return above, below, jnp.concatenate([above, packed, below], 1)
-
-
-def around(packed, ng, nb):
-    above, below, tall = tall_of(packed, nb)
-    left, right = ring((tall, tall), "grp", ng)
-    return packed, right, left, above, below
+    left, right = ring((packed, packed), "grp", ng)
+    above, below, left, right = lax.optimization_barrier((above, below, left, right))
+    corners = jnp.concatenate([above, below], 1)
+    corner_left, corner_right = ring((corners, corners), "grp", ng)
+    return packed, right, left, above, below, corner_right, corner_left
 
 
 def gather_all(payload):

time: 137 us -> 142 us (1.036)
  starting transfers between devices: 29.4 us -> 32.8 us
  waiting for transfers between devices: 16.2 us -> 19.3 us
    ppermute x7 -> x9, starting transfers between devices: 5.66 us -> 9.45 us  [ring(): before = lax.ppermute(x[0], axis, [(i, (i + 1) % n) for i in range(n)])]
    ppermute x7 -> x9, waiting for transfers between devices: 6.99 us -> 9.87 us  [ring(): after = lax.ppermute(x[1], axis, [(i, (i - 1) % n) for i in range(n)])]
    ppermute x7 -> x9, starting transfers between devices: 23.7 us -> 23.3 us  [ring(): after = lax.ppermute(x[1], axis, [(i, (i - 1) % n) for i in range(n)])]
    ppermute x7 -> x9, waiting for transfers between devices: 9.24 us -> 9.39 us  [ring(): before = lax.ppermute(x[0], axis, [(i, (i + 1) % n) for i in range(n)])]
  transfers between devices with their start and end apart: 14 -> 18, of which waited for: 6 -> 10; matrix products, arithmetic and copies ran while one was open for 0% -> 0% of each run, Pallas kernels for 3% -> 2%
where the time goes in v11:
time: 142 us
  blocking collectives  56.3 us (40%)
  Pallas kernels  33 us (23%)
  starting transfers between devices  32.8 us (23%)
  waiting for transfers between devices  19.3 us (14%)
    all_to_all x2, blocking collectives, gather_all(): got = lax.all_to_all(payload, ('grp', 'box'), 0, 0, tiled=True)  56.3 us
    pallas_call x9, Pallas kernels, call(): pl.pallas_call(kernel, out_shape=[shape_of(i, s) for i, s in enumerate(ou...  33 us
    ppermute x9, starting transfers between devices, ring(): after = lax.ppermute(x[1], axis, [(i, (i - 1) % n) for i in range(n)])  23.3 us
    ppermute x9, waiting for transfers between devices, ring(): after = lax.ppermute(x[1], axis, [(i, (i - 1) % n) for i in range(n)])  9.87 us
    ppermute x9, starting transfers between devices, ring(): before = lax.ppermute(x[0], axis, [(i, (i + 1) % n) for i in range(n)])  9.45 us
    ppermute x9, waiting for transfers between devices, ring(): before = lax.ppermute(x[0], axis, [(i, (i + 1) % n) for i in range(n)])  9.39 us
  transfers between devices with their start and end apart: 18, of which 10 were waited for; matrix products, arithmetic and copies ran while one was open for 0% of the time, Pallas kernels for 2%

profile of v11, /device:TPU:1, one launch (start us, length us, event | category | flops | bytes accessed | tf_op | source)
XLA Modules:
  0.0 142.1 jit_solution(13727016450687311260)
XLA Ops:
  0.6 2.0 %shard_map.59 = (f32[32,32,128]{2,1,0:T(8,128)S(1)}, f32[84,8,128]{2,1,0:T(8,128)S(1)}, f32[84,8,128]{2,1,0:T(8,128)S(1)}, f32[21,32,128]{2,1,0:T(8,128)S(1)}, f...) custom-call(f32[32,32,128]{2,1,0:T(8,128)} %refs_0_.1, s32[32,32,128]{2,1,0:T(8,128)} %tags_hbm.1, f32[8]{0:T(128)} %table_hbm.1, ...), custom_call_target="tpu_custom_call" | custom-call | tf_op jit(solution)/shard_map/pallas_call | solution.py:31
  2.6 2.5 %collective-permute-start.2 = (f32[84,8,128]{2,1,0:T(8,128)S(1)}, f32[84,8,128]{2,1,0:T(8,128)S(1)}, u32[]{:S(2)}, u32[]{:S(2)}) collective-permute-start(f32[84,8,128]{2,1,0:T(8,128)S(1)} %get-tuple-element.61), channel_id=1, source_target_pairs={{0,1},{1,2},{2,3},{3,4},{4,5},{5,6},{6,7},{7,8},{8,9},{9,10},{10,1... | collective-permute-start | bytes 1032200 | tf_op jit(solution)/shard_map/ppermute | solution.py:660
  5.2 6.5 %collective-permute-start.3 = (f32[84,8,128]{2,1,0:T(8,128)S(1)}, f32[84,8,128]{2,1,0:T(8,128)S(1)}, u32[]{:S(2)}, u32[]{:S(2)}) collective-permute-start(f32[84,8,128]{2,1,0:T(8,128)S(1)} %get-tuple-element.62), channel_id=1, source_target_pairs={{0,31},{1,0},{2,1},{3,2},{4,3},{5,4},{6,5},{7,6},{8,7},{9,8},{10,9... | collective-permute-start | bytes 1032200 | tf_op jit(solution)/shard_map/ppermute | solution.py:661
  11.6 1.0 collective-permute-start
  12.6 1.1 collective-permute-start.1
  13.7 5.6 %collective-permute-done.2.above.refs_2_.refs_3_ = f32[84,8,128]{2,1,0:T(8,128)S(1)} collective-permute-done((f32[84,8,128]{2,1,0:T(8,128)S(1)}, f32[84,8,128]{2,1,0:T(8,128)S(1)}, u32[]{:S(2)}, u32[]{:S(2)}) %collective-permute-start.2) | collective-permute-done | bytes 344096 | tf_op jit(solution)/shard_map/ppermute | solution.py:660
  19.4 1.2 collective-permute-start.4
  20.6 1.1 collective-permute-start.5
  21.7 1.2 shard_map.61
  23.0 3.3 %collective-permute-done.4.refs_2_.refs_5_ = f32[35,16,128]{2,1,0:T(8,128)S(1)} collective-permute-done((f32[35,16,128]{2,1,0:T(8,128)S(1)}, f32[35,16,128]{2,1,0:T(8,128)S(1)}, u32[]{:S(2)}, u32[]{:S(2)}) %collective-permute-start.4) | collective-permute-done | bytes 286752 | tf_op jit(solution)/shard_map/ppermute | solution.py:661
  26.3 2.8 %shard_map.62 = (f32[48,48,128]{2,1,0:T(8,128)S(1)}, f32[48,48,128]{2,1,0:T(8,128)S(1)}, f32[48,48,128]{2,1,0:T(8,128)S(1)}, f32[48,48,128]{2,1,0:T(8,128)S(1)},...) custom-call(f32[21,32,128]{2,1,0:T(8,128)S(1)} %collective-permute-d, ...), custom_call_target="tpu_custom_call", output_to_operand_aliasing={{0}: (4, {}), {1}: (5, {}), {2}: (6, {}), {3}: (7, {}), {4}... | custom-call | tf_op jit(solution)/shard_map/pallas_call | solution.py:31
  29.2 4.9 %collective-permute-start.7 = (f32[8,16,128]{2,1,0:T(8,128)S(1)}, f32[8,16,128]{2,1,0:T(8,128)S(1)}, u32[]{:S(2)}, u32[]{:S(2)}) collective-permute-start(f32[8,16,128]{2,1,0:T(8,128)S(1)} %get-tuple-element.74.own), channel_id=1, source_target_pairs={{0,31},{1,0},{2,1},{3,2},{4,3},{5,4},{6,5},{7,6},{8,7},{9,8},{10,9... | collective-permute-start | bytes 196616 | tf_op jit(solution)/shard_map/ppermute | solution.py:661
  34.2 1.9 %collective-permute-start.8 = (f32[8,16,128]{2,1,0:T(8,128)S(1)}, f32[8,16,128]{2,1,0:T(8,128)S(1)}, u32[]{:S(2)}, u32[]{:S(2)}) collective-permute-start(f32[8,16,128]{2,1,0:T(8,128)S(1)} %get-tuple-element.74.own), channel_id=1, source_target_pairs={{0,32},{32,64},{64,96},{96,128},{128,160},{160,192},{192,224},{224... | collective-permute-start | bytes 196616 | tf_op jit(solution)/shard_map/ppermute | solution.py:660
  36.0 1.7 %collective-permute-start.9 = (f32[8,16,128]{2,1,0:T(8,128)S(1)}, f32[8,16,128]{2,1,0:T(8,128)S(1)}, u32[]{:S(2)}, u32[]{:S(2)}) collective-permute-start(f32[8,16,128]{2,1,0:T(8,128)S(1)} %get-tuple-element.74.own), channel_id=1, source_target_pairs={{0,224},{32,0},{64,32},{96,64},{128,96},{160,128},{192,160},{224,1... | collective-permute-start | bytes 196616 | tf_op jit(solution)/shard_map/ppermute | solution.py:661
  37.8 0.7 collective-permute-done.8.left
  38.5 1.2 collective-permute-done.9.right
  39.7 3.0 %collective-permute-start.10 = (f32[8,32,128]{2,1,0:T(8,128)S(1)}, f32[8,32,128]{2,1,0:T(8,128)S(1)}, u32[]{:S(2)}, u32[]{:S(2)}) collective-permute-start(f32[8,32,128]{2,1,0:T(8,128)S(1)} %constant_dynamic-update-slice_fusion), channel_id=1, source_target_pairs={{0,224},{32,0},{64,32},{96,64},{128,96},{160,128},{192,160},{224,1... | collective-permute-start | bytes 393224 | tf_op jit(solution)/shard_map/ppermute | solution.py:661
  42.7 2.2 %shard_map.63 = (f32[24,48,128]{2,1,0:T(8,128)S(1)}, f32[24,48,128]{2,1,0:T(8,128)S(1)}, f32[24,48,128]{2,1,0:T(8,128)S(1)}, f32[24,48,128]{2,1,0:T(8,128)S(1)},...) custom-call(f32[8,16,128]{2,1,0:T(8,128)S(1)} %get-tuple-element.79., ...), custom_call_target="tpu_custom_call" | custom-call | tf_op jit(solution)/shard_map/pallas_call | solution.py:31
  44.9 1.5 %collective-permute-done.11.corner_left = f32[8,32,128]{2,1,0:T(8,128)S(1)} collective-permute-done((f32[8,32,128]{2,1,0:T(8,128)S(1)}, f32[8,32,128]{2,1,0:T(8,128)S(1)}, u32[]{:S(2)}, u32[]{:S(2)}) %collective-permute-start.11) | collective-permute-done | bytes 131104 | tf_op jit(solution)/shard_map/ppermute | solution.py:660
  46.5 2.9 %shard_map.64 = (f32[24,48,128]{2,1,0:T(8,128)S(1)}, f32[24,48,128]{2,1,0:T(8,128)S(1)}, f32[24,24,128]{2,1,0:T(8,128)S(1)}, f32[24,24,128]{2,1,0:T(8,128)S(1)}, f32[256,4,128]{2,1,0:T(4,128)S(1)}) custom-call(f32[8,16,128]{2,1,0:T(8,128)S(1)} %get-tuple-element.74.own, f32[8,16,128]{2,1,0:T(8,128)S(1)} %collective-permute-done.9.right, ...), custom_call_target="tpu_custom_call" | custom-call | tf_op jit(solution)/shard_map/pallas_call | solution.py:31
  49.4 31.0 %all_to_all.10 = f32[256,4,128]{2,1,0:T(4,128)S(1)} all-to-all(f32[256,4,128]{2,1,0:T(4,128)S(1)} %get-tuple-element.89), channel_id=1, replica_groups=mesh['grp'=8,'box'=32] {'grp','box'}, dimensions={0} | all-to-all | bytes 1048576 | tf_op jit(solution)/shard_map/all_to_all | solution.py:675
  80.4 10.0 %shard_map.65 = (f32[48,48,128]{2,1,0:T(8,128)S(1)}, f32[8,16,128]{2,1,0:T(8,128)S(1)}, f32[40,16,128]{2,1,0:T(8,128)S(1)}, f32[40,16,128]{2,1,0:T(8,128)S(1)}, ...) custom-call(f32[1024,128]{1,0:T(8,128)S(1)} %bitcast.2, ...), custom_call_target="tpu_custom_call", output_to_operand_aliasing={{0}: (16, {})} | custom-call | tf_op jit(solution)/shard_map/pallas_call | solution.py:31
  91.0 4.3 %collective-permute-start.13 = (f32[8,16,128]{2,1,0:T(8,128)S(1)}, f32[8,16,128]{2,1,0:T(8,128)S(1)}, u32[]{:S(2)}, u32[]{:S(2)}) collective-permute-start(f32[8,16,128]{2,1,0:T(8,128)S(1)} %get-tuple-element.100.own), channel_id=1, source_target_pairs={{0,31},{1,0},{2,1},{3,2},{4,3},{5,4},{6,5},{7,6},{8,7},{9,8},{10,9... | collective-permute-start | bytes 196616 | tf_op jit(solution)/shard_map/ppermute | solution.py:661
  95.3 1.1 collective-permute-start.14
  96.9 0.8 collective-permute-done.14.left
  97.7 2.7 %collective-permute-done.15.right = f32[8,16,128]{2,1,0:T(8,128)S(1)} collective-permute-done((f32[8,16,128]{2,1,0:T(8,128)S(1)}, f32[8,16,128]{2,1,0:T(8,128)S(1)}, u32[]{:S(2)}, u32[]{:S(2)}) %collective-permute-start.15) | collective-permute-done | bytes 65568 | tf_op jit(solution)/shard_map/ppermute | solution.py:661
  100.4 0.8 collective-permute-start.16
  101.2 1.0 collective-permute-start.17
  102.2 2.6 %collective-permute-done.16.corner_right = f32[8,32,128]{2,1,0:T(8,128)S(1)} collective-permute-done((f32[8,32,128]{2,1,0:T(8,128)S(1)}, f32[8,32,128]{2,1,0:T(8,128)S(1)}, u32[]{:S(2)}, u32[]{:S(2)}) %collective-permute-start.16) | collective-permute-done | bytes 131104 | tf_op jit(solution)/shard_map/ppermute | solution.py:661
  105.0 3.0 %shard_map.66 = (f32[24,48,128]{2,1,0:T(8,128)S(1)}, f32[24,48,128]{2,1,0:T(8,128)S(1)}, f32[24,24,128]{2,1,0:T(8,128)S(1)}, f32[24,24,128]{2,1,0:T(8,128)S(1)}, f32[256,2,128]{2,1,0:T(2,128)S(1)}) custom-call(f32[8,16,128]{2,1,0:T(8,128)S(1)} %get-tuple-element.100.own, f32[8,16,128]{2,1,0:T(8,128)S(1)} %collective-permute-done.15.right, ...), custom_call_target="tpu_custom_call" | custom-call | tf_op jit(solution)/shard_map/pallas_call | solution.py:31
  107.9 25.3 %all_to_all.11 = f32[256,2,128]{2,1,0:T(2,128)S(1)} all-to-all(f32[256,2,128]{2,1,0:T(2,128)S(1)} %get-tuple-element.105), channel_id=1, replica_groups=mesh['grp'=8,'box'=32] {'grp','box'}, dimensions={0} | all-to-all | bytes 524288 | tf_op jit(solution)/shard_map/all_to_all | solution.py:675
  133.2 8.8 %shard_map.67 = (f32[32,32,128]{2,1,0:T(8,128)}, f32[32,32,128]{2,1,0:T(8,128)}) custom-call(f32[512,128]{1,0:T(8,128)S(1)} %bitcast.3, f32[40,16,128]{2,1,0:T(8,128)S(1)} %get-tuple-element.106.refs_1_, f32[40,16,128]{2,1,0:T(8,128)S(1)} %get-tuple-element.107.refs_2_, f32[40,16,128]{2,1,0:T(8,128)S(1)} %get-tuple-element.108.refs_3_, ...), custom_call_target="tpu_custom_call" | custom-call | tf_op jit(solution)/shard_map/pallas_call | solution.py:31
  (21 shorter events, 1.4 us)
Async XLA Ops:
  0.6 21.1 %copy-start = (f32[32,32,128]{2,1,0:T(8,128)S(1)}, f32[32,32,128]{2,1,0:T(8,128)}, u32[]{:S(2)}) copy-start(f32[32,32,128]{2,1,0:T(8,128)} %refs_0_.1) | copy-start | bytes 1572868
  2.6 16.7 %collective-permute-start.2 = (f32[84,8,128]{2,1,0:T(8,128)S(1)}, f32[84,8,128]{2,1,0:T(8,128)S(1)}, u32[]{:S(2)}, u32[]{:S(2)}) collective-permute-start(f32[84,8,128]{2,1,0:T(8,128)S(1)} %get-tuple-element.61), channel_id=1, source_target_pairs={{0,1},{1,2},{2,3},{3,4},{4,5},{5,6},{6,7},{7,8},{8,9},{9,10},{10,1... | collective-permute-start | bytes 1032200 | tf_op jit(solution)/shard_map/ppermute | solution.py:660
  5.2 14.2 %collective-permute-start.3 = (f32[84,8,128]{2,1,0:T(8,128)S(1)}, f32[84,8,128]{2,1,0:T(8,128)S(1)}, u32[]{:S(2)}, u32[]{:S(2)}) collective-permute-start(f32[84,8,128]{2,1,0:T(8,128)S(1)} %get-tuple-element.62), channel_id=1, source_target_pairs={{0,31},{1,0},{2,1},{3,2},{4,3},{5,4},{6,5},{7,6},{8,7},{9,8},{10,9... | collective-permute-start | bytes 1032200 | tf_op jit(solution)/shard_map/ppermute | solution.py:661
  11.6 11.3 %collective-permute-start = (f32[21,32,128]{2,1,0:T(8,128)S(1)}, f32[21,32,128]{2,1,0:T(8,128)S(1)}, u32[]{:S(2)}, u32[]{:S(2)}) collective-permute-start(f32[21,32,128]{2,1,0:T(8,128)S(1)} %get-tuple-element.59), channel_id=1, source_target_pairs={{0,224},{32,0},{64,32},{96,64},{128,96},{160,128},{192,160},{224,1... | collective-permute-start | bytes 1032200 | tf_op jit(solution)/shard_map/ppermute | solution.py:661
  12.6 10.4 %collective-permute-start.1 = (f32[21,32,128]{2,1,0:T(8,128)S(1)}, f32[21,32,128]{2,1,0:T(8,128)S(1)}, u32[]{:S(2)}, u32[]{:S(2)}) collective-permute-start(f32[21,32,128]{2,1,0:T(8,128)S(1)} %get-tuple-element.60), channel_id=1, source_target_pairs={{0,32},{32,64},{64,96},{96,128},{128,160},{160,192},{192,224},{224... | collective-permute-start | bytes 1032200 | tf_op jit(solution)/shard_map/ppermute | solution.py:660
  19.4 7.0 %collective-permute-start.4 = (f32[35,16,128]{2,1,0:T(8,128)S(1)}, f32[35,16,128]{2,1,0:T(8,128)S(1)}, u32[]{:S(2)}, u32[]{:S(2)}) collective-permute-start(f32[35,16,128]{2,1,0:T(8,128)S(1)} %get-tuple-element.63), channel_id=1, source_target_pairs={{0,224},{32,0},{64,32},{96,64},{128,96},{160,128},{192,160},{224,1... | collective-permute-start | bytes 860168 | tf_op jit(solution)/shard_map/ppermute | solution.py:661
  20.6 5.7 %collective-permute-start.5 = (f32[35,16,128]{2,1,0:T(8,128)S(1)}, f32[35,16,128]{2,1,0:T(8,128)S(1)}, u32[]{:S(2)}, u32[]{:S(2)}) collective-permute-start(f32[35,16,128]{2,1,0:T(8,128)S(1)} %get-tuple-element.64), channel_id=1, source_target_pairs={{0,32},{32,64},{64,96},{96,128},{128,160},{160,192},{192,224},{224... | collective-permute-start | bytes 860168 | tf_op jit(solution)/shard_map/ppermute | solution.py:660
  29.1 8.6 %collective-permute-start.6 = (f32[8,16,128]{2,1,0:T(8,128)S(1)}, f32[8,16,128]{2,1,0:T(8,128)S(1)}, u32[]{:S(2)}, u32[]{:S(2)}) collective-permute-start(f32[8,16,128]{2,1,0:T(8,128)S(1)} %get-tuple-element.74.own), channel_id=1, source_target_pairs={{0,1},{1,2},{2,3},{3,4},{4,5},{5,6},{6,7},{7,8},{8,9},{9,10},{10,1... | collective-permute-start | bytes 196616 | tf_op jit(solution)/shard_map/ppermute | solution.py:660
  29.2 8.5 %collective-permute-start.7 = (f32[8,16,128]{2,1,0:T(8,128)S(1)}, f32[8,16,128]{2,1,0:T(8,128)S(1)}, u32[]{:S(2)}, u32[]{:S(2)}) collective-permute-start(f32[8,16,128]{2,1,0:T(8,128)S(1)} %get-tuple-element.74.own), channel_id=1, source_target_pairs={{0,31},{1,0},{2,1},{3,2},{4,3},{5,4},{6,5},{7,6},{8,7},{9,8},{10,9... | collective-permute-start | bytes 196616 | tf_op jit(solution)/shard_map/ppermute | solution.py:661
  34.2 4.3 %collective-permute-start.8 = (f32[8,16,128]{2,1,0:T(8,128)S(1)}, f32[8,16,128]{2,1,0:T(8,128)S(1)}, u32[]{:S(2)}, u32[]{:S(2)}) collective-permute-start(f32[8,16,128]{2,1,0:T(8,128)S(1)} %get-tuple-element.74.own), channel_id=1, source_target_pairs={{0,32},{32,64},{64,96},{96,128},{128,160},{160,192},{192,224},{224... | collective-permute-start | bytes 196616 | tf_op jit(solution)/shard_map/ppermute | solution.py:660
  36.0 3.7 %collective-permute-start.9 = (f32[8,16,128]{2,1,0:T(8,128)S(1)}, f32[8,16,128]{2,1,0:T(8,128)S(1)}, u32[]{:S(2)}, u32[]{:S(2)}) collective-permute-start(f32[8,16,128]{2,1,0:T(8,128)S(1)} %get-tuple-element.74.own), channel_id=1, source_target_pairs={{0,224},{32,0},{64,32},{96,64},{128,96},{160,128},{192,160},{224,1... | collective-permute-start | bytes 196616 | tf_op jit(solution)/shard_map/ppermute | solution.py:661
  39.7 5.2 %collective-permute-start.10 = (f32[8,32,128]{2,1,0:T(8,128)S(1)}, f32[8,32,128]{2,1,0:T(8,128)S(1)}, u32[]{:S(2)}, u32[]{:S(2)}) collective-permute-start(f32[8,32,128]{2,1,0:T(8,128)S(1)} %constant_dynamic-update-slice_fusion), channel_id=1, source_target_pairs={{0,224},{32,0},{64,32},{96,64},{128,96},{160,128},{192,160},{224,1... | collective-permute-start | bytes 393224 | tf_op jit(solution)/shard_map/ppermute | solution.py:661
  42.7 3.8 %collective-permute-start.11 = (f32[8,32,128]{2,1,0:T(8,128)S(1)}, f32[8,32,128]{2,1,0:T(8,128)S(1)}, u32[]{:S(2)}, u32[]{:S(2)}) collective-permute-start(f32[8,32,128]{2,1,0:T(8,128)S(1)} %constant_dynamic-update-slice_fusion), channel_id=1, source_target_pairs={{0,32},{32,64},{64,96},{96,128},{128,160},{160,192},{192,224},{224... | collective-permute-start | bytes 393224 | tf_op jit(solution)/shard_map/ppermute | solution.py:660
  90.4 6.5 %collective-permute-start.12 = (f32[8,16,128]{2,1,0:T(8,128)S(1)}, f32[8,16,128]{2,1,0:T(8,128)S(1)}, u32[]{:S(2)}, u32[]{:S(2)}) collective-permute-start(f32[8,16,128]{2,1,0:T(8,128)S(1)} %get-tuple-element.100.own), channel_id=1, source_target_pairs={{0,1},{1,2},{2,3},{3,4},{4,5},{5,6},{6,7},{7,8},{8,9},{9,10},{10,1... | collective-permute-start | bytes 196616 | tf_op jit(solution)/shard_map/ppermute | solution.py:660
  91.0 5.9 %collective-permute-start.13 = (f32[8,16,128]{2,1,0:T(8,128)S(1)}, f32[8,16,128]{2,1,0:T(8,128)S(1)}, u32[]{:S(2)}, u32[]{:S(2)}) collective-permute-start(f32[8,16,128]{2,1,0:T(8,128)S(1)} %get-tuple-element.100.own), channel_id=1, source_target_pairs={{0,31},{1,0},{2,1},{3,2},{4,3},{5,4},{6,5},{7,6},{8,7},{9,8},{10,9... | collective-permute-start | bytes 196616 | tf_op jit(solution)/shard_map/ppermute | solution.py:661
  95.3 2.5 %collective-permute-start.14 = (f32[8,16,128]{2,1,0:T(8,128)S(1)}, f32[8,16,128]{2,1,0:T(8,128)S(1)}, u32[]{:S(2)}, u32[]{:S(2)}) collective-permute-start(f32[8,16,128]{2,1,0:T(8,128)S(1)} %get-tuple-element.100.own), channel_id=1, source_target_pairs={{0,32},{32,64},{64,96},{96,128},{128,160},{160,192},{192,224},{224... | collective-permute-start | bytes 196616 | tf_op jit(solution)/shard_map/ppermute | solution.py:660
  96.4 4.0 %collective-permute-start.15 = (f32[8,16,128]{2,1,0:T(8,128)S(1)}, f32[8,16,128]{2,1,0:T(8,128)S(1)}, u32[]{:S(2)}, u32[]{:S(2)}) collective-permute-start(f32[8,16,128]{2,1,0:T(8,128)S(1)} %get-tuple-element.100.own), channel_id=1, source_target_pairs={{0,224},{32,0},{64,32},{96,64},{128,96},{160,128},{192,160},{224,1... | collective-permute-start | bytes 196616 | tf_op jit(solution)/shard_map/ppermute | solution.py:661
  100.4 4.4 %collective-permute-start.16 = (f32[8,32,128]{2,1,0:T(8,128)S(1)}, f32[8,32,128]{2,1,0:T(8,128)S(1)}, u32[]{:S(2)}, u32[]{:S(2)}) collective-permute-start(f32[8,32,128]{2,1,0:T(8,128)S(1)} %constant_dynamic-update-slice_fusion.2), channel_id=1, source_target_pairs={{0,224},{32,0},{64,32},{96,64},{128,96},{160,128},{192,160},{224,1... | collective-permute-start | bytes 393224 | tf_op jit(solution)/shard_map/ppermute | solution.py:661
  101.2 3.8 %collective-permute-start.17 = (f32[8,32,128]{2,1,0:T(8,128)S(1)}, f32[8,32,128]{2,1,0:T(8,128)S(1)}, u32[]{:S(2)}, u32[]{:S(2)}) collective-permute-start(f32[8,32,128]{2,1,0:T(8,128)S(1)} %constant_dynamic-update-slice_fusion.2), channel_id=1, source_target_pairs={{0,32},{32,64},{64,96},{96,128},{128,160},{160,192},{192,224},{224... | collective-permute-start | bytes 393224 | tf_op jit(solution)/shard_map/ppermute | solution.py:660
